TPU v7x, 128 devices: a whole 4x4x4 slice. The times are simulated.
128 devices in a mesh: rows: 8 (over z, core), cols: 16 (over y, x).
Axes of the slice: x: 4, y: 4, z: 4, core: 2. Of those that a mesh axis runs over, the one named last changes fastest.
Arguments:
- model_dir: float32 [131072, 128], P('cols'), may hold values from -6 to 6
- sens_blocks: bfloat16 [8, 6144, 128, 128], P('rows', 'cols'), may hold values from -0.0625 to 0.0625
- blk_row: int32 [8, 6144], P('rows', 'cols'), may hold values from 0 to 31, as said below
- blk_col: int32 [8, 6144], P('rows', 'cols'), may hold values from 0 to 63, as said below
- blk_count: int32 [8, 16], P('rows', 'cols'), may hold values from 48 to 384, as said below
- send_order: int32 [16, 64], P('cols'), may hold values from 0 to 63, each once within a row
- neighbors: int32 [4, 131072], P(None, 'cols'), may hold values from 0 to 131071, as said below
- face_weight: float32 [4, 131072], P(None, 'cols'), may hold values from 0.05 to 0.5
Outputs:
- data_image: float32 [32768, 128], P('rows')
- normal_product: float32 [131072, 128], P('cols')
Inputs may be any that keep to these rules, and one draw needn't show every extreme that they name: Within one device's 384 slots the pairs (blk_row, blk_col) are all different. `blk_col`: paired with blk_row as stated there. The live slots of a device are its first blk_count slots; some device has all 384 live. `send_order`: each row is a permutation. `neighbors`: every neighbour lies within 64 of the cell's own number.
All inputs are finite; a program needn't handle non-finite values.
Results may differ from a plain program's by a relative error of at most 0.0029.
Values may be sent and summed in bfloat16 or wider, within the bound.
A program may use at most 192 MiB of HBM per device.

v0:
```python
import math

import jax
import jax.numpy as jnp
from jax import lax
from jax.sharding import PartitionSpec as P

BLK = 128
RB_DEV = 32
RIM = 64


def padded_2(block, sides, width):
    for axis, dim in sides:
        count = lax.axis_size(axis)
        forward = [(i, i + 1) for i in range(count - 1)]
        backward = [(target, source) for source, target in forward]
        low = lax.ppermute(
            lax.slice_in_dim(block, block.shape[dim] - width, None, axis=dim), axis, forward
        )
        high = lax.ppermute(lax.slice_in_dim(block, 0, width, axis=dim), axis, backward)
        block = jnp.concatenate([low, block, high], axis=dim)
    return block


def haar_matrix(order_n):
    matrix = jnp.ones((1, 1), jnp.float32)
    factor = 1.0 / math.sqrt(2.0)
    while matrix.shape[0] < order_n:
        length = matrix.shape[0]
        upper_half = jnp.kron(matrix, jnp.array([[1.0, 1.0]], jnp.float32))
        lower_half = jnp.kron(
            jnp.eye(length, dtype=jnp.float32), jnp.array([[1.0, -1.0]], jnp.float32)
        )
        matrix = jnp.concatenate([upper_half, lower_half], axis=0) * factor
    return matrix


def one_hot(indices, length, dtype):
    return (indices[:, None] == lax.iota(jnp.int32, length)[None, :]).astype(dtype)


def smoothing(extended, center, neighbors, face_weight, offset):
    cell_count, width = center.shape
    tile_count = cell_count // BLK
    tiles = extended.reshape(tile_count + 1, BLK, width)
    window = jnp.concatenate([tiles[:-1], tiles[1:]], axis=1)
    starts = lax.iota(jnp.int32, tile_count) * BLK
    local_index = (neighbors - offset).reshape(4, tile_count, BLK) - starts[None, :, None]
    span = lax.iota(jnp.int32, 2 * BLK)
    weights = jnp.zeros((tile_count, BLK, 2 * BLK), jnp.float32)
    for face in range(4):
        face_w = face_weight[face].reshape(tile_count, BLK)
        weights = weights + jnp.where(
            local_index[face][:, :, None] == span[None, None, :], face_w[:, :, None], 0.0
        )
    mixed = jnp.einsum("bij,bjn->bin", weights, window, precision=lax.Precision.HIGHEST)
    total_w = jnp.sum(face_weight, axis=0)
    return total_w[:, None] * center - mixed.reshape(cell_count, width)


def synthesize(haar_basis, returned, send_onehot, block_count, cell_count):
    share_cols = returned.shape[-1]
    flat_back = returned.reshape(block_count, BLK * share_cols)
    cell_side = jnp.einsum("jb,jm->bm", send_onehot, flat_back, precision=lax.Precision.HIGHEST)
    cell_side = cell_side.reshape(block_count, BLK, share_cols)
    result = jnp.einsum("ji,bjn->bin", haar_basis, cell_side, precision=lax.Precision.HIGHEST)
    return result.reshape(cell_count, share_cols)


def local(model_dir, sens_blocks, blk_row, blk_col, blk_count, send_order, neighbors, face_weight):
    highest = lax.Precision.HIGHEST
    cell_count, vec_width = model_dir.shape
    block_count = cell_count // BLK
    col_devices = lax.axis_size("cols")
    per_peer = block_count // col_devices
    haar_basis = jnp.asarray(haar_matrix(BLK), jnp.float32)
    cell_blocks = model_dir.reshape(block_count, BLK, vec_width)
    coeffs = jnp.einsum("ij,bjn->bin", haar_basis, cell_blocks, precision=highest).astype(
        jnp.bfloat16
    )
    order_here = send_order[0]
    send_half = one_hot(order_here, block_count, jnp.bfloat16)
    ordered = jnp.dot(
        send_half, coeffs.reshape(block_count, BLK * vec_width), preferred_element_type=jnp.float32
    )
    outgoing = ordered.astype(jnp.bfloat16).reshape(col_devices, per_peer * BLK, vec_width)
    wavelet = lax.all_to_all(outgoing, "cols", split_axis=0, concat_axis=0, tiled=True).reshape(
        block_count, BLK * vec_width
    )
    rows_here = blk_row[0]
    cols_here = blk_col[0]
    sensors = sens_blocks[0]
    slot_count = sensors.shape[0]
    live_slot = lax.iota(jnp.int32, slot_count) < blk_count[0, 0]
    pick_cols = one_hot(cols_here, block_count, jnp.bfloat16)
    picked = jnp.dot(pick_cols, wavelet, preferred_element_type=jnp.float32).astype(jnp.bfloat16)
    picked = picked.reshape(slot_count, BLK, vec_width)
    forward = jnp.einsum("kij,kjn->kin", sensors, picked, preferred_element_type=jnp.float32)
    row_mask = (one_hot(rows_here, RB_DEV, jnp.float32) * live_slot[:, None].astype(jnp.float32)).T
    partial_rows = jnp.dot(
        row_mask, forward.reshape(slot_count, BLK * vec_width), precision=highest
    )
    partial_rows = partial_rows.reshape(RB_DEV, BLK, vec_width)
    predicted = lax.psum(partial_rows, "cols")
    data_image = predicted.reshape(RB_DEV * BLK, vec_width)
    image_half = predicted.astype(jnp.bfloat16).reshape(RB_DEV, BLK * vec_width)
    pick_rows = one_hot(rows_here, RB_DEV, jnp.bfloat16)
    chosen = jnp.dot(pick_rows, image_half, preferred_element_type=jnp.float32).astype(jnp.bfloat16)
    chosen = chosen.reshape(slot_count, BLK, vec_width)
    adjoint = jnp.einsum("kij,kin->kjn", sensors, chosen, preferred_element_type=jnp.float32)
    col_mask = (
        one_hot(cols_here, block_count, jnp.float32) * live_slot[:, None].astype(jnp.float32)
    ).T
    partial_cols = jnp.dot(
        col_mask, adjoint.reshape(slot_count, BLK * vec_width), precision=highest
    )
    partial_cols = partial_cols.reshape(block_count, BLK, vec_width)
    extended = padded_2(model_dir, (("cols", 0),), RIM)
    offset = lax.axis_index("cols") * cell_count - RIM
    send_full = one_hot(order_here, block_count, jnp.float32)
    summed = lax.psum(partial_cols, "rows")
    returned = lax.all_to_all(
        summed.reshape(col_devices, per_peer * BLK, vec_width),
        "cols",
        split_axis=0,
        concat_axis=0,
        tiled=True,
    )
    synthesis = synthesize(haar_basis, returned, send_full, block_count, cell_count)
    normal_product = synthesis + smoothing(extended, model_dir, neighbors, face_weight, offset)
    return (data_image, normal_product)


def solution(mesh):
    placed = (
        P("cols", None),
        P("rows", "cols", None, None),
        P("rows", "cols"),
        P("rows", "cols"),
        P("rows", "cols"),
        P("cols", None),
        P(None, "cols"),
        P(None, "cols"),
    )
    return jax.shard_map(
        local,
        mesh=mesh,
        in_specs=placed,
        out_specs=(P("rows", None), P("cols", None)),
        check_vma=False,
    )
```

profile of v0, /device:TPU:65, one launch (start us, length us, event | category | flops | bytes accessed | tf_op | source)
XLA Modules:
  0.0 500.2 jit_solution(12547211673845322062)
XLA Ops:
  13.8 6.0 %convolution_convert_fusion.3 = bf16[128,64,128]{2,0,1:T(8,128)(2,1)S(1)} fusion(f32[64,128,128]{2,1,0:T(8,128)} %bitcast.118, f32[64,128]{1,0:T(8,128)S(1)} %broadcast_multiply_fusion, f32[64,128]{1,0:T(8,128)S(1)} %copy.31), kind=kOutput, calls=%fused_computation.50 | convolution fusion | flops 1611694080 | bytes 6356992 | tf_op jit(solution)/shard_map/ij,bjn->bin/dot_general | solution.py:79
  19.9 1.7 convolution_convert_fusion.2
  21.6 2.3 reshape.406
  23.9 6.8 %all-to-all-start = ((bf16[16,512,128]{2,1,0:T(8,128)(2,1)}), bf16[16,512,128]{2,1,0:T(8,128)(2,1)S(1)}, u32[]{:S(2)}, u32[]{:S(2)}) async-start(bf16[16,512,128]{2,1,0:T(8,128)(2,1)} %reshape.406), calls=%async_computation | async-start | bytes 4194304 | tf_op jit(solution)/shard_map/all_to_all | solution.py:88
  31.9 29.3 %all-to-all-done = bf16[16,512,128]{2,1,0:T(8,128)(2,1)S(1)} async-done(((bf16[16,512,128]{2,1,0:T(8,128)(2,1)}), bf16[16,512,128]{2,1,0:T(8,128)(2,1)S(1)}, u32[]{:S(2)}, u32[]{:S(2)}) %all-to-all-start) | async-done | bytes 2097184 | tf_op jit(solution)/shard_map/all_to_all | solution.py:88
  61.2 2.3 reshape.407
  63.4 5.1 %fusion.25 = bf16[48,8,128,128]{3,1,2,0:T(8,128)(2,1)S(1)} fusion(bf16[64,16384]{1,0:T(8,128)(2,1)} %reshape.407, s32[384]{0:T(512)S(1)} %reduce.1), kind=kOutput, calls=%fused_computation.28 | convolution fusion | flops 811622400 | bytes 14681600 | tf_op jit(solution)/shard_map/dot_general | solution.py:97
  68.5 6.5 %copy.49 = bf16[48,8,128,128]{3,2,1,0:T(8,128)(2,1)} copy(bf16[48,8,128,128]{3,1,2,0:T(8,128)(2,1)S(1)} %fusion.25) | data formatting | bytes 25165824
  75.0 22.1 %fusion.8 = f32[384,128,128]{1,2,0:T(8,128)} fusion(bf16[384,128,128]{2,1,0:T(8,128)(2,1)} %bitcast.116, bf16[1,384,128,128]{3,2,1,0:T(8,128)(2,1)} %param.23), kind=kOutput, calls=%fused_computation.11 | convolution fusion | flops 1610612736 | bytes 50331648 | tf_op jit(solution)/shard_map/kij,kjn->kin/dot_general | solution.py:99
  97.1 25.0 %copy.33 = f32[384,128,128]{0,2,1:T(8,128)} copy(f32[384,128,128]{1,2,0:T(8,128)} %fusion.8) | data formatting | bytes 50331648 | tf_op jit(solution)/shard_map/kij,kjn->kin/dot_general | solution.py:99
  122.1 27.2 %fusion.2 = f32[32,128,128]{2,0,1:T(8,128)} fusion(f32[384,128,128]{0,2,1:T(8,128)} %copy.33, f32[384]{0:T(512)S(1)} %fusion.70, s32[384]{0:T(512)S(1)} %reduce), kind=kOutput, calls=%fused_computation.2 | convolution fusion | flops 2415943680 | bytes 27266048 | tf_op jit(solution)/shard_map/dot_general | solution.py:101
  149.4 88.7 %all-reduce.3.cloned.1.call-done = f32[32,128,128]{2,0,1:T(8,128)} async-done(((f32[32,128,128]{2,0,1:T(8,128)}), f32[32,128,128]{2,0,1:T(8,128)}) %all-reduce.3.cloned.1.call-update) | async-done | bytes 2097168 | tf_op jit(solution)/shard_map/psum | solution.py:105
  238.1 9.7 %fusion.26 = bf16[48,8,128,128]{3,1,2,0:T(8,128)(2,1)} fusion(s32[384]{0:T(512)S(1)} %reduce, f32[32,128,128]{2,0,1:T(8,128)} %all-reduce.3.cloned.1.call-done), kind=kOutput, calls=%fused_computation.29 | convolution fusion | flops 409481216 | bytes 14681600 | tf_op jit(solution)/shard_map/dot_general | solution.py:109
  247.8 12.0 %copy.50 = bf16[48,8,128,128]{3,2,1,0:T(8,128)(2,1)} copy(bf16[48,8,128,128]{3,1,2,0:T(8,128)(2,1)} %fusion.26) | data formatting | bytes 25165824
  259.8 13.2 %fusion.11 = f32[384,128,128]{1,2,0:T(8,128)} fusion(bf16[384,128,128]{2,1,0:T(8,128)(2,1)} %bitcast.117, bf16[1,384,128,128]{3,2,1,0:T(8,128)(2,1)S(1)} %bitcast.115), kind=kOutput, calls=%fused_computation.12 | convolution fusion | flops 1610612736 | bytes 50331648 | tf_op jit(solution)/shard_map/kij,kin->kjn/dot_general | solution.py:111
  273.0 25.0 %copy.37 = f32[384,128,128]{0,2,1:T(8,128)} copy(f32[384,128,128]{1,2,0:T(8,128)} %fusion.11) | data formatting | bytes 50331648 | tf_op jit(solution)/shard_map/kij,kin->kjn/dot_general | solution.py:111
  298.0 27.9 %fusion = f32[64,128,128]{2,0,1:T(8,128)S(1)} fusion(f32[384,128,128]{0,2,1:T(8,128)} %copy.37, f32[384]{0:T(512)S(1)} %fusion.70, s32[384]{0:T(512)S(1)} %reduce.1), kind=kOutput, calls=%fused_computation | convolution fusion | flops 4831887360 | bytes 29363200 | tf_op jit(solution)/shard_map/dot_general | solution.py:115
  325.9 4.4 copy.38
  330.3 0.8 fusion.80
  331.1 2.5 collective-permute-start
  333.7 1.3 collective-permute-start.1
  335.1 65.8 %all-reduce.5.cloned.1.call-done = f32[16,512,128]{2,1,0:T(8,128)} async-done(((f32[16,512,128]{2,1,0:T(8,128)}), f32[16,512,128]{2,1,0:T(8,128)}) %all-reduce.5.cloned.1.call-update) | async-done | bytes 4194320 | tf_op jit(solution)/shard_map/psum | solution.py:122
  400.9 6.8 %all-to-all-start.1 = ((f32[16,512,128]{2,1,0:T(8,128)}), f32[16,512,128]{2,1,0:T(8,128)}, u32[]{:S(2)}, u32[]{:S(2)}) async-start(f32[16,512,128]{2,1,0:T(8,128)} %all-reduce.5.cloned.1.call-done), calls=%async_computation.1 | async-start | bytes 8388608 | tf_op jit(solution)/shard_map/all_to_all | solution.py:123
  408.0 4.0 pad_maximum_fusion.1
  412.0 3.8 fusion.93
  415.7 20.2 %fusion.14 = f32[64,128,128]{2,1,0:T(8,128)} fusion(f32[64,128]{1,0:T(8,128)S(1)} %bitcast.134, s32[64,128]{1,0:T(8,128)S(1)} %get-tuple-element.7, f32[64,128]{1,0:T(8,128)S(1)} %bitcast.135, s32[64,128]{1,0:T(8,128)S(1)} %get-tuple-element.8, f32[64,128]{1,0:T(8,128)S(1)} %bitcast.133, s32[64,128]{1,0:T(8,128)S(1)} %get-tuple-element.9, ...), kind=kOutput, calls=%fused_computation.13 | convolution fusion | flops 3244294144 | bytes 12845056 | tf_op jit(solution)/shard_map/bij,bjn->bin/dot_general | solution.py:57
  435.9 2.5 copy.34
  438.4 34.3 %all-to-all-done.1 = f32[16,512,128]{2,1,0:T(8,128)} async-done(((f32[16,512,128]{2,1,0:T(8,128)}), f32[16,512,128]{2,1,0:T(8,128)}, u32[]{:S(2)}, u32[]{:S(2)}) %all-to-all-start.1) | async-done | bytes 4194336 | tf_op jit(solution)/shard_map/all_to_all | solution.py:123
  472.7 4.9 reshape.415
  477.6 4.6 fusion.27
  482.3 6.3 %fusion.30 = f32[64,128,128]{1,2,0:T(8,128)S(1)} fusion(f32[64,128,128]{2,0,1:T(8,128)S(1)} %fusion.27, f32[64,128]{1,0:T(8,128)S(1)} %broadcast_multiply_fusion, f32[64,128]{1,0:T(8,128)S(1)} %copy.31), kind=kOutput, calls=%fused_computation.37 | convolution fusion | flops 1610645504 | bytes 8454144 | tf_op jit(solution)/shard_map/ji,bjn->bin/dot_general | solution.py:67
  488.6 4.6 bitcast_add_fusion
  (84 shorter events, 7.5 us)
Async XLA Ops:
  7.2 12.7 %copy-start.5 = (s32[1,64]{1,0:T(1,128)S(1)}, s32[1,64]{1,0:T(1,128)}, u32[]{:S(2)}) copy-start(s32[1,64]{1,0:T(1,128)} %param.27) | copy-start | bytes 772
  21.6 10.3 %copy-start.6 = (s32[1,384]{1,0:T(1,128)S(1)}, s32[1,384]{1,0:T(1,128)}, u32[]{:S(2)}) copy-start(s32[1,384]{1,0:T(1,128)} %param.25) | copy-start | bytes 4612
  21.6 10.3 %copy-start.7 = (s32[1,384]{1,0:T(1,128)S(1)}, s32[1,384]{1,0:T(1,128)}, u32[]{:S(2)}) copy-start(s32[1,384]{1,0:T(1,128)} %param.24) | copy-start | bytes 4612
  23.9 37.3 %all-to-all-start = ((bf16[16,512,128]{2,1,0:T(8,128)(2,1)}), bf16[16,512,128]{2,1,0:T(8,128)(2,1)S(1)}, u32[]{:S(2)}, u32[]{:S(2)}) async-start(bf16[16,512,128]{2,1,0:T(8,128)(2,1)} %reshape.406), calls=%async_computation | async-start | bytes 4194304 | tf_op jit(solution)/shard_map/all_to_all | solution.py:88
  30.7 207.4 %all-reduce.3.cloned.1.call-start = ((), (), s32[]{:S(2)}) async-start(), calls=%async_computation.2 | async-start | bytes 4194304 | tf_op jit(solution)/shard_map/psum | solution.py:105
  149.3 251.6 %all-reduce.5.cloned.1.call-start = ((), (), s32[]{:S(2)}) async-start(), calls=%async_computation.3 | async-start | bytes 8388608 | tf_op jit(solution)/shard_map/psum | solution.py:122
  238.1 21.7 %slice-start = ((s8[12582912]{0:T(1024)(128)(4,1)}), s8[4194304]{0:T(1024)(128)(4,1)S(1)}, s32[]{:S(2)}) async-start(s8[12582912]{0:T(1024)(128)(4,1)} %bitcast.114), calls=%async_computation.4 | async-start | bytes 8388608
  238.1 21.7 %slice-start.1 = ((s8[12582912]{0:T(1024)(128)(4,1)}), s8[4194304]{0:T(1024)(128)(4,1)S(1)}, s32[]{:S(2)}) async-start(s8[12582912]{0:T(1024)(128)(4,1)} %bitcast.114), calls=%async_computation.5 | async-start | bytes 8388608
  247.8 12.0 %slice-start.2 = ((s8[12582912]{0:T(1024)(128)(4,1)}), s8[4194304]{0:T(1024)(128)(4,1)S(1)}, s32[]{:S(2)}) async-start(s8[12582912]{0:T(1024)(128)(4,1)} %bitcast.114), calls=%async_computation.6 | async-start | bytes 8388608
  330.3 4.7 copy-start.4
  331.1 76.8 %collective-permute-start = (f32[64,128]{1,0:T(8,128)S(1)}, f32[64,128]{1,0:T(8,128)S(1)}, u32[]{:S(2)}, u32[]{:S(2)}) collective-permute-start(f32[64,128]{1,0:T(8,128)S(1)} %get-tuple-element.4), channel_id=1, source_target_pairs={{0,1},{1,2},{2,3},{3,4},{4,5},{5,6},{6,7},{7,8},{8,9},{9,10},{10,1... | collective-permute-start | bytes 98312 | tf_op jit(solution)/shard_map/ppermute | solution.py:18
  333.7 74.3 %collective-permute-start.1 = (f32[64,128]{1,0:T(8,128)S(1)}, f32[64,128]{1,0:T(8,128)S(1)}, u32[]{:S(2)}, u32[]{:S(2)}) collective-permute-start(f32[64,128]{1,0:T(8,128)S(1)} %get-tuple-element.5), channel_id=1, source_target_pairs={{1,0},{2,1},{3,2},{4,3},{5,4},{6,5},{7,6},{8,7},{9,8},{10,9},{11,1... | collective-permute-start | bytes 98312 | tf_op jit(solution)/shard_map/ppermute | solution.py:21
  335.1 72.6 %copy-start.3 = (f32[4,8192]{1,0:T(4,128)S(1)}, f32[4,8192]{1,0:T(4,128)}, u32[]{:S(2)}) copy-start(f32[4,8192]{1,0:T(4,128)} %param.29) | copy-start | bytes 393220
  400.9 71.8 %all-to-all-start.1 = ((f32[16,512,128]{2,1,0:T(8,128)}), f32[16,512,128]{2,1,0:T(8,128)}, u32[]{:S(2)}, u32[]{:S(2)}) async-start(f32[16,512,128]{2,1,0:T(8,128)} %all-reduce.5.cloned.1.call-done), calls=%async_computation.1 | async-start | bytes 8388608 | tf_op jit(solution)/shard_map/all_to_all | solution.py:123
  415.7 20.2 %copy-start.1 = (f32[32,128,128]{2,0,1:T(8,128)S(1)}, f32[32,128,128]{2,0,1:T(8,128)}, u32[]{:S(2)}) copy-start(f32[32,128,128]{2,0,1:T(8,128)} %all-reduce.3.cloned.1.call-done) | copy-start | bytes 6291460
  482.3 6.3 %copy-start = (f32[8192,128]{1,0:T(8,128)S(1)}, f32[8192,128]{1,0:T(8,128)}, u32[]{:S(2)}) copy-start(f32[8192,128]{1,0:T(8,128)} %param.22) | copy-start | bytes 12582916
  482.3 6.3 %copy-start.2 = (f32[64,128,128]{2,1,0:T(8,128)S(1)}, f32[64,128,128]{2,1,0:T(8,128)}, u32[]{:S(2)}) copy-start(f32[64,128,128]{2,1,0:T(8,128)} %fusion.14) | copy-start | bytes 12582916
Sparse Core Ops, SparseCore 0:
  149.4 88.5 all-reduce.2
  330.4 70.4 all-reduce.4
where the time goes:
time: 507 us; the launch traced here: 500 us
  waiting for transfers between devices  218 us (43%)
  matrix products  144 us (28%)
  local copies, waits for them, and re-layouts  91.8 us (18%)
  starting transfers between devices  17.9 us (4%)
  between operations  15.3 us (3%)
  other arithmetic  13.2 us (3%)
    psum x1, waiting for transfers between devices, local(): predicted = lax.psum(partial_rows, 'cols')  88.7 us
    psum x1, waiting for transfers between devices, local(): summed = lax.psum(partial_cols, 'rows')  65.8 us
    all_to_all x1, waiting for transfers between devices, local(): lax.all_to_all(summed.reshape(col_devices, per_peer * BLK, vec_width), 'c...  34.3 us
    all_to_all x1, waiting for transfers between devices, local(): lax.all_to_all(outgoing, 'cols', split_axis=0, concat_axis=0, tiled=True)  29.3 us
    dot_general x1, matrix products, local(): jnp.dot(col_mask, adjoint.reshape(slot_count, BLK * vec_width), precision...  27.9 us
    dot_general x1, matrix products, local(): jnp.dot(row_mask, forward.reshape(slot_count, BLK * vec_width), precision...  27.2 us
    dot_general x1, local copies, waits for them, and re-layouts, local(): jnp.einsum('kij,kin->kjn', sensors, chosen, preferred_element_type=jnp.fl...  25 us
    dot_general x1, local copies, waits for them, and re-layouts, local(): jnp.einsum('kij,kjn->kin', sensors, picked, preferred_element_type=jnp.fl...  25 us
  transfers between devices with their start and end apart: 6, of which 4 were waited for; matrix products, arithmetic and copies ran while one was open for 6% of the time, Pallas kernels for 0%

commit v1 on v0

v1 whole, which is shorter than its diff:
```python
import math

import jax
import jax.numpy as jnp
import numpy as np
from jax import lax
from jax.experimental import pallas as pl
from jax.experimental.pallas import tpu as pltpu
from jax.sharding import PartitionSpec as P

BLK = 128
HALF = 64
RIM = 64
NROWS = 8
NCOLS = 16
NZ = 4
ROW_BLOCKS = 32
COL_BLOCKS = 64
SLOTS = 384
CHUNK = 32
UNROLL = 4
VMEM_LIMIT = 56 << 20
MESH = pl.DeviceIdType.MESH
F32 = jnp.float32
BF16 = jnp.bfloat16


def haar_parts():
    matrix = np.ones((1, 1))
    while matrix.shape[0] < BLK:
        length = matrix.shape[0]
        upper = np.kron(matrix, np.array([[1.0, 1.0]]))
        lower = np.kron(np.eye(length), np.array([[1.0, -1.0]]))
        matrix = np.concatenate([upper, lower], axis=0) / math.sqrt(2.0)
    scale = np.abs(matrix).max(axis=1)
    signs = np.round(matrix / scale[:, None])
    return signs, scale


SIGNS, SCALE = haar_parts()


def split(value):
    high = value.astype(BF16)
    low = (value - high.astype(F32)).astype(BF16)
    return high, low


def dot(a, b):
    return jnp.dot(a, b, preferred_element_type=F32)


def remote(src, dst, send_sem, recv_sem, device):
    return pltpu.make_async_remote_copy(
        src_ref=src,
        dst_ref=dst,
        send_sem=send_sem,
        recv_sem=recv_sem,
        device_id=device,
        device_id_type=MESH,
    )


def place():
    row = lax.axis_index("rows")
    col = lax.axis_index("cols")
    return row, col, lax.div(row, 2), lax.rem(row, 2)


def z_device(z, step, core, col):
    return (lax.rem(z + step, NZ) * 2 + core, col)


def greet(devices, loop_devices=None):
    barrier = pltpu.get_barrier_semaphore()
    for device in devices:
        pl.semaphore_signal(barrier, inc=1, device_id=device, device_id_type=MESH)
    count = len(devices)
    if loop_devices is not None:
        row, col = loop_devices

        def signal(i, carry):
            pl.semaphore_signal(
                barrier,
                inc=1,
                device_id=(row, lax.rem(col + i, NCOLS)),
                device_id_type=MESH,
            )
            return carry

        lax.fori_loop(1, NCOLS, signal, 0)
        count += NCOLS - 1
    pl.semaphore_wait(barrier, count)


def spread_copy(stage, out, sems, where, i):
    row, col, z, core = where
    target = lax.rem(col + i, NCOLS)
    return remote(
        stage.at[target],
        out.at[z, col, pl.ds(core * HALF, HALF)],
        sems["a_send"].at[i],
        sems["a_recv"].at[col],
        (row, target),
    )


def gather_rows(stage, out, sems, where):
    row, col, z, core = where
    own_rows = pl.ds(core * HALF, HALF)
    plus, minus = z_device(z, 1, core, col), z_device(z, NZ - 1, core, col)
    partner = (z * 2 + 1 - core, col)
    z_before, z_after, z_far = lax.rem(z + 3, NZ), lax.rem(z + 1, NZ), lax.rem(z + 2, NZ)
    group = NCOLS // 2
    sends = []

    def piece(q, p):
        return out.at[q, pl.ds(p * group, group), own_rows]

    def send(q, p, device, recv_sem):
        copy = remote(piece(q, p), piece(q, p), sems["g_send"].at[len(sends)], recv_sem, device)
        copy.start()
        sends.append(copy)

    def arrived(q, p, recv_sem, rows=None):
        ref = piece(q, p) if rows is None else out.at[q, pl.ds(p * group, group), rows]
        remote(ref, ref, sems["g_send"].at[0], recv_sem, partner).wait_recv()

    for p in range(2):

        def wait_part(s, carry):
            @pl.when(s != col)
            def _():
                ref = out.at[z, s, own_rows]
                remote(ref, ref, sems["a_send"].at[0], sems["a_recv"].at[s], partner).wait_recv()

            return carry

        lax.fori_loop(p * group, (p + 1) * group, wait_part, 0)
        send(z, p, plus, sems["minus"].at[p])
        send(z, p, minus, sems["plus"].at[p])
        send(z, p, partner, sems["pair"].at[0, p])
    arrived(z_before, 0, sems["minus"].at[0])
    send(z_before, 0, plus, sems["far"].at[0])
    send(z_before, 0, partner, sems["pair"].at[1, 0])
    arrived(z_after, 1, sems["plus"].at[1])
    send(z_after, 1, minus, sems["far"].at[1])
    send(z_after, 1, partner, sems["pair"].at[2, 1])
    arrived(z_after, 0, sems["plus"].at[0])
    send(z_after, 0, partner, sems["pair"].at[2, 0])
    arrived(z_before, 1, sems["minus"].at[1])
    send(z_before, 1, partner, sems["pair"].at[1, 1])
    for p in range(2):
        arrived(z_far, p, sems["far"].at[p])
        send(z_far, p, partner, sems["pair"].at[3, p])
    other_rows = pl.ds((1 - core) * HALF, HALF)
    for p in range(2):
        for slot, q in enumerate((z, z_before, z_after, z_far)):
            arrived(q, p, sems["pair"].at[slot, p], other_rows)

    def finish(i, carry):
        spread_copy(stage, out, sems, where, i).wait_send()
        return carry

    lax.fori_loop(1, NCOLS, finish, 0)
    for copy in sends:
        copy.wait_send()


EXCHANGE_SEMS = [
    pltpu.SemaphoreType.DMA((NCOLS,)),
    pltpu.SemaphoreType.DMA((NCOLS,)),
    pltpu.SemaphoreType.DMA((14,)),
    pltpu.SemaphoreType.DMA((2,)),
    pltpu.SemaphoreType.DMA((2,)),
    pltpu.SemaphoreType.DMA((2,)),
    pltpu.SemaphoreType.DMA((4, 2)),
]
EXCHANGE_NAMES = ("a_send", "a_recv", "g_send", "minus", "plus", "far", "pair")


def analyse_kernel(order, model, signs, scale, wavelet, halo, stage, halo_sems, *sem_refs):
    sems = dict(zip(EXCHANGE_NAMES, sem_refs))
    where = place()
    row, col, z, core = where
    greet(
        [z_device(z, 1, core, col), z_device(z, 3, core, col), (z * 2 + 1 - core, col)],
        (row, col),
    )
    below, above = lax.rem(col + NCOLS - 1, NCOLS), lax.rem(col + 1, NCOLS)
    up = remote(
        model.at[COL_BLOCKS - 1, pl.ds(BLK - RIM, RIM)],
        halo.at[0],
        halo_sems.at[0],
        halo_sems.at[2],
        (row, above),
    )
    down = remote(
        model.at[0, pl.ds(0, RIM)],
        halo.at[1],
        halo_sems.at[1],
        halo_sems.at[3],
        (row, below),
    )
    up.start()
    down.start()
    sign_rows = signs[pl.ds(core * HALF, HALF), :]
    sign_pair = jnp.concatenate([sign_rows, sign_rows], axis=1)
    row_scale = scale[pl.ds(core * HALF, HALF), :]

    def coefficients(target):
        high, low = split(model[order[target * 4 + z]])
        product = dot(sign_pair, jnp.concatenate([high, low], axis=0))
        return (product * row_scale).astype(BF16)

    def spread(i, carry):
        target = lax.rem(col + i, NCOLS)
        stage[target] = coefficients(target)
        spread_copy(stage, wavelet, sems, where, i).start()
        return carry

    lax.fori_loop(1, NCOLS, spread, 0)
    wavelet[z, col, pl.ds(core * HALF, HALF), :] = coefficients(col)
    gather_rows(stage, wavelet, sems, where)
    up.wait()
    down.wait()


def analyse(order, model_dir):
    model = model_dir.reshape(COL_BLOCKS, BLK, BLK)
    vmem = pl.BlockSpec(memory_space=pltpu.VMEM)
    return pl.pallas_call(
        analyse_kernel,
        out_shape=(
            jax.ShapeDtypeStruct((4, NCOLS, BLK, BLK), BF16),
            jax.ShapeDtypeStruct((2, RIM, BLK), F32),
        ),
        in_specs=[pl.BlockSpec(memory_space=pltpu.SMEM), vmem, vmem, vmem],
        out_specs=(vmem, vmem),
        scratch_shapes=[
            pltpu.VMEM((NCOLS, HALF, BLK), BF16),
            pltpu.SemaphoreType.DMA((4,)),
            *EXCHANGE_SEMS,
        ],
        compiler_params=pltpu.CompilerParams(
            collective_id=0, has_side_effects=True, vmem_limit_bytes=VMEM_LIMIT
        ),
        name="analyse",
    )(
        order,
        model,
        jnp.asarray(SIGNS, BF16),
        jnp.asarray(np.broadcast_to(SCALE[:, None], (BLK, BLK)), F32),
    )


def live_slots(count, step, add):
    live = jnp.clip(count[0] - step * CHUNK, 0, CHUNK)
    groups = live // UNROLL

    def group(g, carry):
        add(g * UNROLL, UNROLL)
        return carry

    def single(k, carry):
        add(k, 1)
        return carry

    lax.fori_loop(0, groups, group, 0)
    lax.fori_loop(groups * UNROLL, live, single, 0)


def forward_kernel(count, rows, cols, sens, wavelet, image):
    step = pl.program_id(0)

    @pl.when(step == 0)
    def _():
        image[...] = jnp.zeros_like(image)

    def add(first, width):
        terms = []
        for u in range(width):
            at = cols[step * CHUNK + first + u]
            terms.append(dot(sens[0, first + u], wavelet[at & 3, at >> 2]))
        for u in range(width):
            image[rows[step * CHUNK + first + u]] += terms[u]

    live_slots(count, step, add)


def sens_spec():
    def index(i, count, rows, cols):
        return 0, jnp.minimum(i, (count[0] - 1) // CHUNK), 0, 0

    return pl.BlockSpec((1, CHUNK, BLK, BLK), index)


def whole(*shape):
    return pl.BlockSpec(shape, lambda i, *refs: (0,) * len(shape))


def forward(count, rows, cols, sens, wavelet):
    return pl.pallas_call(
        forward_kernel,
        out_shape=jax.ShapeDtypeStruct((ROW_BLOCKS, BLK, BLK), F32),
        grid_spec=pltpu.PrefetchScalarGridSpec(
            num_scalar_prefetch=3,
            grid=(SLOTS // CHUNK,),
            in_specs=[sens_spec(), whole(4, NCOLS, BLK, BLK)],
            out_specs=whole(ROW_BLOCKS, BLK, BLK),
        ),
        compiler_params=pltpu.CompilerParams(vmem_limit_bytes=VMEM_LIMIT),
        name="forward",
    )(count, rows, cols, sens, wavelet)


class Ring:
    def __init__(self, me, plus, minus, send, recv):
        self.me, self.plus, self.minus = me, plus, minus
        self.send, self.recv = send, recv
        self.started = []

    def at(self, step):
        return lax.rem(self.me + step, 4)

    def copy(self, src, dst, device, slot):
        copy = remote(src, dst, self.send.at[slot], self.recv.at[slot], device)
        copy.start()
        self.started.append(copy)

    def arrived(self, ref, slot):
        remote(ref, ref, self.send.at[slot], self.recv.at[slot], self.plus).wait_recv()

    def drain(self):
        for copy in self.started:
            copy.wait_send()
        self.started = []


class Reduce:
    def __init__(self, ring, data, base, chunk, relay, landed):
        self.ring, self.data, self.base, self.chunk = ring, data, base, chunk
        self.half = chunk // 2
        self.relay, self.landed = relay, landed

    def rows(self, step, h):
        start = self.base + self.ring.at(step) * self.chunk + h * self.half
        return pl.ds(pl.multiple_of(start, self.half), self.half)

    def relay_at(self, side):
        return self.relay.at[side, pl.ds(0, self.half)]

    def landed_at(self, side, h):
        return self.landed.at[side, pl.ds(h * self.half, self.half)]

    def begin(self):
        ring, data = self.ring, self.data
        ring.copy(data.at[self.rows(2, 0)], self.relay_at(0), ring.plus, 0)
        ring.copy(data.at[self.rows(2, 1)], self.relay_at(1), ring.minus, 1)
        ring.copy(data.at[self.rows(1, 1)], self.landed_at(0, 1), ring.plus, 2)
        ring.copy(data.at[self.rows(3, 0)], self.landed_at(1, 0), ring.minus, 3)

    def pass_on(self):
        ring, data = self.ring, self.data
        ring.arrived(self.relay_at(0), 0)
        data[self.rows(1, 0), :] += self.relay[0, : self.half]
        ring.copy(data.at[self.rows(1, 0)], self.landed_at(0, 0), ring.plus, 4)
        ring.arrived(self.relay_at(1), 1)
        data[self.rows(3, 1), :] += self.relay[1, : self.half]
        ring.copy(data.at[self.rows(3, 1)], self.landed_at(1, 1), ring.minus, 5)

    def finish(self):
        ring, data = self.ring, self.data
        ring.arrived(self.landed_at(0, 1), 2)
        ring.arrived(self.landed_at(1, 0), 3)
        ring.arrived(self.landed_at(0, 0), 4)
        ring.arrived(self.landed_at(1, 1), 5)
        for h in range(2):
            part = pl.ds(h * self.half, self.half)
            data[self.rows(0, h), :] += self.landed[0, part, :] + self.landed[1, part, :]


class Gather:
    def __init__(self, ring, data, base, chunk):
        self.ring, self.data, self.base, self.chunk = ring, data, base, chunk

    def rows(self, step, h=None):
        start = self.base + self.ring.at(step) * self.chunk
        if h is None:
            return self.data.at[pl.ds(pl.multiple_of(start, self.chunk), self.chunk)]
        half = self.chunk // 2
        return self.data.at[pl.ds(pl.multiple_of(start + h * half, half), half)]

    def begin(self):
        ring = self.ring
        ring.copy(self.rows(0), self.rows(0), ring.plus, 0)
        ring.copy(self.rows(0), self.rows(0), ring.minus, 1)

    def pass_on(self):
        ring = self.ring
        ring.arrived(self.rows(3), 0)
        ring.copy(self.rows(3, 0), self.rows(3, 0), ring.plus, 2)
        ring.arrived(self.rows(1), 1)
        ring.copy(self.rows(1, 1), self.rows(1, 1), ring.minus, 3)

    def finish(self):
        ring = self.ring
        ring.arrived(self.rows(2, 0), 2)
        ring.arrived(self.rows(2, 1), 3)


HALF_ROWS = ROW_BLOCKS * BLK // 2
BIG = HALF_ROWS // 4
SMALL = BIG // 4


def combine_kernel(partial, image, data, big_relay, big_landed, small_relay, small_landed, send, recv):
    row, col, _, _ = place()
    y, x = lax.div(col, 4), lax.rem(col, 4)
    x_plus, x_minus = (row, y * 4 + lax.rem(x + 1, 4)), (row, y * 4 + lax.rem(x + 3, 4))
    y_plus, y_minus = (row, lax.rem(y + 1, 4) * 4 + x), (row, lax.rem(y + 3, 4) * 4 + x)
    greet([x_plus, x_minus, y_plus, y_minus])

    def ring(axis, slot):
        sems = send.at[slot], recv.at[slot]
        return Ring(x, x_plus, x_minus, *sems) if axis == 0 else Ring(y, y_plus, y_minus, *sems)

    def both(stages):
        for stage in stages:
            stage.begin()
        for stage in stages:
            stage.pass_on()
        for stage in stages:
            stage.finish()

    bases = [0, HALF_ROWS]
    inner = [x * BIG, HALF_ROWS + y * BIG]
    rings = [ring(a, a) for a in range(2)]
    wide = [Reduce(rings[a], partial, bases[a], BIG, big_relay.at[a], big_landed.at[a]) for a in range(2)]
    both(wide)
    cross = [ring(1 - a, 2 + a) for a in range(2)]
    narrow = [
        Reduce(cross[a], partial, inner[a], SMALL, small_relay.at[a], small_landed.at[a])
        for a in range(2)
    ]
    both(narrow)
    for a, other in ((0, y), (1, x)):
        own = pl.ds(pl.multiple_of(inner[a] + other * SMALL, SMALL), SMALL)
        image[own, :] = partial[own, :].astype(BF16)
    back = [ring(1 - a, 4 + a) for a in range(2)]
    both([Gather(back[a], image, inner[a], SMALL) for a in range(2)])
    last = [ring(a, 6 + a) for a in range(2)]
    both([Gather(last[a], image, bases[a], BIG) for a in range(2)])
    for group in (rings, cross, back, last):
        for one in group:
            one.drain()


def combine(partial):
    vmem = pl.BlockSpec(memory_space=pltpu.VMEM)
    rows = ROW_BLOCKS * BLK

    def kernel(partial_ref, image_ref, data, *rest):
        copy = pltpu.make_async_copy(partial_ref, data, rest[-1])
        copy.start()
        copy.wait()
        combine_kernel(data, image_ref, data, *rest[:-1])

    return pl.pallas_call(
        kernel,
        out_shape=jax.ShapeDtypeStruct((rows, BLK), BF16),
        in_specs=[pl.BlockSpec(memory_space=pl.ANY)],
        out_specs=vmem,
        scratch_shapes=[
            pltpu.VMEM((rows, BLK), F32),
            pltpu.VMEM((2, 2, BIG // 2, BLK), F32),
            pltpu.VMEM((2, 2, BIG, BLK), F32),
            pltpu.VMEM((2, 2, SMALL // 2, BLK), F32),
            pltpu.VMEM((2, 2, SMALL, BLK), F32),
            pltpu.SemaphoreType.DMA((8, 6)),
            pltpu.SemaphoreType.DMA((8, 6)),
            pltpu.SemaphoreType.DMA,
        ],
        compiler_params=pltpu.CompilerParams(
            collective_id=1, has_side_effects=True, vmem_limit_bytes=VMEM_LIMIT
        ),
        name="combine",
    )(partial.reshape(rows, BLK))


def adjoint_kernel(count, rows, cols, sens, image, data_image, adjoint, flipped):
    step = pl.program_id(0)

    @pl.when(step == 0)
    def _():
        adjoint[...] = jnp.zeros_like(adjoint)

        def flip(b, carry):
            block = image[b].astype(F32)
            data_image[b] = block
            flipped[b] = block.T.astype(BF16)
            return carry

        lax.fori_loop(0, ROW_BLOCKS, flip, 0)

    def add(first, width):
        terms = []
        for u in range(width):
            at = rows[step * CHUNK + first + u]
            terms.append(dot(flipped[at], sens[0, first + u]))
        for u in range(width):
            at = cols[step * CHUNK + first + u]
            adjoint[0, at & 3, at >> 2] += terms[u][:HALF]
            adjoint[1, at & 3, at >> 2] += terms[u][HALF:]

    live_slots(count, step, add)


def adjoin(count, rows, cols, sens, image):
    return pl.pallas_call(
        adjoint_kernel,
        out_shape=(
            jax.ShapeDtypeStruct((ROW_BLOCKS, BLK, BLK), F32),
            jax.ShapeDtypeStruct((2, 4, NCOLS, HALF, BLK), F32),
        ),
        grid_spec=pltpu.PrefetchScalarGridSpec(
            num_scalar_prefetch=3,
            grid=(SLOTS // CHUNK,),
            in_specs=[sens_spec(), whole(ROW_BLOCKS, BLK, BLK)],
            out_specs=(whole(ROW_BLOCKS, BLK, BLK), whole(2, 4, NCOLS, HALF, BLK)),
            scratch_shapes=[pltpu.VMEM((ROW_BLOCKS, BLK, BLK), BF16)],
        ),
        compiler_params=pltpu.CompilerParams(vmem_limit_bytes=VMEM_LIMIT),
        name="adjoin",
    )(count, rows, cols, sens, image)


GROUP = NCOLS // 2


def return_kernel(partial, scale, out, stage, pair, relay_out, relay, landed, send, recv, *sem_refs):
    sems = dict(zip(EXCHANGE_NAMES, sem_refs))
    where = place()
    row, col, z, core = where
    plus, minus = z_device(z, 1, core, col), z_device(z, NZ - 1, core, col)
    partner = (z * 2 + 1 - core, col)
    greet([plus, minus, partner], (row, col))
    ring = Ring(z, plus, minus, send, recv)
    for slot, step in ((6, 2), (7, 1), (8, 3), (9, 0)):
        ring.copy(partial.at[1 - core, ring.at(step)], pair.at[ring.at(step)], partner, slot)

    def total(step, h):
        group = pl.ds(h * GROUP, GROUP)
        return partial[core, ring.at(step), group] + pair[ring.at(step), group]

    def paired(step, slot):
        ring.arrived(pair.at[ring.at(step)], slot)

    def ship(value, slot, dst, device, sem):
        relay_out[slot] = value.astype(BF16)
        ring.copy(relay_out.at[slot], dst, device, sem)

    paired(2, 6)
    ship(total(2, 0), 0, relay.at[0], plus, 0)
    ship(total(2, 1), 1, relay.at[1], minus, 1)
    paired(1, 7)
    ship(total(1, 1), 3, landed.at[0, 1], plus, 2)
    paired(3, 8)
    ship(total(3, 0), 4, landed.at[1, 0], minus, 3)
    ring.arrived(relay.at[0], 0)
    ship(total(1, 0) + relay[0].astype(F32), 2, landed.at[0, 0], plus, 4)
    ring.arrived(relay.at[1], 1)
    ship(total(3, 1) + relay[1].astype(F32), 5, landed.at[1, 1], minus, 5)
    paired(0, 9)
    ring.arrived(landed.at[0, 1], 2)
    ring.arrived(landed.at[1, 0], 3)
    ring.arrived(landed.at[0, 0], 4)
    ring.arrived(landed.at[1, 1], 5)
    lane_scale = scale[0:1, :].reshape(1, 1, BLK)
    for h in range(2):
        value = total(0, h) + landed[0, h].astype(F32) + landed[1, h].astype(F32)
        stage[pl.ds(h * GROUP, GROUP)] = (value * lane_scale).astype(BF16)

    def spread(i, carry):
        spread_copy(stage, out, sems, where, i).start()
        return carry

    lax.fori_loop(1, NCOLS, spread, 0)
    out[z, col, pl.ds(core * HALF, HALF), :] = stage[col]
    gather_rows(stage, out, sems, where)
    ring.drain()


def give_back(partial):
    vmem = pl.BlockSpec(memory_space=pltpu.VMEM)
    return pl.pallas_call(
        return_kernel,
        out_shape=jax.ShapeDtypeStruct((4, NCOLS, BLK, BLK), BF16),
        in_specs=[vmem, vmem],
        out_specs=vmem,
        scratch_shapes=[
            pltpu.VMEM((NCOLS, HALF, BLK), BF16),
            pltpu.VMEM((4, NCOLS, HALF, BLK), F32),
            pltpu.VMEM((6, GROUP, HALF, BLK), BF16),
            pltpu.VMEM((2, GROUP, HALF, BLK), BF16),
            pltpu.VMEM((2, 2, GROUP, HALF, BLK), BF16),
            pltpu.SemaphoreType.DMA((10,)),
            pltpu.SemaphoreType.DMA((10,)),
            *EXCHANGE_SEMS,
        ],
        compiler_params=pltpu.CompilerParams(
            collective_id=2, has_side_effects=True, vmem_limit_bytes=VMEM_LIMIT
        ),
        name="give_back",
    )(partial, jnp.asarray(np.broadcast_to(SCALE[None, :], (8, BLK)), F32))


def smooth_tile(extended, neighbors, weights, tile, first_cell):
    at = pl.ds(pl.multiple_of(tile * BLK, BLK), BLK)
    local = (neighbors[:, at] - (first_cell + tile * BLK - RIM)).astype(F32)
    table = jnp.concatenate([local, weights[:, at]], axis=0).T
    span = lax.broadcasted_iota(jnp.int32, (BLK, 2 * BLK), 1).astype(F32)
    mix = jnp.zeros((BLK, 2 * BLK), F32)
    for face in range(4):
        mix += jnp.where(table[:, face : face + 1] == span, table[:, 4 + face : 5 + face], 0.0)
    mix_high, mix_low = split(mix)
    near_high, near_low = split(extended[pl.ds(pl.multiple_of(tile * BLK, BLK), 2 * BLK), :])
    mixed = dot(mix_high, near_high) + dot(mix_low, near_high) + dot(mix_high, near_low)
    total = table[:, 4:5] + table[:, 5:6] + table[:, 6:7] + table[:, 7:8]
    center = extended[pl.ds(pl.multiple_of(tile * BLK + RIM, RIM), BLK), :]
    return total * center - mixed


def smooth_kernel(model, halo, neighbors, weights, out, extended, sems):
    first_cell = lax.axis_index("cols") * (COL_BLOCKS * BLK)
    cells = COL_BLOCKS * BLK
    copies = [
        pltpu.make_async_copy(model, extended.at[pl.ds(RIM, cells)], sems.at[0]),
        pltpu.make_async_copy(halo.at[0], extended.at[pl.ds(0, RIM)], sems.at[1]),
        pltpu.make_async_copy(halo.at[1], extended.at[pl.ds(RIM + cells, RIM)], sems.at[2]),
    ]
    for copy in copies:
        copy.start()
    for copy in copies:
        copy.wait()

    def tile(t, carry):
        out[pl.ds(pl.multiple_of(t * BLK, BLK), BLK), :] = smooth_tile(
            extended, neighbors, weights, t, first_cell
        )
        return carry

    lax.fori_loop(0, COL_BLOCKS, tile, 0)


def smooth(model, halo, neighbors, weights):
    vmem = pl.BlockSpec(memory_space=pltpu.VMEM)
    anywhere = pl.BlockSpec(memory_space=pl.ANY)
    return pl.pallas_call(
        smooth_kernel,
        out_shape=jax.ShapeDtypeStruct(model.shape, F32),
        in_specs=[anywhere, anywhere, vmem, vmem],
        out_specs=vmem,
        scratch_shapes=[
            pltpu.VMEM((model.shape[0] + 2 * RIM, BLK), F32),
            pltpu.SemaphoreType.DMA((3,)),
        ],
        compiler_params=pltpu.CompilerParams(vmem_limit_bytes=VMEM_LIMIT),
        name="smooth",
    )(model, halo, neighbors, weights)


TILES = 8


def synthesise_kernel(order, signs, returned, smooth_term, out, inverse):
    step = pl.program_id(0)

    @pl.when(step == 0)
    def _():
        def note(j, carry):
            inverse[order[j]] = j
            return carry

        lax.fori_loop(0, COL_BLOCKS, note, 0)

    for t in range(TILES):
        j = inverse[step * TILES + t]
        block = returned[j & 3, j >> 2]
        cells = lax.dot_general(
            signs[...], block, (((1,), (1,)), ((), ())), preferred_element_type=F32
        )
        at = slice(t * BLK, (t + 1) * BLK)
        out[at, :] = cells + smooth_term[at, :]


def synthesise(order, returned, smooth_term):
    block = pl.BlockSpec((TILES * BLK, BLK), lambda i, order: (i, 0))
    return pl.pallas_call(
        synthesise_kernel,
        out_shape=jax.ShapeDtypeStruct(smooth_term.shape, F32),
        grid_spec=pltpu.PrefetchScalarGridSpec(
            num_scalar_prefetch=1,
            grid=(COL_BLOCKS // TILES,),
            in_specs=[whole(BLK, BLK), whole(4, NCOLS, BLK, BLK), block],
            out_specs=block,
            scratch_shapes=[pltpu.SMEM((COL_BLOCKS,), jnp.int32)],
        ),
        compiler_params=pltpu.CompilerParams(vmem_limit_bytes=VMEM_LIMIT),
        name="synthesise",
    )(order, jnp.asarray(SIGNS.T, BF16), returned, smooth_term)


def local(model_dir, sens_blocks, blk_row, blk_col, blk_count, send_order, neighbors, face_weight):
    rows, cols = blk_row.reshape(-1), blk_col.reshape(-1)
    count, order = blk_count.reshape(-1), send_order.reshape(-1)
    wavelet, halo = analyse(order, model_dir)
    partial_image = forward(count, rows, cols, sens_blocks, wavelet)
    image_half = combine(partial_image).reshape(ROW_BLOCKS, BLK, BLK)
    data_image, partial_adjoint = adjoin(count, rows, cols, sens_blocks, image_half)
    returned = give_back(partial_adjoint)
    smooth_term = smooth(model_dir, halo, neighbors, face_weight)
    normal_product = synthesise(order, returned, smooth_term)
    return data_image.reshape(ROW_BLOCKS * BLK, BLK), normal_product


def solution(mesh):
    placed = (
        P("cols", None),
        P("rows", "cols", None, None),
        P("rows", "cols"),
        P("rows", "cols"),
        P("rows", "cols"),
        P("cols", None),
        P(None, "cols"),
        P(None, "cols"),
    )
    return jax.shard_map(
        local,
        mesh=mesh,
        in_specs=placed,
        out_specs=(P("rows", None), P("cols", None)),
        check_vma=False,
    )
```

time: 507 us -> 199 us (0.39)
  the two profiles are of different devices: /device:TPU:65 before, /device:TPU:1 now
where the time goes in v1:
time: 199 us; the launch traced here: 198 us
  Pallas kernels  195 us (98%)
  other arithmetic  2.53 us (1%)
    pallas_call x1, Pallas kernels, give_back(): pl.pallas_call(return_kernel, out_shape=jax.ShapeDtypeStruct((4, NCOLS, B...  50.7 us
    pallas_call x1, Pallas kernels, combine(): pl.pallas_call(kernel, out_shape=jax.ShapeDtypeStruct((rows, BLK), BF16),...  39.4 us
    pallas_call x1, Pallas kernels, smooth(): pl.pallas_call(smooth_kernel, out_shape=jax.ShapeDtypeStruct(model.shape,...  39.1 us
    pallas_call x1, Pallas kernels, analyse(): pl.pallas_call(analyse_kernel, out_shape=(jax.ShapeDtypeStruct((4, NCOLS,...  30.3 us
    pallas_call x1, Pallas kernels, adjoin(): pl.pallas_call(adjoint_kernel, out_shape=(jax.ShapeDtypeStruct((ROW_BLOCK...  15.2 us
    pallas_call x1, Pallas kernels, forward(): pl.pallas_call(forward_kernel, out_shape=jax.ShapeDtypeStruct((ROW_BLOCKS...  11 us
    pallas_call x1, Pallas kernels, synthesise(): pl.pallas_call(synthesise_kernel, out_shape=jax.ShapeDtypeStruct(smooth_t...  8.94 us

profile of v1, /device:TPU:1, one launch (start us, length us, event | category | flops | bytes accessed | tf_op | source)
XLA Modules:
  0.0 198.5 jit_solution(13441371288474376553)
XLA Ops:
  1.3 1.3 reduce.rows
  2.5 1.3 reduce.1.cols
  3.8 30.3 %analyse.1 = (bf16[4,16,128,128]{3,2,1,0:T(8,128)(2,1)}, f32[2,64,128]{2,1,0:T(8,128)}) custom-call(s32[64]{0:T(128)} %bitcast.11, f32[64,128,128]{2,1,0:T(8,128)} %bitcast.8, bf16[128,128]{1,0:T(8,128)(2,1)} %constant.8.clone.signs, f32[128,128]{1,0:T(8,128)} %constant.9.clone.scale), custom_call_target="tpu_custom_call" | custom-call | tf_op jit(solution)/shard_map/analyse/pallas_call | solution.py:232
  34.1 11.0 %forward.1 = f32[32,128,128]{2,1,0:T(8,128)} custom-call(s32[1]{0:T(128)} %bitcast.6.count, s32[384]{0:T(512)} %reduce.rows, s32[384]{0:T(512)} %reduce.1.cols, bf16[1,384,128,128]{3,2,1,0:T(8,128)(2,1)} %sens.3, bf16[4,16,128,128]{3,2,1,0:T(8,128)(2,1)} %get-tuple-element.6.wavelet), custom_call_target="tpu_custom_call" | custom-call | tf_op jit(solution)/shard_map/forward/pallas_call | solution.py:303
  45.1 39.4 %combine.1 = bf16[4096,128]{1,0:T(8,128)(2,1)} custom-call(f32[4096,128]{1,0:T(8,128)} %bitcast.9), custom_call_target="tpu_custom_call" | custom-call | tf_op jit(solution)/shard_map/combine/pallas_call | solution.py:469
  84.5 39.1 %smooth.1.smooth_term = f32[8192,128]{1,0:T(8,128)} custom-call(f32[8192,128]{1,0:T(8,128)} %model.1, f32[2,64,128]{2,1,0:T(8,128)} %get-tuple-element.9.halo, s32[4,8192]{1,0:T(4,128)} %neighbors.1, f32[4,8192]{1,0:T(4,128)} %weights.1), custom_call_target="tpu_custom_call" | custom-call | tf_op jit(solution)/shard_map/smooth/pallas_call | solution.py:659
  123.6 15.2 %adjoin.1 = (f32[32,128,128]{2,1,0:T(8,128)}, f32[2,4,16,64,128]{4,3,2,1,0:T(8,128)}) custom-call(s32[1]{0:T(128)} %bitcast.7.count, s32[384]{0:T(512)} %reduce.rows, s32[384]{0:T(512)} %reduce.1.cols, bf16[1,384,128,128]{3,2,1,0:T(8,128)(2,1)} %sens.3, bf16[32,128,128]{2,1,0:T(8,128)(2,1)} %bitcast.10), custom_call_target="tpu_custom_call" | custom-call | tf_op jit(solution)/shard_map/adjoin/pallas_call | solution.py:520
  138.8 50.7 %give_back.1.returned = bf16[4,16,128,128]{3,2,1,0:T(8,128)(2,1)} custom-call(f32[2,4,16,64,128]{4,3,2,1,0:T(8,128)} %get-tuple-element.8.partial, f32[8,128]{1,0:T(8,128)} %constant.10.clone.scale), custom_call_target="tpu_custom_call" | custom-call | tf_op jit(solution)/shard_map/give_back/pallas_call | solution.py:596
  189.5 8.9 %synthesise.1 = f32[8192,128]{1,0:T(8,128)} custom-call(s32[64]{0:T(128)} %bitcast.12, bf16[128,128]{1,0:T(8,128)(2,1)} %constant.11.clone.signs, bf16[4,16,128,128]{3,2,1,0:T(8,128)(2,1)} %give_back.1.returned, f32[8192,128]{1,0:T(8,128)} %smooth.1.smooth_term), custom_call_target="tpu_custom_call" | custom-call | tf_op jit(solution)/shard_map/synthesise/pallas_call | solution.py:699

commit v2 on v1

v2 whole, which is shorter than its diff:
```python
import math

import jax
import jax.numpy as jnp
import numpy as np
from jax import lax
from jax.experimental import pallas as pl
from jax.experimental.pallas import tpu as pltpu
from jax.sharding import PartitionSpec as P

BLK = 128
RIM = 64
NROWS = 8
NCOLS = 16
NZ = 4
ROW_BLOCKS = 32
COL_BLOCKS = 64
SLOTS = 384
CHUNK = 128
UNROLLS = (32, 4, 1)
VMEM_LIMIT = 56 << 20
MESH = pl.DeviceIdType.MESH
F32 = jnp.float32
BF16 = jnp.bfloat16


def haar_parts():
    matrix = np.ones((1, 1))
    while matrix.shape[0] < BLK:
        length = matrix.shape[0]
        upper = np.kron(matrix, np.array([[1.0, 1.0]]))
        lower = np.kron(np.eye(length), np.array([[1.0, -1.0]]))
        matrix = np.concatenate([upper, lower], axis=0) / math.sqrt(2.0)
    scale = np.abs(matrix).max(axis=1)
    signs = np.round(matrix / scale[:, None])
    return signs, scale


SIGNS, SCALE = haar_parts()


def split(value):
    high = value.astype(BF16)
    low = (value - high.astype(F32)).astype(BF16)
    return high, low


def dot(a, b):
    return jnp.dot(a, b, preferred_element_type=F32)


def remote(src, dst, send_sem, recv_sem, device):
    return pltpu.make_async_remote_copy(
        src_ref=src,
        dst_ref=dst,
        send_sem=send_sem,
        recv_sem=recv_sem,
        device_id=device,
        device_id_type=MESH,
    )


def place():
    row = lax.axis_index("rows")
    col = lax.axis_index("cols")
    return row, col, lax.div(row, 2), lax.rem(row, 2)


def z_device(z, step, core, col):
    return (lax.rem(z + step, NZ) * 2 + core, col)


def greet(devices, extra=None):
    barrier = pltpu.get_barrier_semaphore()
    for device in devices:
        pl.semaphore_signal(barrier, inc=1, device_id=device, device_id_type=MESH)
    count = len(devices)
    if extra is not None:
        first, device_of = extra

        def signal(i, carry):
            pl.semaphore_signal(barrier, inc=1, device_id=device_of(i), device_id_type=MESH)
            return carry

        lax.fori_loop(first, PARTS, signal, 0)
        count = count + PARTS - first
    pl.semaphore_wait(barrier, count)


PARTS = NCOLS // 2


class Exchange:
    def __init__(self, stage, out, sem_refs, where):
        self.stage, self.out = stage, out
        self.a_send, self.a_recv, self.g_send, self.minus, self.plus, self.far, self.pair = sem_refs
        self.row, self.col, self.z, self.core = where
        self.first = jnp.where(self.core == lax.rem(self.col, 2), 1, 0)
        self.sends = []

    def slot(self, i):
        return lax.rem(lax.div(self.col, 2) + i, PARTS)

    def device(self, i):
        return self.z * 2 + lax.rem(self.col, 2), self.slot(i) * 2 + self.core

    def arrivals(self, landing):
        return landing.at[lax.div(self.col, 2)]

    def copy(self, i, landing):
        return remote(
            self.stage.at[self.slot(i)],
            self.arrivals(landing),
            self.a_send.at[i],
            self.a_recv.at[lax.div(self.col, 2)],
            self.device(i),
        )

    def wait_part(self, m, landing):
        @pl.when(m * 2 + self.core != self.col)
        def _():
            ref = landing.at[m]
            remote(
                ref, ref, self.a_send.at[0], self.a_recv.at[m], self.device(1)
            ).wait_recv()

    def drain_parts(self, landing):
        def finish(i, carry):
            self.copy(i, landing).wait_send()
            return carry

        lax.fori_loop(self.first, PARTS, finish, 0)

    def piece(self, step, p, core=None):
        core = self.core if core is None else core
        size = PARTS // 2
        return self.out.at[lax.rem(self.z + step, NZ), core, pl.ds(p * size, size)]

    def send(self, step, p, device, recv_sem):
        piece = self.piece(step, p)
        copy = remote(piece, piece, self.g_send.at[len(self.sends)], recv_sem, device)
        copy.start()
        self.sends.append(copy)

    def arrived(self, step, p, recv_sem, core=None):
        piece = self.piece(step, p, core)
        remote(piece, piece, self.g_send.at[0], recv_sem, self.partner()).wait_recv()

    def partner(self):
        return self.z * 2 + 1 - self.core, self.col

    def neighbour(self, step):
        return z_device(self.z, step, self.core, self.col)

    def begin(self, p):
        self.send(0, p, self.neighbour(1), self.minus.at[p])
        self.send(0, p, self.neighbour(3), self.plus.at[p])
        self.send(0, p, self.partner(), self.pair.at[0, p])

    def finish(self):
        self.arrived(3, 0, self.minus.at[0])
        self.send(3, 0, self.neighbour(1), self.far.at[0])
        self.send(3, 0, self.partner(), self.pair.at[3, 0])
        self.arrived(1, 1, self.plus.at[1])
        self.send(1, 1, self.neighbour(3), self.far.at[1])
        self.send(1, 1, self.partner(), self.pair.at[1, 1])
        self.arrived(1, 0, self.plus.at[0])
        self.send(1, 0, self.partner(), self.pair.at[1, 0])
        self.arrived(3, 1, self.minus.at[1])
        self.send(3, 1, self.partner(), self.pair.at[3, 1])
        for p in range(2):
            self.arrived(2, p, self.far.at[p])
            self.send(2, p, self.partner(), self.pair.at[2, p])
        for p in range(2):
            for step in (0, 1, 3, 2):
                self.arrived(step, p, self.pair.at[step, p], 1 - self.core)
        for copy in self.sends:
            copy.wait_send()


EXCHANGE_SEMS = [
    pltpu.SemaphoreType.DMA((PARTS,)),
    pltpu.SemaphoreType.DMA((PARTS,)),
    pltpu.SemaphoreType.DMA((14,)),
    pltpu.SemaphoreType.DMA((2,)),
    pltpu.SemaphoreType.DMA((2,)),
    pltpu.SemaphoreType.DMA((2,)),
    pltpu.SemaphoreType.DMA((4, 2)),
]
CELLS = COL_BLOCKS * BLK


def cells_of(body, block):
    return jnp.concatenate([body[2 * block], body[2 * block + 1]], axis=0)


def tabulate(neighbors, weights, tables, first_cell):
    def tile(t, carry):
        at = pl.ds(pl.multiple_of(t * BLK, BLK), BLK)
        near = (neighbors[:, at] - (first_cell + t * BLK - RIM)).astype(F32)
        tables[t] = jnp.concatenate([near, weights[:, at]], axis=0)
        return carry

    lax.fori_loop(0, COL_BLOCKS, tile, 0)


def smooth_tile(body, rims, tables, tile):
    table = tables[tile].T
    span = lax.broadcasted_iota(jnp.int32, (BLK, 2 * BLK), 1).astype(F32)
    mix = jnp.zeros((BLK, 2 * BLK), F32)
    for face in range(4):
        mix += jnp.where(table[:, face : face + 1] == span, table[:, 4 + face : 5 + face], 0.0)
    mix_high, mix_low = split(mix)
    center = cells_of(body, tile)
    last = COL_BLOCKS - 1
    low = jnp.where(tile == 0, rims[0], body[jnp.maximum(2 * tile - 1, 0)])
    high = jnp.where(tile == last, rims[1], body[jnp.minimum(2 * tile + 2, 2 * last)])
    window = jnp.concatenate([low, center, high], axis=0)
    near_high, near_low = split(window)
    mixed = dot(mix_high, near_high) + dot(mix_low, near_high) + dot(mix_high, near_low)
    total = table[:, 4:5] + table[:, 5:6] + table[:, 6:7] + table[:, 7:8]
    return total * center - mixed


def analyse_kernel(
    order, model, neighbors, weights, signs, scale, wavelet, smooth, body, rims, tables, stage, sems, *sem_refs
):
    where = place()
    row, col, z, core = where
    fill = pltpu.make_async_copy(model, body, sems.at[4])
    fill.start()
    exchange = Exchange(stage, wavelet, sem_refs, where)
    below, above = (row, lax.rem(col + NCOLS - 1, NCOLS)), (row, lax.rem(col + 1, NCOLS))
    greet(
        [exchange.neighbour(1), exchange.neighbour(3), exchange.partner(), below, above],
        (exchange.first, exchange.device),
    )
    up = remote(
        model.at[2 * COL_BLOCKS - 1],
        rims.at[0],
        sems.at[0],
        sems.at[2],
        above,
    )
    down = remote(
        model.at[0],
        rims.at[1],
        sems.at[1],
        sems.at[3],
        below,
    )
    up.start()
    down.start()
    fill.wait()
    sign_pair = jnp.concatenate([signs[...], signs[...]], axis=1)
    landing = wavelet.at[z, core]
    target = wavelet.at[z, lax.rem(col, 2)]

    def block_of(m):
        return order[0, (m * 2 + core) * 4 + z]

    def coefficients(m):
        high, low = split(cells_of(body, block_of(m)))
        product = dot(sign_pair, jnp.concatenate([high, low], axis=0))
        return (product * scale[...]).astype(BF16)

    @pl.when(exchange.first == 1)
    def _():
        wavelet[z, core, lax.div(col, 2)] = coefficients(lax.div(col, 2))

    def spread(i, carry):
        stage[exchange.slot(i)] = coefficients(exchange.slot(i))
        exchange.copy(i, target).start()
        return carry

    lax.fori_loop(exchange.first, PARTS, spread, 0)
    tabulate(neighbors, weights, tables, col * CELLS)

    def smooth_one(m, carry):
        smooth[m] = smooth_tile(body, rims, tables, block_of(m))
        return carry

    up.wait_recv()
    down.wait_recv()
    lax.fori_loop(0, 3, smooth_one, 0)

    def wait_part(m, carry):
        exchange.wait_part(m, landing)
        return carry

    for p in range(2):
        lax.fori_loop(p * PARTS // 2, (p + 1) * PARTS // 2, wait_part, 0)
        exchange.begin(p)
    lax.fori_loop(3, PARTS, smooth_one, 0)
    exchange.finish()
    exchange.drain_parts(target)
    up.wait_send()
    down.wait_send()


def analyse(order, model, neighbors, weights):
    vmem = pl.BlockSpec(memory_space=pltpu.VMEM)
    return pl.pallas_call(
        analyse_kernel,
        out_shape=(
            jax.ShapeDtypeStruct((NZ, 2, PARTS, BLK, BLK), BF16),
            jax.ShapeDtypeStruct((PARTS, BLK, BLK), F32),
        ),
        in_specs=[
            pl.BlockSpec(memory_space=pltpu.SMEM),
            pl.BlockSpec(memory_space=pl.ANY),
            vmem,
            vmem,
            vmem,
            vmem,
        ],
        out_specs=(vmem, vmem),
        scratch_shapes=[
            pltpu.VMEM((2 * COL_BLOCKS, RIM, BLK), F32),
            pltpu.VMEM((2, RIM, BLK), F32),
            pltpu.VMEM((COL_BLOCKS, 8, BLK), F32),
            pltpu.VMEM((PARTS, BLK, BLK), BF16),
            pltpu.SemaphoreType.DMA((5,)),
            *EXCHANGE_SEMS,
        ],
        compiler_params=pltpu.CompilerParams(
            collective_id=0, has_side_effects=True, vmem_limit_bytes=VMEM_LIMIT
        ),
        name="analyse",
    )(
        order,
        model.reshape(2 * COL_BLOCKS, RIM, BLK),
        neighbors,
        weights,
        jnp.asarray(SIGNS, BF16),
        jnp.asarray(np.broadcast_to(SCALE[:, None], (BLK, BLK)), F32),
    )


def live_slots(count, step, add):
    live = jnp.clip(count[0, 0] - step * CHUNK, 0, CHUNK)
    done = 0
    for width in UNROLLS:

        def group(g, carry, width=width, done=done):
            add(done + g * width, width)
            return carry

        groups = (live - done) // width
        lax.fori_loop(0, groups, group, 0)
        done = done + groups * width


def forward_kernel(count, rows, cols, sens, wavelet, image):
    step = pl.program_id(0)

    @pl.when(step == 0)
    def _():
        image[...] = jnp.zeros_like(image)

    def add(first, width):
        terms = []
        for u in range(width):
            at = cols[0, step * CHUNK + first + u]
            terms.append(dot(sens[0, first + u], wavelet[at & 3, (at >> 2) & 1, at >> 3]))
        for u in range(width):
            image[rows[0, step * CHUNK + first + u]] += terms[u]

    live_slots(count, step, add)


def sens_spec():
    def index(i, count, rows, cols):
        return 0, jnp.minimum(i, (count[0, 0] - 1) // CHUNK), 0, 0

    return pl.BlockSpec((1, CHUNK, BLK, BLK), index)


def whole(*shape):
    return pl.BlockSpec(shape, lambda i, *refs: (0,) * len(shape))


def forward(count, rows, cols, sens, wavelet):
    return pl.pallas_call(
        forward_kernel,
        out_shape=jax.ShapeDtypeStruct((ROW_BLOCKS, BLK, BLK), F32),
        grid_spec=pltpu.PrefetchScalarGridSpec(
            num_scalar_prefetch=3,
            grid=(SLOTS // CHUNK,),
            in_specs=[sens_spec(), whole(NZ, 2, PARTS, BLK, BLK)],
            out_specs=whole(ROW_BLOCKS, BLK, BLK),
        ),
        compiler_params=pltpu.CompilerParams(vmem_limit_bytes=VMEM_LIMIT),
        name="forward",
    )(count, rows, cols, sens, wavelet)


class Ring:
    def __init__(self, me, plus, minus, send, recv):
        self.me, self.plus, self.minus = me, plus, minus
        self.send, self.recv = send, recv
        self.started = []

    def at(self, step):
        return lax.rem(self.me + step, 4)

    def copy(self, src, dst, device, slot):
        copy = remote(src, dst, self.send.at[slot], self.recv.at[slot], device)
        copy.start()
        self.started.append(copy)

    def arrived(self, ref, slot):
        remote(ref, ref, self.send.at[slot], self.recv.at[slot], self.plus).wait_recv()

    def drain(self):
        for copy in self.started:
            copy.wait_send()
        self.started = []


class Reduce:
    def __init__(self, ring, data, base, chunk, relay, landed):
        self.ring, self.data, self.base, self.chunk = ring, data, base, chunk
        self.half = chunk // 2
        self.relay, self.landed = relay, landed

    def rows(self, step, h):
        start = self.base + self.ring.at(step) * self.chunk + h * self.half
        return pl.ds(pl.multiple_of(start, self.half), self.half)

    def relay_at(self, side):
        return self.relay.at[side, pl.ds(0, self.half)]

    def landed_at(self, side, h):
        return self.landed.at[side, pl.ds(h * self.half, self.half)]

    def begin(self):
        ring, data = self.ring, self.data
        ring.copy(data.at[self.rows(2, 0)], self.relay_at(0), ring.plus, 0)
        ring.copy(data.at[self.rows(2, 1)], self.relay_at(1), ring.minus, 1)
        ring.copy(data.at[self.rows(1, 1)], self.landed_at(0, 1), ring.plus, 2)
        ring.copy(data.at[self.rows(3, 0)], self.landed_at(1, 0), ring.minus, 3)

    def pass_on(self):
        ring, data = self.ring, self.data
        ring.arrived(self.relay_at(0), 0)
        data[self.rows(1, 0), :] += self.relay[0, : self.half]
        ring.copy(data.at[self.rows(1, 0)], self.landed_at(0, 0), ring.plus, 4)
        ring.arrived(self.relay_at(1), 1)
        data[self.rows(3, 1), :] += self.relay[1, : self.half]
        ring.copy(data.at[self.rows(3, 1)], self.landed_at(1, 1), ring.minus, 5)

    def finish(self):
        ring, data = self.ring, self.data
        ring.arrived(self.landed_at(0, 1), 2)
        ring.arrived(self.landed_at(1, 0), 3)
        ring.arrived(self.landed_at(0, 0), 4)
        ring.arrived(self.landed_at(1, 1), 5)
        for h in range(2):
            part = pl.ds(h * self.half, self.half)
            data[self.rows(0, h), :] += self.landed[0, part, :] + self.landed[1, part, :]


class Gather:
    def __init__(self, ring, data, base, chunk):
        self.ring, self.data, self.base, self.chunk = ring, data, base, chunk

    def rows(self, step, h=None):
        start = self.base + self.ring.at(step) * self.chunk
        if h is None:
            return self.data.at[pl.ds(pl.multiple_of(start, self.chunk), self.chunk)]
        half = self.chunk // 2
        return self.data.at[pl.ds(pl.multiple_of(start + h * half, half), half)]

    def begin(self):
        ring = self.ring
        ring.copy(self.rows(0), self.rows(0), ring.plus, 0)
        ring.copy(self.rows(0), self.rows(0), ring.minus, 1)

    def pass_on(self):
        ring = self.ring
        ring.arrived(self.rows(3), 0)
        ring.copy(self.rows(3, 0), self.rows(3, 0), ring.plus, 2)
        ring.arrived(self.rows(1), 1)
        ring.copy(self.rows(1, 1), self.rows(1, 1), ring.minus, 3)

    def finish(self):
        ring = self.ring
        ring.arrived(self.rows(2, 0), 2)
        ring.arrived(self.rows(2, 1), 3)


HALF_ROWS = ROW_BLOCKS * BLK // 2
BIG = HALF_ROWS // 4
SMALL = BIG // 4


def combine_kernel(partial, image, fill, big_relay, big_landed, small_relay, small_landed, send, recv):
    row, col, _, _ = place()
    y, x = lax.div(col, 4), lax.rem(col, 4)
    x_plus, x_minus = (row, y * 4 + lax.rem(x + 1, 4)), (row, y * 4 + lax.rem(x + 3, 4))
    y_plus, y_minus = (row, lax.rem(y + 1, 4) * 4 + x), (row, lax.rem(y + 3, 4) * 4 + x)
    greet([x_plus, x_minus, y_plus, y_minus])
    fill.wait()

    def ring(axis, slot):
        sems = send.at[slot], recv.at[slot]
        return Ring(x, x_plus, x_minus, *sems) if axis == 0 else Ring(y, y_plus, y_minus, *sems)

    def both(stages):
        for stage in stages:
            stage.begin()
        for stage in stages:
            stage.pass_on()
        for stage in stages:
            stage.finish()

    bases = [0, HALF_ROWS]
    inner = [x * BIG, HALF_ROWS + y * BIG]
    rings = [ring(a, a) for a in range(2)]
    wide = [Reduce(rings[a], partial, bases[a], BIG, big_relay.at[a], big_landed.at[a]) for a in range(2)]
    both(wide)
    cross = [ring(1 - a, 2 + a) for a in range(2)]
    narrow = [
        Reduce(cross[a], partial, inner[a], SMALL, small_relay.at[a], small_landed.at[a])
        for a in range(2)
    ]
    both(narrow)
    for a, other in ((0, y), (1, x)):
        own = pl.ds(pl.multiple_of(inner[a] + other * SMALL, SMALL), SMALL)
        image[own, :] = partial[own, :].astype(BF16)
    back = [ring(1 - a, 4 + a) for a in range(2)]
    both([Gather(back[a], image, inner[a], SMALL) for a in range(2)])
    last = [ring(a, 6 + a) for a in range(2)]
    both([Gather(last[a], image, bases[a], BIG) for a in range(2)])
    for group in (rings, cross, back, last):
        for one in group:
            one.drain()


def combine(partial):
    vmem = pl.BlockSpec(memory_space=pltpu.VMEM)
    rows = ROW_BLOCKS * BLK

    def kernel(partial_ref, image_ref, data, *rest):
        copy = pltpu.make_async_copy(partial_ref, data, rest[-1])
        copy.start()
        combine_kernel(data, image_ref, copy, *rest[:-1])

    return pl.pallas_call(
        kernel,
        out_shape=jax.ShapeDtypeStruct((rows, BLK), BF16),
        in_specs=[pl.BlockSpec(memory_space=pl.ANY)],
        out_specs=vmem,
        scratch_shapes=[
            pltpu.VMEM((rows, BLK), F32),
            pltpu.VMEM((2, 2, BIG // 2, BLK), F32),
            pltpu.VMEM((2, 2, BIG, BLK), F32),
            pltpu.VMEM((2, 2, SMALL // 2, BLK), F32),
            pltpu.VMEM((2, 2, SMALL, BLK), F32),
            pltpu.SemaphoreType.DMA((8, 6)),
            pltpu.SemaphoreType.DMA((8, 6)),
            pltpu.SemaphoreType.DMA,
        ],
        compiler_params=pltpu.CompilerParams(
            collective_id=1, has_side_effects=True, vmem_limit_bytes=VMEM_LIMIT
        ),
        name="combine",
    )(partial.reshape(rows, BLK))


def adjoint_kernel(count, rows, cols, sens, image, data_image, adjoint, flipped):
    step = pl.program_id(0)

    @pl.when(step == 0)
    def _():
        adjoint[...] = jnp.zeros_like(adjoint)

        def flip(b, carry):
            block = image[b].astype(F32)
            data_image[b] = block
            flipped[b] = block.T.astype(BF16)
            return carry

        lax.fori_loop(0, ROW_BLOCKS, flip, 0)

    def add(first, width):
        terms = []
        for u in range(width):
            at = rows[0, step * CHUNK + first + u]
            terms.append(dot(flipped[at], sens[0, first + u]))
        for u in range(width):
            at = cols[0, step * CHUNK + first + u]
            adjoint[(at >> 2) & 1, at & 3, at >> 3] += terms[u]

    live_slots(count, step, add)


def adjoin(count, rows, cols, sens, image):
    return pl.pallas_call(
        adjoint_kernel,
        out_shape=(
            jax.ShapeDtypeStruct((ROW_BLOCKS, BLK, BLK), F32),
            jax.ShapeDtypeStruct((2, NZ, PARTS, BLK, BLK), F32),
        ),
        grid_spec=pltpu.PrefetchScalarGridSpec(
            num_scalar_prefetch=3,
            grid=(SLOTS // CHUNK,),
            in_specs=[sens_spec(), whole(ROW_BLOCKS, BLK, BLK)],
            out_specs=(whole(ROW_BLOCKS, BLK, BLK), whole(2, NZ, PARTS, BLK, BLK)),
            scratch_shapes=[pltpu.VMEM((ROW_BLOCKS, BLK, BLK), BF16)],
        ),
        compiler_params=pltpu.CompilerParams(vmem_limit_bytes=VMEM_LIMIT),
        name="adjoin",
    )(count, rows, cols, sens, image)


GROUP = PARTS // 2


def return_kernel(
    partial, smooth, scale, signs, out, own, stage, pair, relay_out, relay, landed, gathered, sem, send, recv, *sem_refs
):
    where = place()
    row, col, z, core = where
    fill = pltpu.make_async_copy(partial.at[core], own, sem)
    fill.start()
    exchange = Exchange(stage, out, sem_refs, where)
    plus, minus, partner = exchange.neighbour(1), exchange.neighbour(3), exchange.partner()
    greet([plus, minus, partner], (exchange.first, exchange.device))
    ring = Ring(z, plus, minus, send, recv)
    for slot, step in ((6, 2), (7, 1), (8, 3), (9, 0)):
        ring.copy(partial.at[1 - core, ring.at(step)], pair.at[ring.at(step)], partner, slot)
    fill.wait()

    def total(step, h):
        group = pl.ds(h * GROUP, GROUP)
        return own[ring.at(step), group] + pair[ring.at(step), group]

    def paired(step, slot):
        ring.arrived(pair.at[ring.at(step)], slot)

    def ship(value, slot, dst, device, sem):
        relay_out[slot] = value.astype(BF16)
        ring.copy(relay_out.at[slot], dst, device, sem)

    paired(2, 6)
    ship(total(2, 0), 0, relay.at[0], plus, 0)
    ship(total(2, 1), 1, relay.at[1], minus, 1)
    paired(1, 7)
    ship(total(1, 1), 3, landed.at[0, 1], plus, 2)
    paired(3, 8)
    ship(total(3, 0), 4, landed.at[1, 0], minus, 3)
    ring.arrived(relay.at[0], 0)
    ship(total(1, 0) + relay[0].astype(F32), 2, landed.at[0, 0], plus, 4)
    ring.arrived(relay.at[1], 1)
    ship(total(3, 1) + relay[1].astype(F32), 5, landed.at[1, 1], minus, 5)
    paired(0, 9)
    ring.arrived(landed.at[0, 1], 2)
    ring.arrived(landed.at[1, 0], 3)
    ring.arrived(landed.at[0, 0], 4)
    ring.arrived(landed.at[1, 1], 5)
    lane_scale = scale[0:1, :].reshape(1, 1, BLK)
    for h in range(2):
        value = total(0, h) + landed[0, h].astype(F32) + landed[1, h].astype(F32)
        stage[pl.ds(h * GROUP, GROUP)] = (value * lane_scale).astype(BF16)

    @pl.when(exchange.first == 1)
    def _():
        gathered[lax.div(col, 2)] = stage[lax.div(col, 2)]

    def spread(i, carry):
        exchange.copy(i, gathered).start()
        return carry

    lax.fori_loop(exchange.first, PARTS, spread, 0)

    def synthesise(m, carry):
        exchange.wait_part(m, gathered)
        cells = lax.dot_general(
            signs[...], gathered[m], (((1,), (1,)), ((), ())), preferred_element_type=F32
        )
        out[z, core, m] = (cells + smooth[m]).astype(BF16)
        return carry

    for p in range(2):
        lax.fori_loop(p * GROUP, (p + 1) * GROUP, synthesise, 0)
        exchange.begin(p)
    exchange.finish()
    exchange.drain_parts(gathered)
    ring.drain()


def give_back(partial, smooth):
    vmem = pl.BlockSpec(memory_space=pltpu.VMEM)
    return pl.pallas_call(
        return_kernel,
        out_shape=jax.ShapeDtypeStruct((NZ, 2, PARTS, BLK, BLK), BF16),
        in_specs=[pl.BlockSpec(memory_space=pl.ANY), vmem, vmem, vmem],
        out_specs=vmem,
        scratch_shapes=[
            pltpu.VMEM((NZ, PARTS, BLK, BLK), F32),
            pltpu.VMEM((PARTS, BLK, BLK), BF16),
            pltpu.VMEM((NZ, PARTS, BLK, BLK), F32),
            pltpu.VMEM((6, GROUP, BLK, BLK), BF16),
            pltpu.VMEM((2, GROUP, BLK, BLK), BF16),
            pltpu.VMEM((2, 2, GROUP, BLK, BLK), BF16),
            pltpu.VMEM((PARTS, BLK, BLK), BF16),
            pltpu.SemaphoreType.DMA,
            pltpu.SemaphoreType.DMA((10,)),
            pltpu.SemaphoreType.DMA((10,)),
            *EXCHANGE_SEMS,
        ],
        compiler_params=pltpu.CompilerParams(
            collective_id=2, has_side_effects=True, vmem_limit_bytes=VMEM_LIMIT
        ),
        name="give_back",
    )(
        partial,
        smooth,
        jnp.asarray(np.broadcast_to(SCALE[None, :], (8, BLK)), F32),
        jnp.asarray(SIGNS.T, BF16),
    )


TILES = 8


def place_kernel(order, product, out, inverse):
    step = pl.program_id(0)

    @pl.when(step == 0)
    def _():
        def note(j, carry):
            inverse[order[0, j]] = j
            return carry

        lax.fori_loop(0, COL_BLOCKS, note, 0)

    for t in range(TILES):
        j = inverse[step * TILES + t]
        out[t * BLK : (t + 1) * BLK, :] = product[j & 3, (j >> 2) & 1, j >> 3].astype(F32)


def place_cells(order, product):
    return pl.pallas_call(
        place_kernel,
        out_shape=jax.ShapeDtypeStruct((CELLS, BLK), F32),
        grid_spec=pltpu.PrefetchScalarGridSpec(
            num_scalar_prefetch=1,
            grid=(COL_BLOCKS // TILES,),
            in_specs=[whole(NZ, 2, PARTS, BLK, BLK)],
            out_specs=pl.BlockSpec((TILES * BLK, BLK), lambda i, order: (i, 0)),
            scratch_shapes=[pltpu.SMEM((COL_BLOCKS,), jnp.int32)],
        ),
        compiler_params=pltpu.CompilerParams(vmem_limit_bytes=VMEM_LIMIT),
        name="place_cells",
    )(order, product)


def local(model_dir, sens_blocks, blk_row, blk_col, blk_count, send_order, neighbors, face_weight):
    wavelet, smooth = analyse(send_order, model_dir, neighbors, face_weight)
    partial_image = forward(blk_count, blk_row, blk_col, sens_blocks, wavelet)
    image_half = combine(partial_image).reshape(ROW_BLOCKS, BLK, BLK)
    data_image, partial_adjoint = adjoin(blk_count, blk_row, blk_col, sens_blocks, image_half)
    normal_product = place_cells(send_order, give_back(partial_adjoint, smooth))
    return data_image.reshape(ROW_BLOCKS * BLK, BLK), normal_product


def solution(mesh):
    placed = (
        P("cols", None),
        P("rows", "cols", None, None),
        P("rows", "cols"),
        P("rows", "cols"),
        P("rows", "cols"),
        P("cols", None),
        P(None, "cols"),
        P(None, "cols"),
    )
    return jax.shard_map(
        local,
        mesh=mesh,
        in_specs=placed,
        out_specs=(P("rows", None), P("cols", None)),
        check_vma=False,
    )
```

time: 199 us -> 135 us (0.68)
  Pallas kernels: 195 us -> 134 us
  other arithmetic: 2.53 us -> 0 us
    pallas_call x4 -> x3, Pallas kernels: 129 us -> 77 us  [the longest x1 41.6 us: give_back(): pl.pallas_call(return_kernel, out_shape=jax.ShapeDtypeStruct((NZ, 2, PART...]
    pallas_call x1, Pallas kernels: 39.4 us -> 32.5 us  [combine(): pl.pallas_call(kernel, out_shape=jax.ShapeDtypeStruct((rows, BLK), BF16),...]
    unnamed x2 -> x0, other arithmetic: 2.53 us -> none
where the time goes in v2:
time: 135 us
  Pallas kernels  134 us (99%)
    pallas_call x1, Pallas kernels, give_back(): pl.pallas_call(return_kernel, out_shape=jax.ShapeDtypeStruct((NZ, 2, PART...  41.6 us
    pallas_call x1, Pallas kernels, combine(): pl.pallas_call(kernel, out_shape=jax.ShapeDtypeStruct((rows, BLK), BF16),...  32.5 us
    pallas_call x1, Pallas kernels, analyse(): pl.pallas_call(analyse_kernel, out_shape=(jax.ShapeDtypeStruct((NZ, 2, PA...  29.7 us
    pallas_call x1, Pallas kernels, adjoin(): pl.pallas_call(adjoint_kernel, out_shape=(jax.ShapeDtypeStruct((ROW_BLOCK...  14.3 us
    pallas_call x1, Pallas kernels, forward(): pl.pallas_call(forward_kernel, out_shape=jax.ShapeDtypeStruct((ROW_BLOCKS...  9.89 us
    pallas_call x1, Pallas kernels, place_cells(): pl.pallas_call(place_kernel, out_shape=jax.ShapeDtypeStruct((CELLS, BLK),...  5.77 us

profile of v2, /device:TPU:1, one launch (start us, length us, event | category | flops | bytes accessed | tf_op | source)
XLA Modules:
  0.0 135.0 jit_solution(12824826998316075642)
XLA Ops:
  1.3 29.7 %analyse.1 = (bf16[4,2,8,128,128]{4,3,2,1,0:T(8,128)(2,1)}, f32[8,128,128]{2,1,0:T(8,128)}) custom-call(s32[1,64]{1,0:T(1,128)} %order.3, f32[128,64,128]{2,1,0:T(8,128)} %bitcast.6, s32[4,8192]{1,0:T(4,128)} %neighbors.1, f32[4,8192]{1,0:T(4,128)} %weights.1, bf16[128,128]{1,0:T(8,128)(2,1)} %constant.8.clone.signs, f32[128,128]{1,0:T(8,128)} %constant.9.clone.scale), custom_call_target="tpu_custom_call" | custom-call | tf_op jit(solution)/shard_map/analyse/pallas_call | solution.py:303
  30.9 9.9 %forward.1 = f32[32,128,128]{2,1,0:T(8,128)} custom-call(s32[1,1]{1,0:T(1,128)S(6)} %copy.14.count, s32[1,384]{1,0:T(1,128)} %rows.3, s32[1,384]{1,0:T(1,128)} %cols.3, bf16[1,384,128,128]{3,2,1,0:T(8,128)(2,1)} %sens.3, bf16[4,2,8,128,128]{4,3,2,1,0:T(8,128)(2,1)} %get-tuple-element.6.wavelet), custom_call_target="tpu_custom_call" | custom-call | tf_op jit(solution)/shard_map/forward/pallas_call | solution.py:384
  40.8 32.5 %combine.1 = bf16[4096,128]{1,0:T(8,128)(2,1)} custom-call(f32[4096,128]{1,0:T(8,128)} %bitcast.4), custom_call_target="tpu_custom_call" | custom-call | tf_op jit(solution)/shard_map/combine/pallas_call | solution.py:550
  73.4 14.3 %adjoin.1 = (f32[32,128,128]{2,1,0:T(8,128)}, f32[2,4,8,128,128]{4,3,2,1,0:T(8,128)}) custom-call(s32[1,1]{1,0:T(1,128)S(6)} %copy.14.count, s32[1,384]{1,0:T(1,128)} %rows.3, s32[1,384]{1,0:T(1,128)} %cols.3, bf16[1,384,128,128]{3,2,1,0:T(8,128)(2,1)} %sens.3, bf16[32,128,128]{2,1,0:T(8,128)(2,1)} %bitcast.5), custom_call_target="tpu_custom_call" | custom-call | tf_op jit(solution)/shard_map/adjoin/pallas_call | solution.py:600
  87.6 41.6 %give_back.1.product = bf16[4,2,8,128,128]{4,3,2,1,0:T(8,128)(2,1)} custom-call(f32[2,4,8,128,128]{4,3,2,1,0:T(8,128)} %get-tuple-element.8.partial, f32[8,128,128]{2,1,0:T(8,128)} %get-tuple-element.9.smooth, f32[8,128]{1,0:T(8,128)} %constant.10.clone.scale, bf16[128,128]{1,0:T(8,128)(2,1)} %constant.11.clone.signs), custom_call_target="tpu_custom_call" | custom-call | tf_op jit(solution)/shard_map/give_back/pallas_call | solution.py:696
  129.2 5.8 %place_cells.1 = f32[8192,128]{1,0:T(8,128)} custom-call(s32[1,64]{1,0:T(1,128)} %order.3, bf16[4,2,8,128,128]{4,3,2,1,0:T(8,128)(2,1)} %give_back.1.product), custom_call_target="tpu_custom_call" | custom-call | tf_op jit(solution)/shard_map/place_cells/pallas_call | solution.py:746

commit v3 on v2

--- a/solution.py
+++ b/solution.py
@@ -16,12 +16,20 @@
 ROW_BLOCKS = 32
 COL_BLOCKS = 64
 SLOTS = 384
-CHUNK = 128
-UNROLLS = (32, 4, 1)
+CHUNK = 32
 VMEM_LIMIT = 56 << 20
 MESH = pl.DeviceIdType.MESH
 F32 = jnp.float32
 BF16 = jnp.bfloat16
+
+
+VMEM = pl.BlockSpec(memory_space=pltpu.VMEM)
+SMEM = pl.BlockSpec(memory_space=pltpu.SMEM)
+ANY = pl.BlockSpec(memory_space=pl.ANY)
+
+
+def cost(flops, moved):
+    return pl.CostEstimate(flops=flops, bytes_accessed=moved, transcendentals=0)
 
 
 def haar_parts():
@@ -223,12 +231,41 @@
 
 
 def analyse_kernel(
-    order, model, neighbors, weights, signs, scale, wavelet, smooth, body, rims, tables, stage, sems, *sem_refs
+    order,
+    model,
+    neighbors_hbm,
+    weights_hbm,
+    signs_hbm,
+    scale_hbm,
+    wavelet,
+    smooth,
+    body,
+    neighbors,
+    weights,
+    signs,
+    scale,
+    rims,
+    tables,
+    stage,
+    sems,
+    *sem_refs,
 ):
     where = place()
     row, col, z, core = where
-    fill = pltpu.make_async_copy(model, body, sems.at[4])
-    fill.start()
+    fills = [
+        pltpu.make_async_copy(src, dst, sems.at[4 + i])
+        for i, (src, dst) in enumerate(
+            (
+                (model, body),
+                (signs_hbm, signs),
+                (scale_hbm, scale),
+                (neighbors_hbm, neighbors),
+                (weights_hbm, weights),
+            )
+        )
+    ]
+    for fill in fills:
+        fill.start()
     exchange = Exchange(stage, wavelet, sem_refs, where)
     below, above = (row, lax.rem(col + NCOLS - 1, NCOLS)), (row, lax.rem(col + 1, NCOLS))
     greet(
@@ -251,7 +288,8 @@
     )
     up.start()
     down.start()
-    fill.wait()
+    for fill in fills:
+        fill.wait()
     sign_pair = jnp.concatenate([signs[...], signs[...]], axis=1)
     landing = wavelet.at[z, core]
     target = wavelet.at[z, lax.rem(col, 2)]
@@ -299,33 +337,30 @@
 
 
 def analyse(order, model, neighbors, weights):
-    vmem = pl.BlockSpec(memory_space=pltpu.VMEM)
     return pl.pallas_call(
         analyse_kernel,
         out_shape=(
             jax.ShapeDtypeStruct((NZ, 2, PARTS, BLK, BLK), BF16),
             jax.ShapeDtypeStruct((PARTS, BLK, BLK), F32),
         ),
-        in_specs=[
-            pl.BlockSpec(memory_space=pltpu.SMEM),
-            pl.BlockSpec(memory_space=pl.ANY),
-            vmem,
-            vmem,
-            vmem,
-            vmem,
-        ],
-        out_specs=(vmem, vmem),
+        in_specs=[SMEM, *[ANY] * 5],
+        out_specs=(VMEM, VMEM),
         scratch_shapes=[
             pltpu.VMEM((2 * COL_BLOCKS, RIM, BLK), F32),
+            pltpu.VMEM((4, CELLS), jnp.int32),
+            pltpu.VMEM((4, CELLS), F32),
+            pltpu.VMEM((BLK, BLK), BF16),
+            pltpu.VMEM((BLK, BLK), F32),
             pltpu.VMEM((2, RIM, BLK), F32),
             pltpu.VMEM((COL_BLOCKS, 8, BLK), F32),
             pltpu.VMEM((PARTS, BLK, BLK), BF16),
-            pltpu.SemaphoreType.DMA((5,)),
+            pltpu.SemaphoreType.DMA((9,)),
             *EXCHANGE_SEMS,
         ],
         compiler_params=pltpu.CompilerParams(
             collective_id=0, has_side_effects=True, vmem_limit_bytes=VMEM_LIMIT
         ),
+        cost_estimate=cost(1 << 30, 60 << 20),
         name="analyse",
     )(
         order,
@@ -337,67 +372,94 @@
     )
 
 
-def live_slots(count, step, add):
-    live = jnp.clip(count[0, 0] - step * CHUNK, 0, CHUNK)
-    done = 0
-    for width in UNROLLS:
-
-        def group(g, carry, width=width, done=done):
-            add(done + g * width, width)
+class Sensors:
+    def __init__(self, count, source, held, sems):
+        self.live, self.source, self.held, self.sems = count[0, 0], source, held, sems
+
+    def copy(self, g):
+        part = pl.ds(g * CHUNK, CHUNK)
+        return pltpu.make_async_copy(self.source.at[0, part], self.held.at[part], self.sems.at[g])
+
+    def start(self):
+        def begin(g, carry):
+            self.copy(g).start()
             return carry
 
-        groups = (live - done) // width
-        lax.fori_loop(0, groups, group, 0)
-        done = done + groups * width
-
-
-def forward_kernel(count, rows, cols, sens, wavelet, image):
-    step = pl.program_id(0)
-
-    @pl.when(step == 0)
-    def _():
-        image[...] = jnp.zeros_like(image)
+        lax.fori_loop(0, pl.cdiv(self.live, CHUNK), begin, 0)
+
+    def run(self, add):
+        full = self.live // CHUNK
+
+        def group(g, carry):
+            self.copy(g).wait()
+            add(g * CHUNK, CHUNK)
+            return carry
+
+        lax.fori_loop(0, full, group, 0)
+        done = full * CHUNK
+
+        @pl.when(done < self.live)
+        def _():
+            self.copy(full).wait()
+
+        for width in (4, 1):
+
+            def few(g, carry, width=width, done=done):
+                add(done + g * width, width)
+                return carry
+
+            groups = (self.live - done) // width
+            lax.fori_loop(0, groups, few, 0)
+            done = done + groups * width
+
+
+def forward_kernel(count, rows, cols, source, wavelet_hbm, image, held, wavelet, sem, sems):
+    load = pltpu.make_async_copy(wavelet_hbm, wavelet, sem)
+    load.start()
+    sensors = Sensors(count, source, held, sems)
+    sensors.start()
+    image[...] = jnp.zeros_like(image)
+    load.wait()
 
     def add(first, width):
         terms = []
         for u in range(width):
-            at = cols[0, step * CHUNK + first + u]
-            terms.append(dot(sens[0, first + u], wavelet[at & 3, (at >> 2) & 1, at >> 3]))
+            at = cols[0, first + u]
+            terms.append(dot(held[first + u], wavelet[at & 3, (at >> 2) & 1, at >> 3]))
         for u in range(width):
-            image[rows[0, step * CHUNK + first + u]] += terms[u]
-
-    live_slots(count, step, add)
-
-
-def sens_spec():
-    def index(i, count, rows, cols):
-        return 0, jnp.minimum(i, (count[0, 0] - 1) // CHUNK), 0, 0
-
-    return pl.BlockSpec((1, CHUNK, BLK, BLK), index)
-
-
-def whole(*shape):
-    return pl.BlockSpec(shape, lambda i, *refs: (0,) * len(shape))
+            image[rows[0, first + u]] += terms[u]
+
+    sensors.run(add)
+
+
+SENSOR_SCRATCH = (
+    pltpu.VMEM((SLOTS, BLK, BLK), BF16),
+    pltpu.SemaphoreType.DMA((SLOTS // CHUNK,)),
+)
 
 
 def forward(count, rows, cols, sens, wavelet):
+    held, sems = SENSOR_SCRATCH
     return pl.pallas_call(
         forward_kernel,
         out_shape=jax.ShapeDtypeStruct((ROW_BLOCKS, BLK, BLK), F32),
-        grid_spec=pltpu.PrefetchScalarGridSpec(
-            num_scalar_prefetch=3,
-            grid=(SLOTS // CHUNK,),
-            in_specs=[sens_spec(), whole(NZ, 2, PARTS, BLK, BLK)],
-            out_specs=whole(ROW_BLOCKS, BLK, BLK),
-        ),
+        in_specs=[SMEM, SMEM, SMEM, ANY, ANY],
+        out_specs=VMEM,
+        scratch_shapes=[
+            held,
+            pltpu.VMEM(wavelet.shape, BF16),
+            pltpu.SemaphoreType.DMA,
+            sems,
+        ],
         compiler_params=pltpu.CompilerParams(vmem_limit_bytes=VMEM_LIMIT),
         name="forward",
     )(count, rows, cols, sens, wavelet)
 
 
 class Ring:
-    def __init__(self, me, plus, minus, send, recv):
+    def __init__(self, me, plus, minus, send, recv, far=None):
         self.me, self.plus, self.minus = me, plus, minus
+        self.others = ((2, far), (1, plus), (3, minus))
         self.send, self.recv = send, recv
         self.started = []
 
@@ -461,33 +523,49 @@
             data[self.rows(0, h), :] += self.landed[0, part, :] + self.landed[1, part, :]
 
 
-class Gather:
+class DirectReduce:
+    def __init__(self, ring, data, base, chunk, landed):
+        self.ring, self.data, self.base, self.chunk = ring, data, base, chunk
+        self.landed = landed
+
+    def rows(self, step):
+        start = self.base + self.ring.at(step) * self.chunk
+        return pl.ds(pl.multiple_of(start, self.chunk), self.chunk)
+
+    def begin(self):
+        for step, device in self.ring.others:
+            self.ring.copy(
+                self.data.at[self.rows(step)], self.landed.at[step - 1], device, step - 1
+            )
+
+    def pass_on(self):
+        for step in range(3):
+            self.ring.arrived(self.landed.at[step], step)
+
+    def finish(self):
+        own = self.rows(0)
+        total = self.data[own, :] + self.landed[0]
+        self.data[own, :] = total + (self.landed[1] + self.landed[2])
+
+
+class DirectGather:
     def __init__(self, ring, data, base, chunk):
         self.ring, self.data, self.base, self.chunk = ring, data, base, chunk
 
-    def rows(self, step, h=None):
+    def rows(self, step):
         start = self.base + self.ring.at(step) * self.chunk
-        if h is None:
-            return self.data.at[pl.ds(pl.multiple_of(start, self.chunk), self.chunk)]
-        half = self.chunk // 2
-        return self.data.at[pl.ds(pl.multiple_of(start + h * half, half), half)]
+        return self.data.at[pl.ds(pl.multiple_of(start, self.chunk), self.chunk)]
 
     def begin(self):
-        ring = self.ring
-        ring.copy(self.rows(0), self.rows(0), ring.plus, 0)
-        ring.copy(self.rows(0), self.rows(0), ring.minus, 1)
+        for step, device in self.ring.others:
+            self.ring.copy(self.rows(0), self.rows(0), device, step - 1)
 
     def pass_on(self):
-        ring = self.ring
-        ring.arrived(self.rows(3), 0)
-        ring.copy(self.rows(3, 0), self.rows(3, 0), ring.plus, 2)
-        ring.arrived(self.rows(1), 1)
-        ring.copy(self.rows(1, 1), self.rows(1, 1), ring.minus, 3)
+        pass
 
     def finish(self):
-        ring = self.ring
-        ring.arrived(self.rows(2, 0), 2)
-        ring.arrived(self.rows(2, 1), 3)
+        for step in (1, 3, 2):
+            self.ring.arrived(self.rows(4 - step), step - 1)
 
 
 HALF_ROWS = ROW_BLOCKS * BLK // 2
@@ -495,17 +573,17 @@
 SMALL = BIG // 4
 
 
-def combine_kernel(partial, image, fill, big_relay, big_landed, small_relay, small_landed, send, recv):
+def combine_kernel(partial, image, fill, big_relay, big_landed, small_landed, send, recv):
     row, col, _, _ = place()
     y, x = lax.div(col, 4), lax.rem(col, 4)
-    x_plus, x_minus = (row, y * 4 + lax.rem(x + 1, 4)), (row, y * 4 + lax.rem(x + 3, 4))
-    y_plus, y_minus = (row, lax.rem(y + 1, 4) * 4 + x), (row, lax.rem(y + 3, 4) * 4 + x)
-    greet([x_plus, x_minus, y_plus, y_minus])
+    x_ring = [(row, y * 4 + lax.rem(x + step, 4)) for step in range(4)]
+    y_ring = [(row, lax.rem(y + step, 4) * 4 + x) for step in range(4)]
+    greet(x_ring[1:] + y_ring[1:])
     fill.wait()
 
     def ring(axis, slot):
-        sems = send.at[slot], recv.at[slot]
-        return Ring(x, x_plus, x_minus, *sems) if axis == 0 else Ring(y, y_plus, y_minus, *sems)
+        me, devices = ((x, x_ring), (y, y_ring))[axis]
+        return Ring(me, devices[1], devices[3], send.at[slot], recv.at[slot], devices[2])
 
     def both(stages):
         for stage in stages:
@@ -521,18 +599,14 @@
     wide = [Reduce(rings[a], partial, bases[a], BIG, big_relay.at[a], big_landed.at[a]) for a in range(2)]
     both(wide)
     cross = [ring(1 - a, 2 + a) for a in range(2)]
-    narrow = [
-        Reduce(cross[a], partial, inner[a], SMALL, small_relay.at[a], small_landed.at[a])
-        for a in range(2)
-    ]
-    both(narrow)
+    both([DirectReduce(cross[a], partial, inner[a], SMALL, small_landed.at[a]) for a in range(2)])
     for a, other in ((0, y), (1, x)):
         own = pl.ds(pl.multiple_of(inner[a] + other * SMALL, SMALL), SMALL)
         image[own, :] = partial[own, :].astype(BF16)
     back = [ring(1 - a, 4 + a) for a in range(2)]
-    both([Gather(back[a], image, inner[a], SMALL) for a in range(2)])
+    both([DirectGather(back[a], image, inner[a], SMALL) for a in range(2)])
     last = [ring(a, 6 + a) for a in range(2)]
-    both([Gather(last[a], image, bases[a], BIG) for a in range(2)])
+    both([DirectGather(last[a], image, bases[a], BIG) for a in range(2)])
     for group in (rings, cross, back, last):
         for one in group:
             one.drain()
@@ -556,8 +630,7 @@
             pltpu.VMEM((rows, BLK), F32),
             pltpu.VMEM((2, 2, BIG // 2, BLK), F32),
             pltpu.VMEM((2, 2, BIG, BLK), F32),
-            pltpu.VMEM((2, 2, SMALL // 2, BLK), F32),
-            pltpu.VMEM((2, 2, SMALL, BLK), F32),
+            pltpu.VMEM((2, 3, SMALL, BLK), F32),
             pltpu.SemaphoreType.DMA((8, 6)),
             pltpu.SemaphoreType.DMA((8, 6)),
             pltpu.SemaphoreType.DMA,
@@ -565,51 +638,61 @@
         compiler_params=pltpu.CompilerParams(
             collective_id=1, has_side_effects=True, vmem_limit_bytes=VMEM_LIMIT
         ),
+        cost_estimate=cost(1 << 20, 80 << 20),
         name="combine",
     )(partial.reshape(rows, BLK))
 
 
-def adjoint_kernel(count, rows, cols, sens, image, data_image, adjoint, flipped):
-    step = pl.program_id(0)
-
-    @pl.when(step == 0)
-    def _():
-        adjoint[...] = jnp.zeros_like(adjoint)
-
-        def flip(b, carry):
-            block = image[b].astype(F32)
-            data_image[b] = block
-            flipped[b] = block.T.astype(BF16)
-            return carry
-
-        lax.fori_loop(0, ROW_BLOCKS, flip, 0)
+def adjoint_kernel(
+    count, rows, cols, source, image_hbm, data_image, adjoint, held, image, flipped, plain, sem, sems
+):
+    load = pltpu.make_async_copy(image_hbm, image, sem.at[0])
+    load.start()
+    sensors = Sensors(count, source, held, sems)
+    sensors.start()
+    adjoint[...] = jnp.zeros_like(adjoint)
+    load.wait()
+
+    def flip(b, carry):
+        block = image[b].astype(F32)
+        plain[b] = block
+        flipped[b] = block.T.astype(BF16)
+        return carry
+
+    lax.fori_loop(0, ROW_BLOCKS, flip, 0, unroll=2)
+    store = pltpu.make_async_copy(plain, data_image, sem.at[1])
+    store.start()
 
     def add(first, width):
         terms = []
         for u in range(width):
-            at = rows[0, step * CHUNK + first + u]
-            terms.append(dot(flipped[at], sens[0, first + u]))
+            terms.append(dot(flipped[rows[0, first + u]], held[first + u]))
         for u in range(width):
-            at = cols[0, step * CHUNK + first + u]
+            at = cols[0, first + u]
             adjoint[(at >> 2) & 1, at & 3, at >> 3] += terms[u]
 
-    live_slots(count, step, add)
+    sensors.run(add)
+    store.wait()
 
 
 def adjoin(count, rows, cols, sens, image):
+    held, sems = SENSOR_SCRATCH
     return pl.pallas_call(
         adjoint_kernel,
         out_shape=(
             jax.ShapeDtypeStruct((ROW_BLOCKS, BLK, BLK), F32),
             jax.ShapeDtypeStruct((2, NZ, PARTS, BLK, BLK), F32),
         ),
-        grid_spec=pltpu.PrefetchScalarGridSpec(
-            num_scalar_prefetch=3,
-            grid=(SLOTS // CHUNK,),
-            in_specs=[sens_spec(), whole(ROW_BLOCKS, BLK, BLK)],
-            out_specs=(whole(ROW_BLOCKS, BLK, BLK), whole(2, NZ, PARTS, BLK, BLK)),
-            scratch_shapes=[pltpu.VMEM((ROW_BLOCKS, BLK, BLK), BF16)],
-        ),
+        in_specs=[SMEM, SMEM, SMEM, ANY, ANY],
+        out_specs=(ANY, VMEM),
+        scratch_shapes=[
+            held,
+            pltpu.VMEM((ROW_BLOCKS, BLK, BLK), BF16),
+            pltpu.VMEM((ROW_BLOCKS, BLK, BLK), BF16),
+            pltpu.VMEM((ROW_BLOCKS, BLK, BLK), F32),
+            pltpu.SemaphoreType.DMA((2,)),
+            sems,
+        ],
         compiler_params=pltpu.CompilerParams(vmem_limit_bytes=VMEM_LIMIT),
         name="adjoin",
     )(count, rows, cols, sens, image)
@@ -696,7 +779,7 @@
     return pl.pallas_call(
         return_kernel,
         out_shape=jax.ShapeDtypeStruct((NZ, 2, PARTS, BLK, BLK), BF16),
-        in_specs=[pl.BlockSpec(memory_space=pl.ANY), vmem, vmem, vmem],
+        in_specs=[ANY, vmem, vmem, vmem],
         out_specs=vmem,
         scratch_shapes=[
             pltpu.VMEM((NZ, PARTS, BLK, BLK), F32),
@@ -714,6 +797,7 @@
         compiler_params=pltpu.CompilerParams(
             collective_id=2, has_side_effects=True, vmem_limit_bytes=VMEM_LIMIT
         ),
+        cost_estimate=cost(1 << 30, 80 << 20),
         name="give_back",
     )(
         partial,
@@ -723,36 +807,43 @@
     )
 
 
-TILES = 8
-
-
-def place_kernel(order, product, out, inverse):
-    step = pl.program_id(0)
-
-    @pl.when(step == 0)
-    def _():
-        def note(j, carry):
-            inverse[order[0, j]] = j
-            return carry
-
-        lax.fori_loop(0, COL_BLOCKS, note, 0)
-
-    for t in range(TILES):
-        j = inverse[step * TILES + t]
-        out[t * BLK : (t + 1) * BLK, :] = product[j & 3, (j >> 2) & 1, j >> 3].astype(F32)
+def place_kernel(order, product_hbm, out, product, cells, in_sems, out_sems):
+    def load(i):
+        at = lax.div(i, 2), lax.rem(i, 2)
+        return pltpu.make_async_copy(product_hbm.at[at], product.at[at], in_sems.at[i])
+
+    def store(i, block):
+        return pltpu.make_async_copy(cells.at[i], out.at[block], out_sems.at[i])
+
+    for i in range(2 * NZ):
+        load(i).start()
+    for i in range(2 * NZ):
+        load(i).wait()
+        for m in range(PARTS):
+            q, core = i // 2, i % 2
+            at = i * PARTS + m
+            cells[at] = product[q, core, m].astype(F32)
+            store(at, order[0, (m * 2 + core) * 4 + q]).start()
+
+    def finish(i, carry):
+        store(i, 0).wait()
+        return carry
+
+    lax.fori_loop(0, COL_BLOCKS, finish, 0)
 
 
 def place_cells(order, product):
     return pl.pallas_call(
         place_kernel,
-        out_shape=jax.ShapeDtypeStruct((CELLS, BLK), F32),
-        grid_spec=pltpu.PrefetchScalarGridSpec(
-            num_scalar_prefetch=1,
-            grid=(COL_BLOCKS // TILES,),
-            in_specs=[whole(NZ, 2, PARTS, BLK, BLK)],
-            out_specs=pl.BlockSpec((TILES * BLK, BLK), lambda i, order: (i, 0)),
-            scratch_shapes=[pltpu.SMEM((COL_BLOCKS,), jnp.int32)],
-        ),
+        out_shape=jax.ShapeDtypeStruct((COL_BLOCKS, BLK, BLK), F32),
+        in_specs=[SMEM, ANY],
+        out_specs=ANY,
+        scratch_shapes=[
+            pltpu.VMEM(product.shape, BF16),
+            pltpu.VMEM((COL_BLOCKS, BLK, BLK), F32),
+            pltpu.SemaphoreType.DMA((2 * NZ,)),
+            pltpu.SemaphoreType.DMA((COL_BLOCKS,)),
+        ],
         compiler_params=pltpu.CompilerParams(vmem_limit_bytes=VMEM_LIMIT),
         name="place_cells",
     )(order, product)
@@ -764,7 +855,7 @@
     image_half = combine(partial_image).reshape(ROW_BLOCKS, BLK, BLK)
     data_image, partial_adjoint = adjoin(blk_count, blk_row, blk_col, sens_blocks, image_half)
     normal_product = place_cells(send_order, give_back(partial_adjoint, smooth))
-    return data_image.reshape(ROW_BLOCKS * BLK, BLK), normal_product
+    return data_image.reshape(ROW_BLOCKS * BLK, BLK), normal_product.reshape(CELLS, BLK)
 
 
 def solution(mesh):

time: 135 us -> 123 us (0.911)
  Pallas kernels: 134 us -> 121 us
    pallas_call x1, Pallas kernels: 14.3 us -> 7.85 us  [adjoin(): pl.pallas_call(adjoint_kernel, out_shape=(jax.ShapeDtypeStruct((ROW_BLOCK...]
    pallas_call x1, Pallas kernels: 9.89 us -> 6.15 us  [forward(): pl.pallas_call(forward_kernel, out_shape=jax.ShapeDtypeStruct((ROW_BLOCKS...]
    pallas_call x1, Pallas kernels: 5.77 us -> 4.22 us  [place_cells(): pl.pallas_call(place_kernel, out_shape=jax.ShapeDtypeStruct((COL_BLOCKS,...]
where the time goes in v3:
time: 123 us
  Pallas kernels  121 us (98%)
  between operations  1.32 us (1%)
    pallas_call x1, Pallas kernels, give_back(): pl.pallas_call(return_kernel, out_shape=jax.ShapeDtypeStruct((NZ, 2, PART...  41.8 us
    pallas_call x1, Pallas kernels, combine(): pl.pallas_call(kernel, out_shape=jax.ShapeDtypeStruct((rows, BLK), BF16),...  31.9 us
    pallas_call x1, Pallas kernels, analyse(): pl.pallas_call(analyse_kernel, out_shape=(jax.ShapeDtypeStruct((NZ, 2, PA...  29.4 us
    pallas_call x1, Pallas kernels, adjoin(): pl.pallas_call(adjoint_kernel, out_shape=(jax.ShapeDtypeStruct((ROW_BLOCK...  7.85 us
    pallas_call x1, Pallas kernels, forward(): pl.pallas_call(forward_kernel, out_shape=jax.ShapeDtypeStruct((ROW_BLOCKS...  6.15 us
    pallas_call x1, Pallas kernels, place_cells(): pl.pallas_call(place_kernel, out_shape=jax.ShapeDtypeStruct((COL_BLOCKS,...  4.22 us

profile of v3, /device:TPU:1, one launch (start us, length us, event | category | flops | bytes accessed | tf_op | source)
XLA Modules:
  0.0 122.5 jit_solution(824230583023364708)
XLA Ops:
  1.3 29.4 %analyse.1 = (bf16[4,2,8,128,128]{4,3,2,1,0:T(8,128)(2,1)}, f32[8,128,128]{2,1,0:T(8,128)}) custom-call(s32[1,64]{1,0:T(1,128)} %order.3, f32[128,64,128]{2,1,0:T(8,128)} %bitcast.7, s32[4,8192]{1,0:T(4,128)} %neighbors_hbm.1, f32[4,8192]{1,0:T(4,128)} %weights_hbm.1, bf16[128,128]{1,0:T(8,128)(2,1)} %constant.8.clone.signs_hbm, ...), custom_call_target="tpu_custom_call" | custom-call | flops 1073741824 | bytes 62914560 | tf_op jit(solution)/shard_map/analyse/pallas_call | solution.py:340
  30.6 6.2 %forward.1 = f32[32,128,128]{2,1,0:T(8,128)} custom-call(s32[1,1]{1,0:T(1,128)S(6)} %copy.14.count, s32[1,384]{1,0:T(1,128)} %rows.3, s32[1,384]{1,0:T(1,128)} %cols.3, bf16[1,384,128,128]{3,2,1,0:T(8,128)(2,1)} %source.3, bf16[4,2,8,128,128]{4,3,2,1,0:T(8,128)(2,1)} %get-tuple-element.6.wavelet_hbm), custom_call_target="tpu_custom_call" | custom-call | tf_op jit(solution)/shard_map/forward/pallas_call | solution.py:443
  36.8 31.9 %combine.1 = bf16[4096,128]{1,0:T(8,128)(2,1)} custom-call(f32[4096,128]{1,0:T(8,128)} %bitcast.5), custom_call_target="tpu_custom_call" | custom-call | flops 1048576 | bytes 83886080 | tf_op jit(solution)/shard_map/combine/pallas_call | solution.py:624
  68.7 7.9 %adjoin.1 = (f32[32,128,128]{2,1,0:T(8,128)}, f32[2,4,8,128,128]{4,3,2,1,0:T(8,128)}) custom-call(s32[1,1]{1,0:T(1,128)S(6)} %copy.14.count, s32[1,384]{1,0:T(1,128)} %rows.3, s32[1,384]{1,0:T(1,128)} %cols.3, bf16[1,384,128,128]{3,2,1,0:T(8,128)(2,1)} %source.3, bf16[32,128,128]{2,1,0:T(8,128)(2,1)} %bitcast.6), custom_call_target="tpu_custom_call" | custom-call | tf_op jit(solution)/shard_map/adjoin/pallas_call | solution.py:680
  76.5 41.8 %give_back.1.product_hbm = bf16[4,2,8,128,128]{4,3,2,1,0:T(8,128)(2,1)} custom-call(f32[2,4,8,128,128]{4,3,2,1,0:T(8,128)} %get-tuple-element.8.partial, f32[8,128,128]{2,1,0:T(8,128)} %get-tuple-element.9.smooth, f32[8,128]{1,0:T(8,128)} %constant.10.clone.scale, bf16[128,128]{1,0:T(8,128)(2,1)} %constant.11.clone.signs), custom_call_target="tpu_custom_call" | custom-call | flops 1073741824 | bytes 83886080 | tf_op jit(solution)/shard_map/give_back/pallas_call | solution.py:779
  118.3 4.2 %place_cells.1 = f32[64,128,128]{2,1,0:T(8,128)} custom-call(s32[1,64]{1,0:T(1,128)} %order.3, bf16[4,2,8,128,128]{4,3,2,1,0:T(8,128)(2,1)} %give_back.1.product_hbm), custom_call_target="tpu_custom_call" | custom-call | tf_op jit(solution)/shard_map/place_cells/pallas_call | solution.py:836

commit v4 on v3

--- a/solution.py
+++ b/solution.py
@@ -96,6 +96,7 @@
 
 
 PARTS = NCOLS // 2
+GROUP = PARTS // 2
 
 
 class Exchange:
@@ -568,8 +569,9 @@
             self.ring.arrived(self.rows(4 - step), step - 1)
 
 
-HALF_ROWS = ROW_BLOCKS * BLK // 2
-BIG = HALF_ROWS // 4
+STREAMS = 4
+STREAM = ROW_BLOCKS * BLK // STREAMS
+BIG = STREAM // 4
 SMALL = BIG // 4
 
 
@@ -585,29 +587,46 @@
         me, devices = ((x, x_ring), (y, y_ring))[axis]
         return Ring(me, devices[1], devices[3], send.at[slot], recv.at[slot], devices[2])
 
-    def both(stages):
-        for stage in stages:
-            stage.begin()
-        for stage in stages:
-            stage.pass_on()
-        for stage in stages:
-            stage.finish()
-
-    bases = [0, HALF_ROWS]
-    inner = [x * BIG, HALF_ROWS + y * BIG]
-    rings = [ring(a, a) for a in range(2)]
-    wide = [Reduce(rings[a], partial, bases[a], BIG, big_relay.at[a], big_landed.at[a]) for a in range(2)]
-    both(wide)
-    cross = [ring(1 - a, 2 + a) for a in range(2)]
-    both([DirectReduce(cross[a], partial, inner[a], SMALL, small_landed.at[a]) for a in range(2)])
-    for a, other in ((0, y), (1, x)):
-        own = pl.ds(pl.multiple_of(inner[a] + other * SMALL, SMALL), SMALL)
+    streams = range(STREAMS)
+    axis = [a % 2 for a in streams]
+    bases = [a * STREAM for a in streams]
+    inner = [bases[a] + (x, y)[axis[a]] * BIG for a in streams]
+    wide_rings = [ring(axis[a], a) for a in streams]
+    cross_rings = [ring(1 - axis[a], STREAMS + a) for a in streams]
+    back_rings = [ring(1 - axis[a], 2 * STREAMS + a) for a in streams]
+    last_rings = [ring(axis[a], 3 * STREAMS + a) for a in streams]
+    wide = [Reduce(wide_rings[a], partial, bases[a], BIG, big_relay.at[a], big_landed.at[a]) for a in streams]
+    cross = [DirectReduce(cross_rings[a], partial, inner[a], SMALL, small_landed.at[a]) for a in streams]
+    back = [DirectGather(back_rings[a], image, inner[a], SMALL) for a in streams]
+    last = [DirectGather(last_rings[a], image, bases[a], BIG) for a in streams]
+
+    def cast(a):
+        start = inner[a] + (y, x)[axis[a]] * SMALL
+        own = pl.ds(pl.multiple_of(start, SMALL), SMALL)
         image[own, :] = partial[own, :].astype(BF16)
-    back = [ring(1 - a, 4 + a) for a in range(2)]
-    both([DirectGather(back[a], image, inner[a], SMALL) for a in range(2)])
-    last = [ring(a, 6 + a) for a in range(2)]
-    both([DirectGather(last[a], image, bases[a], BIG) for a in range(2)])
-    for group in (rings, cross, back, last):
+
+    pairs = [(a, a + 1) for a in range(0, STREAMS, 2)]
+    for a in streams:
+        wide[a].begin()
+    for a in streams:
+        wide[a].pass_on()
+    for pair in pairs:
+        for a in pair:
+            wide[a].finish()
+            cross[a].begin()
+    for pair in pairs:
+        for a in pair:
+            cross[a].pass_on()
+            cross[a].finish()
+            cast(a)
+            back[a].begin()
+    for pair in pairs:
+        for a in pair:
+            back[a].finish()
+            last[a].begin()
+    for a in streams:
+        last[a].finish()
+    for group in (wide_rings, cross_rings, back_rings, last_rings):
         for one in group:
             one.drain()
 
@@ -628,11 +647,11 @@
         out_specs=vmem,
         scratch_shapes=[
             pltpu.VMEM((rows, BLK), F32),
-            pltpu.VMEM((2, 2, BIG // 2, BLK), F32),
-            pltpu.VMEM((2, 2, BIG, BLK), F32),
-            pltpu.VMEM((2, 3, SMALL, BLK), F32),
-            pltpu.SemaphoreType.DMA((8, 6)),
-            pltpu.SemaphoreType.DMA((8, 6)),
+            pltpu.VMEM((STREAMS, 2, BIG // 2, BLK), F32),
+            pltpu.VMEM((STREAMS, 2, BIG, BLK), F32),
+            pltpu.VMEM((STREAMS, 3, SMALL, BLK), F32),
+            pltpu.SemaphoreType.DMA((4 * STREAMS, 6)),
+            pltpu.SemaphoreType.DMA((4 * STREAMS, 6)),
             pltpu.SemaphoreType.DMA,
         ],
         compiler_params=pltpu.CompilerParams(
@@ -662,6 +681,7 @@
     lax.fori_loop(0, ROW_BLOCKS, flip, 0, unroll=2)
     store = pltpu.make_async_copy(plain, data_image, sem.at[1])
     store.start()
+    shift = lax.axis_index("cols") >> 1
 
     def add(first, width):
         terms = []
@@ -669,7 +689,8 @@
             terms.append(dot(flipped[rows[0, first + u]], held[first + u]))
         for u in range(width):
             at = cols[0, first + u]
-            adjoint[(at >> 2) & 1, at & 3, at >> 3] += terms[u]
+            part = at >> 3
+            adjoint[(at >> 2) & 1, at & 3, (part + shift) & 1, part >> 1] += terms[u]
 
     sensors.run(add)
     store.wait()
@@ -681,7 +702,7 @@
         adjoint_kernel,
         out_shape=(
             jax.ShapeDtypeStruct((ROW_BLOCKS, BLK, BLK), F32),
-            jax.ShapeDtypeStruct((2, NZ, PARTS, BLK, BLK), F32),
+            jax.ShapeDtypeStruct((2, NZ, 2, GROUP, BLK, BLK), F32),
         ),
         in_specs=[SMEM, SMEM, SMEM, ANY, ANY],
         out_specs=(ANY, VMEM),
@@ -698,9 +719,6 @@
     )(count, rows, cols, sens, image)
 
 
-GROUP = PARTS // 2
-
-
 def return_kernel(
     partial, smooth, scale, signs, out, own, stage, pair, relay_out, relay, landed, gathered, sem, send, recv, *sem_refs
 ):
@@ -711,87 +729,108 @@
     exchange = Exchange(stage, out, sem_refs, where)
     plus, minus, partner = exchange.neighbour(1), exchange.neighbour(3), exchange.partner()
     greet([plus, minus, partner], (exchange.first, exchange.device))
-    ring = Ring(z, plus, minus, send, recv)
-    for slot, step in ((6, 2), (7, 1), (8, 3), (9, 0)):
-        ring.copy(partial.at[1 - core, ring.at(step)], pair.at[ring.at(step)], partner, slot)
+    rings = [Ring(z, plus, minus, send.at[p], recv.at[p]) for p in range(2)]
+    half = GROUP // 2
+    for p in range(2):
+        ring = rings[p]
+        for slot, step in ((6, 2), (7, 1), (8, 3), (9, 0)):
+            q = ring.at(step)
+            ring.copy(partial.at[1 - core, q, p], pair.at[q, p], partner, slot)
     fill.wait()
 
-    def total(step, h):
-        group = pl.ds(h * GROUP, GROUP)
-        return own[ring.at(step), group] + pair[ring.at(step), group]
-
-    def paired(step, slot):
-        ring.arrived(pair.at[ring.at(step)], slot)
-
-    def ship(value, slot, dst, device, sem):
-        relay_out[slot] = value.astype(BF16)
-        ring.copy(relay_out.at[slot], dst, device, sem)
-
-    paired(2, 6)
-    ship(total(2, 0), 0, relay.at[0], plus, 0)
-    ship(total(2, 1), 1, relay.at[1], minus, 1)
-    paired(1, 7)
-    ship(total(1, 1), 3, landed.at[0, 1], plus, 2)
-    paired(3, 8)
-    ship(total(3, 0), 4, landed.at[1, 0], minus, 3)
-    ring.arrived(relay.at[0], 0)
-    ship(total(1, 0) + relay[0].astype(F32), 2, landed.at[0, 0], plus, 4)
-    ring.arrived(relay.at[1], 1)
-    ship(total(3, 1) + relay[1].astype(F32), 5, landed.at[1, 1], minus, 5)
-    paired(0, 9)
-    ring.arrived(landed.at[0, 1], 2)
-    ring.arrived(landed.at[1, 0], 3)
-    ring.arrived(landed.at[0, 0], 4)
-    ring.arrived(landed.at[1, 1], 5)
-    lane_scale = scale[0:1, :].reshape(1, 1, BLK)
-    for h in range(2):
-        value = total(0, h) + landed[0, h].astype(F32) + landed[1, h].astype(F32)
-        stage[pl.ds(h * GROUP, GROUP)] = (value * lane_scale).astype(BF16)
-
-    @pl.when(exchange.first == 1)
-    def _():
-        gathered[lax.div(col, 2)] = stage[lax.div(col, 2)]
-
-    def spread(i, carry):
-        exchange.copy(i, gathered).start()
-        return carry
-
-    lax.fori_loop(exchange.first, PARTS, spread, 0)
-
-    def synthesise(m, carry):
-        exchange.wait_part(m, gathered)
-        cells = lax.dot_general(
-            signs[...], gathered[m], (((1,), (1,)), ((), ())), preferred_element_type=F32
-        )
-        out[z, core, m] = (cells + smooth[m]).astype(BF16)
-        return carry
+    def total(p, step, h):
+        group = pl.ds(h * half, half)
+        q = rings[p].at(step)
+        return own[q, p, group] + pair[q, p, group]
+
+    def paired(p, step, slot):
+        rings[p].arrived(pair.at[rings[p].at(step), p], slot)
+
+    def ship(p, value, slot, dst, device, sem):
+        relay_out[p, slot] = value.astype(BF16)
+        rings[p].copy(relay_out.at[p, slot], dst, device, sem)
 
     for p in range(2):
-        lax.fori_loop(p * GROUP, (p + 1) * GROUP, synthesise, 0)
+        paired(p, 2, 6)
+        ship(p, total(p, 2, 0), 0, relay.at[p, 0], plus, 0)
+        ship(p, total(p, 2, 1), 1, relay.at[p, 1], minus, 1)
+        paired(p, 1, 7)
+        ship(p, total(p, 1, 1), 3, landed.at[p, 0, 1], plus, 2)
+        paired(p, 3, 8)
+        ship(p, total(p, 3, 0), 4, landed.at[p, 1, 0], minus, 3)
+    for p in range(2):
+        ring = rings[p]
+        ring.arrived(relay.at[p, 0], 0)
+        ship(p, total(p, 1, 0) + relay[p, 0].astype(F32), 2, landed.at[p, 0, 0], plus, 4)
+        ring.arrived(relay.at[p, 1], 1)
+        ship(p, total(p, 3, 1) + relay[p, 1].astype(F32), 5, landed.at[p, 1, 1], minus, 5)
+    lane_scale = scale[0:1, :]
+    mine = lax.div(col, 2)
+
+    def member(p, i):
+        return i * 2 + lax.rem(mine + p, 2)
+
+    for p in range(2):
+        ring = rings[p]
+        paired(p, 0, 9)
+        for slot, ref in ((2, landed.at[p, 0, 1]), (3, landed.at[p, 1, 0]), (4, landed.at[p, 0, 0]), (5, landed.at[p, 1, 1])):
+            ring.arrived(ref, slot)
+        for i in range(GROUP):
+            h, j = i // half, i % half
+            value = own[z, p, i] + pair[z, p, i]
+            value = value + landed[p, 0, h, j].astype(F32) + landed[p, 1, h, j].astype(F32)
+            stage[member(p, i)] = (value * lane_scale).astype(BF16)
+
+        def spread(i, carry, p=p):
+            exchange.copy(2 * i + p, gathered).start()
+            return carry
+
+        if p == 0:
+
+            @pl.when(exchange.first == 1)
+            def _():
+                gathered[mine] = stage[mine]
+
+        lax.fori_loop(exchange.first if p == 0 else 0, GROUP, spread, 0)
+
+    for p in range(2):
+
+        def synthesise(i, carry, p=p):
+            m = member(p, i)
+            exchange.wait_part(m, gathered)
+            cells = lax.dot_general(
+                signs[...], gathered[m], (((1,), (1,)), ((), ())), preferred_element_type=F32
+            )
+            out[z, core, p * GROUP + i] = (cells + smooth[m]).astype(BF16)
+            return carry
+
+        lax.fori_loop(0, GROUP, synthesise, 0)
         exchange.begin(p)
     exchange.finish()
     exchange.drain_parts(gathered)
-    ring.drain()
+    for ring in rings:
+        ring.drain()
 
 
 def give_back(partial, smooth):
     vmem = pl.BlockSpec(memory_space=pltpu.VMEM)
+    half = GROUP // 2
     return pl.pallas_call(
         return_kernel,
         out_shape=jax.ShapeDtypeStruct((NZ, 2, PARTS, BLK, BLK), BF16),
         in_specs=[ANY, vmem, vmem, vmem],
         out_specs=vmem,
         scratch_shapes=[
-            pltpu.VMEM((NZ, PARTS, BLK, BLK), F32),
+            pltpu.VMEM((NZ, 2, GROUP, BLK, BLK), F32),
             pltpu.VMEM((PARTS, BLK, BLK), BF16),
-            pltpu.VMEM((NZ, PARTS, BLK, BLK), F32),
-            pltpu.VMEM((6, GROUP, BLK, BLK), BF16),
-            pltpu.VMEM((2, GROUP, BLK, BLK), BF16),
-            pltpu.VMEM((2, 2, GROUP, BLK, BLK), BF16),
+            pltpu.VMEM((NZ, 2, GROUP, BLK, BLK), F32),
+            pltpu.VMEM((2, 6, half, BLK, BLK), BF16),
+            pltpu.VMEM((2, 2, half, BLK, BLK), BF16),
+            pltpu.VMEM((2, 2, 2, half, BLK, BLK), BF16),
             pltpu.VMEM((PARTS, BLK, BLK), BF16),
             pltpu.SemaphoreType.DMA,
-            pltpu.SemaphoreType.DMA((10,)),
-            pltpu.SemaphoreType.DMA((10,)),
+            pltpu.SemaphoreType.DMA((2, 10)),
+            pltpu.SemaphoreType.DMA((2, 10)),
             *EXCHANGE_SEMS,
         ],
         compiler_params=pltpu.CompilerParams(
@@ -817,12 +856,14 @@
 
     for i in range(2 * NZ):
         load(i).start()
+    shift = lax.axis_index("cols") >> 1
     for i in range(2 * NZ):
         load(i).wait()
-        for m in range(PARTS):
-            q, core = i // 2, i % 2
-            at = i * PARTS + m
-            cells[at] = product[q, core, m].astype(F32)
+        for n in range(PARTS):
+            q, core, p = i // 2, i % 2, n // GROUP
+            at = i * PARTS + n
+            cells[at] = product[q, core, n].astype(F32)
+            m = (n % GROUP) * 2 + ((shift + p) & 1)
             store(at, order[0, (m * 2 + core) * 4 + q]).start()
 
     def finish(i, carry):

time: 123 us -> 118 us (0.959)
  Pallas kernels: 121 us -> 116 us
    pallas_call x1, Pallas kernels: 41.8 us -> 36.2 us  [give_back(): pl.pallas_call(return_kernel, out_shape=jax.ShapeDtypeStruct((NZ, 2, PART...]
where the time goes in v4:
time: 118 us; the launch traced here: 117 us
  Pallas kernels  116 us (98%)
  between operations  1.32 us (1%)
    pallas_call x1, Pallas kernels, give_back(): pl.pallas_call(return_kernel, out_shape=jax.ShapeDtypeStruct((NZ, 2, PART...  36.2 us
    pallas_call x1, Pallas kernels, combine(): pl.pallas_call(kernel, out_shape=jax.ShapeDtypeStruct((rows, BLK), BF16),...  32.6 us
    pallas_call x1, Pallas kernels, analyse(): pl.pallas_call(analyse_kernel, out_shape=(jax.ShapeDtypeStruct((NZ, 2, PA...  29.4 us
    pallas_call x1, Pallas kernels, adjoin(): pl.pallas_call(adjoint_kernel, out_shape=(jax.ShapeDtypeStruct((ROW_BLOCK...  7.66 us
    pallas_call x1, Pallas kernels, forward(): pl.pallas_call(forward_kernel, out_shape=jax.ShapeDtypeStruct((ROW_BLOCKS...  5.92 us
    pallas_call x1, Pallas kernels, place_cells(): pl.pallas_call(place_kernel, out_shape=jax.ShapeDtypeStruct((COL_BLOCKS,...  4.22 us

profile of v4, /device:TPU:1, one launch (start us, length us, event | category | flops | bytes accessed | tf_op | source)
XLA Modules:
  0.0 117.4 jit_solution(4766225447564613751)
XLA Ops:
  1.3 29.4 %analyse.1 = (bf16[4,2,8,128,128]{4,3,2,1,0:T(8,128)(2,1)}, f32[8,128,128]{2,1,0:T(8,128)}) custom-call(s32[1,64]{1,0:T(1,128)} %order.3, f32[128,64,128]{2,1,0:T(8,128)} %bitcast.7, s32[4,8192]{1,0:T(4,128)} %neighbors_hbm.1, f32[4,8192]{1,0:T(4,128)} %weights_hbm.1, bf16[128,128]{1,0:T(8,128)(2,1)} %constant.8.clone.signs_hbm, ...), custom_call_target="tpu_custom_call" | custom-call | flops 1073741824 | bytes 62914560 | tf_op jit(solution)/shard_map/analyse/pallas_call | solution.py:341
  30.6 5.9 %forward.1 = f32[32,128,128]{2,1,0:T(8,128)} custom-call(s32[1,1]{1,0:T(1,128)S(6)} %copy.14.count, s32[1,384]{1,0:T(1,128)} %rows.3, s32[1,384]{1,0:T(1,128)} %cols.3, bf16[1,384,128,128]{3,2,1,0:T(8,128)(2,1)} %source.3, bf16[4,2,8,128,128]{4,3,2,1,0:T(8,128)(2,1)} %get-tuple-element.6.wavelet_hbm), custom_call_target="tpu_custom_call" | custom-call | tf_op jit(solution)/shard_map/forward/pallas_call | solution.py:444
  36.6 32.6 %combine.1 = bf16[4096,128]{1,0:T(8,128)(2,1)} custom-call(f32[4096,128]{1,0:T(8,128)} %bitcast.5), custom_call_target="tpu_custom_call" | custom-call | flops 1048576 | bytes 83886080 | tf_op jit(solution)/shard_map/combine/pallas_call | solution.py:643
  69.2 7.7 %adjoin.1 = (f32[32,128,128]{2,1,0:T(8,128)}, f32[2,4,2,4,128,128]{5,4,3,2,1,0:T(8,128)}) custom-call(s32[1,1]{1,0:T(1,128)S(6)} %copy.14.count, s32[1,384]{1,0:T(1,128)} %rows.3, s32[1,384]{1,0:T(1,128)} %cols.3, bf16[1,384,128,128]{3,2,1,0:T(8,128)(2,1)} %source.3, bf16[32,128,128]{2,1,0:T(8,128)(2,1)} %bitcast.6), custom_call_target="tpu_custom_call" | custom-call | tf_op jit(solution)/shard_map/adjoin/pallas_call | solution.py:701
  76.9 36.2 %give_back.1.product_hbm = bf16[4,2,8,128,128]{4,3,2,1,0:T(8,128)(2,1)} custom-call(f32[2,4,2,4,128,128]{5,4,3,2,1,0:T(8,128)} %get-tuple-element.8.partial, f32[8,128,128]{2,1,0:T(8,128)} %get-tuple-element.9.smooth, f32[8,128]{1,0:T(8,128)} %constant.10.clone.scale, bf16[128,128]{1,0:T(8,128)(2,1)} %constant.11.clone.signs), custom_call_target="tpu_custom_call" | custom-call | flops 1073741824 | bytes 83886080 | tf_op jit(solution)/shard_map/give_back/pallas_call | solution.py:818
  113.1 4.2 %place_cells.1 = f32[64,128,128]{2,1,0:T(8,128)} custom-call(s32[1,64]{1,0:T(1,128)} %order.3, bf16[4,2,8,128,128]{4,3,2,1,0:T(8,128)(2,1)} %give_back.1.product_hbm), custom_call_target="tpu_custom_call" | custom-call | tf_op jit(solution)/shard_map/place_cells/pallas_call | solution.py:877

commit v5 on v4

--- a/solution.py
+++ b/solution.py
@@ -92,58 +92,26 @@
 
         lax.fori_loop(first, PARTS, signal, 0)
         count = count + PARTS - first
-    pl.semaphore_wait(barrier, count)
+
+    def wait_for_all():
+        pl.semaphore_wait(barrier, count)
+
+    return wait_for_all
 
 
 PARTS = NCOLS // 2
 GROUP = PARTS // 2
 
 
-class Exchange:
-    def __init__(self, stage, out, sem_refs, where):
-        self.stage, self.out = stage, out
-        self.a_send, self.a_recv, self.g_send, self.minus, self.plus, self.far, self.pair = sem_refs
+class RowGather:
+    def __init__(self, piece, sem_refs, where):
+        self.piece_of = piece
+        self.g_send, self.minus, self.plus, self.far, self.pair = sem_refs
         self.row, self.col, self.z, self.core = where
-        self.first = jnp.where(self.core == lax.rem(self.col, 2), 1, 0)
         self.sends = []
 
-    def slot(self, i):
-        return lax.rem(lax.div(self.col, 2) + i, PARTS)
-
-    def device(self, i):
-        return self.z * 2 + lax.rem(self.col, 2), self.slot(i) * 2 + self.core
-
-    def arrivals(self, landing):
-        return landing.at[lax.div(self.col, 2)]
-
-    def copy(self, i, landing):
-        return remote(
-            self.stage.at[self.slot(i)],
-            self.arrivals(landing),
-            self.a_send.at[i],
-            self.a_recv.at[lax.div(self.col, 2)],
-            self.device(i),
-        )
-
-    def wait_part(self, m, landing):
-        @pl.when(m * 2 + self.core != self.col)
-        def _():
-            ref = landing.at[m]
-            remote(
-                ref, ref, self.a_send.at[0], self.a_recv.at[m], self.device(1)
-            ).wait_recv()
-
-    def drain_parts(self, landing):
-        def finish(i, carry):
-            self.copy(i, landing).wait_send()
-            return carry
-
-        lax.fori_loop(self.first, PARTS, finish, 0)
-
     def piece(self, step, p, core=None):
-        core = self.core if core is None else core
-        size = PARTS // 2
-        return self.out.at[lax.rem(self.z + step, NZ), core, pl.ds(p * size, size)]
+        return self.piece_of(lax.rem(self.z + step, NZ), self.core if core is None else core, p)
 
     def send(self, step, p, device, recv_sem):
         piece = self.piece(step, p)
@@ -166,7 +134,7 @@
         self.send(0, p, self.neighbour(3), self.plus.at[p])
         self.send(0, p, self.partner(), self.pair.at[0, p])
 
-    def finish(self):
+    def pass_on(self):
         self.arrived(3, 0, self.minus.at[0])
         self.send(3, 0, self.neighbour(1), self.far.at[0])
         self.send(3, 0, self.partner(), self.pair.at[3, 0])
@@ -177,6 +145,8 @@
         self.send(1, 0, self.partner(), self.pair.at[1, 0])
         self.arrived(3, 1, self.minus.at[1])
         self.send(3, 1, self.partner(), self.pair.at[3, 1])
+
+    def finish(self):
         for p in range(2):
             self.arrived(2, p, self.far.at[p])
             self.send(2, p, self.partner(), self.pair.at[2, p])
@@ -187,15 +157,34 @@
             copy.wait_send()
 
 
-EXCHANGE_SEMS = [
-    pltpu.SemaphoreType.DMA((PARTS,)),
-    pltpu.SemaphoreType.DMA((PARTS,)),
+GATHER_SEMS = [
     pltpu.SemaphoreType.DMA((14,)),
     pltpu.SemaphoreType.DMA((2,)),
     pltpu.SemaphoreType.DMA((2,)),
     pltpu.SemaphoreType.DMA((2,)),
     pltpu.SemaphoreType.DMA((4, 2)),
 ]
+
+
+class Parts:
+    def __init__(self, where):
+        self.row, self.col, self.z, self.core = where
+        self.mine = lax.div(self.col, 2)
+        self.first = jnp.where(self.core == lax.rem(self.col, 2), 1, 0)
+
+    def slot(self, i):
+        return lax.rem(self.mine + i, PARTS)
+
+    def device_at(self, m):
+        return self.z * 2 + lax.rem(self.col, 2), m * 2 + self.core
+
+    def device(self, i):
+        return self.device_at(self.slot(i))
+
+    def own(self, m):
+        return m * 2 + self.core == self.col
+
+
 CELLS = COL_BLOCKS * BLK
 
 
@@ -231,6 +220,17 @@
     return total * center - mixed
 
 
+RING_BLOCKS = COL_BLOCKS // 2
+
+
+def ring_place(z, core, part):
+    return (z * 2 + core) * GROUP + part
+
+
+def plane_place(core, part):
+    return RING_BLOCKS + (core * PARTS + part) * 2
+
+
 def analyse_kernel(
     order,
     model,
@@ -247,9 +247,15 @@
     scale,
     rims,
     tables,
-    stage,
+    ring_stage,
+    plane_stage,
     sems,
-    *sem_refs,
+    ring_send,
+    ring_recv,
+    plane_send,
+    plane_recv,
+    plane_pair,
+    *gather_sems,
 ):
     where = place()
     row, col, z, core = where
@@ -267,11 +273,17 @@
     ]
     for fill in fills:
         fill.start()
-    exchange = Exchange(stage, wavelet, sem_refs, where)
+    parts = Parts(where)
+    mine, lane = parts.mine, lax.div(z, 2)
+
+    def ring_piece(at, k, p):
+        return wavelet.at[pl.ds(ring_place(at, k, p * 2), 2)]
+
+    gather = RowGather(ring_piece, gather_sems, where)
     below, above = (row, lax.rem(col + NCOLS - 1, NCOLS)), (row, lax.rem(col + 1, NCOLS))
-    greet(
-        [exchange.neighbour(1), exchange.neighbour(3), exchange.partner(), below, above],
-        (exchange.first, exchange.device),
+    wait_for_all = greet(
+        [gather.neighbour(1), gather.neighbour(3), gather.partner(), below, above],
+        (parts.first, parts.device),
     )
     up = remote(
         model.at[2 * COL_BLOCKS - 1],
@@ -287,52 +299,132 @@
         sems.at[3],
         below,
     )
-    up.start()
-    down.start()
     for fill in fills:
         fill.wait()
     sign_pair = jnp.concatenate([signs[...], signs[...]], axis=1)
-    landing = wavelet.at[z, core]
-    target = wavelet.at[z, lax.rem(col, 2)]
-
-    def block_of(m):
-        return order[0, (m * 2 + core) * 4 + z]
-
-    def coefficients(m):
-        high, low = split(cells_of(body, block_of(m)))
+
+    def block_of(m, q):
+        return order[0, (m * 2 + core) * 4 + q]
+
+    def coefficients(m, q):
+        high, low = split(cells_of(body, block_of(m, q)))
         product = dot(sign_pair, jnp.concatenate([high, low], axis=0))
         return (product * scale[...]).astype(BF16)
 
-    @pl.when(exchange.first == 1)
+    def ring_part(i):
+        return i * 2 + lax.rem(lane + mine, 2)
+
+    def make_ring(i, carry):
+        ring_stage[i] = coefficients(ring_part(i), 2 + lax.rem(z, 2))
+        return carry
+
+    lax.fori_loop(0, GROUP, make_ring, 0)
+    wait_for_all()
+
+    def ring_copy(i):
+        return remote(
+            ring_stage.at[i],
+            wavelet.at[ring_place(z, lax.rem(col, 2), lax.div(mine, 2))],
+            ring_send.at[i],
+            ring_recv.at[lax.div(mine, 2)],
+            parts.device_at(ring_part(i)),
+        )
+
+    def spread_ring(i, carry):
+        @pl.when(parts.own(ring_part(i)))
+        def _():
+            wavelet[ring_place(z, core, lax.div(mine, 2))] = ring_stage[i]
+
+        @pl.when(jnp.logical_not(parts.own(ring_part(i))))
+        def _():
+            ring_copy(i).start()
+
+        return carry
+
+    lax.fori_loop(0, GROUP, spread_ring, 0)
+    up.start()
+    down.start()
+
+    def plane_copy(i):
+        return remote(
+            plane_stage.at[i],
+            wavelet.at[pl.ds(plane_place(lax.rem(col, 2), mine), 2)],
+            plane_send.at[i],
+            plane_recv.at[mine],
+            parts.device(i),
+        )
+
+    def spread_plane(i, carry):
+        for q in range(2):
+            plane_stage[i, q] = coefficients(parts.slot(i), q)
+        plane_copy(i).start()
+        return carry
+
+    lax.fori_loop(parts.first, PARTS, spread_plane, 0)
+
+    @pl.when(parts.first == 1)
     def _():
-        wavelet[z, core, lax.div(col, 2)] = coefficients(lax.div(col, 2))
-
-    def spread(i, carry):
-        stage[exchange.slot(i)] = coefficients(exchange.slot(i))
-        exchange.copy(i, target).start()
-        return carry
-
-    lax.fori_loop(exchange.first, PARTS, spread, 0)
+        for q in range(2):
+            wavelet[plane_place(core, mine) + q] = coefficients(mine, q)
+
+    def wait_ring(i, carry):
+        @pl.when(jnp.logical_not(parts.own(ring_part(i))))
+        def _():
+            ref = wavelet.at[ring_place(z, core, i)]
+            remote(ref, ref, ring_send.at[0], ring_recv.at[i], gather.partner()).wait_recv()
+
+        return carry
+
+    def wait_plane(m, carry):
+        @pl.when(jnp.logical_not(parts.own(m)))
+        def _():
+            ref = wavelet.at[pl.ds(plane_place(core, m), 2)]
+            remote(ref, ref, plane_send.at[0], plane_recv.at[m], gather.partner()).wait_recv()
+
+        return carry
+
+    def half_plane(core_of, h):
+        return wavelet.at[pl.ds(plane_place(core_of, h * GROUP), PARTS)]
+
+    def swap(h):
+        ref = half_plane(core, h)
+        return remote(ref, ref, plane_pair.at[h], plane_pair.at[2 + h], gather.partner())
+
+    def smooth_one(m, carry):
+        smooth[m] = smooth_tile(body, rims, tables, block_of(m, z))
+        return carry
+
+    for p in range(2):
+        lax.fori_loop(2 * p, 2 * p + 2, wait_ring, 0)
+        gather.begin(p)
     tabulate(neighbors, weights, tables, col * CELLS)
-
-    def smooth_one(m, carry):
-        smooth[m] = smooth_tile(body, rims, tables, block_of(m))
-        return carry
-
     up.wait_recv()
     down.wait_recv()
-    lax.fori_loop(0, 3, smooth_one, 0)
-
-    def wait_part(m, carry):
-        exchange.wait_part(m, landing)
-        return carry
-
-    for p in range(2):
-        lax.fori_loop(p * PARTS // 2, (p + 1) * PARTS // 2, wait_part, 0)
-        exchange.begin(p)
-    lax.fori_loop(3, PARTS, smooth_one, 0)
-    exchange.finish()
-    exchange.drain_parts(target)
+    lax.fori_loop(0, 2, smooth_one, 0)
+    gather.pass_on()
+    lax.fori_loop(2, PARTS, smooth_one, 0)
+    for h in range(2):
+        lax.fori_loop(h * GROUP, (h + 1) * GROUP, wait_plane, 0)
+        swap(h).start()
+    gather.finish()
+    for h in range(2):
+        ref = half_plane(1 - core, h)
+        remote(ref, ref, plane_pair.at[h], plane_pair.at[2 + h], gather.partner()).wait_recv()
+        swap(h).wait_send()
+
+    def drain_ring(i, carry):
+        @pl.when(jnp.logical_not(parts.own(ring_part(i))))
+        def _():
+            ring_copy(i).wait_send()
+
+        return carry
+
+    def drain_plane(i, carry):
+        plane_copy(i).wait_send()
+        return carry
+
+    lax.fori_loop(0, GROUP, drain_ring, 0)
+    lax.fori_loop(parts.first, PARTS, drain_plane, 0)
     up.wait_send()
     down.wait_send()
 
@@ -341,7 +433,7 @@
     return pl.pallas_call(
         analyse_kernel,
         out_shape=(
-            jax.ShapeDtypeStruct((NZ, 2, PARTS, BLK, BLK), BF16),
+            jax.ShapeDtypeStruct((COL_BLOCKS, BLK, BLK), BF16),
             jax.ShapeDtypeStruct((PARTS, BLK, BLK), F32),
         ),
         in_specs=[SMEM, *[ANY] * 5],
@@ -354,9 +446,15 @@
             pltpu.VMEM((BLK, BLK), F32),
             pltpu.VMEM((2, RIM, BLK), F32),
             pltpu.VMEM((COL_BLOCKS, 8, BLK), F32),
-            pltpu.VMEM((PARTS, BLK, BLK), BF16),
+            pltpu.VMEM((GROUP, BLK, BLK), BF16),
+            pltpu.VMEM((PARTS, 2, BLK, BLK), BF16),
             pltpu.SemaphoreType.DMA((9,)),
-            *EXCHANGE_SEMS,
+            pltpu.SemaphoreType.DMA((GROUP,)),
+            pltpu.SemaphoreType.DMA((GROUP,)),
+            pltpu.SemaphoreType.DMA((PARTS,)),
+            pltpu.SemaphoreType.DMA((PARTS,)),
+            pltpu.SemaphoreType.DMA((4,)),
+            *GATHER_SEMS,
         ],
         compiler_params=pltpu.CompilerParams(
             collective_id=0, has_side_effects=True, vmem_limit_bytes=VMEM_LIMIT
@@ -414,19 +512,27 @@
             done = done + groups * width
 
 
-def forward_kernel(count, rows, cols, source, wavelet_hbm, image, held, wavelet, sem, sems):
+def forward_kernel(count, rows, cols, source, wavelet_hbm, image, held, wavelet, places, sem, sems):
     load = pltpu.make_async_copy(wavelet_hbm, wavelet, sem)
     load.start()
     sensors = Sensors(count, source, held, sems)
     sensors.start()
     image[...] = jnp.zeros_like(image)
+    mine = lax.axis_index("cols") >> 1
+
+    def note(at, carry):
+        q, core, part = at & 3, (at >> 2) & 1, at >> 3
+        by_ring = ring_place(2 * ((part + mine) & 1) + (q & 1), core, part >> 1)
+        places[at] = jnp.where(q >= 2, by_ring, plane_place(core, part) + q)
+        return carry
+
+    lax.fori_loop(0, COL_BLOCKS, note, 0)
     load.wait()
 
     def add(first, width):
         terms = []
         for u in range(width):
-            at = cols[0, first + u]
-            terms.append(dot(held[first + u], wavelet[at & 3, (at >> 2) & 1, at >> 3]))
+            terms.append(dot(held[first + u], wavelet[places[cols[0, first + u]]]))
         for u in range(width):
             image[rows[0, first + u]] += terms[u]
 
@@ -449,6 +555,7 @@
         scratch_shapes=[
             held,
             pltpu.VMEM(wavelet.shape, BF16),
+            pltpu.SMEM((COL_BLOCKS,), jnp.int32),
             pltpu.SemaphoreType.DMA,
             sems,
         ],
@@ -580,7 +687,7 @@
     y, x = lax.div(col, 4), lax.rem(col, 4)
     x_ring = [(row, y * 4 + lax.rem(x + step, 4)) for step in range(4)]
     y_ring = [(row, lax.rem(y + step, 4) * 4 + x) for step in range(4)]
-    greet(x_ring[1:] + y_ring[1:])
+    greet(x_ring[1:] + y_ring[1:])()
     fill.wait()
 
     def ring(axis, slot):
@@ -720,15 +827,21 @@
 
 
 def return_kernel(
-    partial, smooth, scale, signs, out, own, stage, pair, relay_out, relay, landed, gathered, sem, send, recv, *sem_refs
+    partial, smooth, scale, signs, out, own, stage, pair, relay_out, relay, landed, gathered, sem, send, recv, part_send, part_recv, *sem_refs
 ):
     where = place()
     row, col, z, core = where
     fill = pltpu.make_async_copy(partial.at[core], own, sem)
     fill.start()
-    exchange = Exchange(stage, out, sem_refs, where)
-    plus, minus, partner = exchange.neighbour(1), exchange.neighbour(3), exchange.partner()
-    greet([plus, minus, partner], (exchange.first, exchange.device))
+    parts = Parts(where)
+    mine = parts.mine
+
+    def out_piece(at, k, p):
+        return out.at[at, k, pl.ds(p * GROUP, GROUP)]
+
+    gather = RowGather(out_piece, sem_refs, where)
+    plus, minus, partner = gather.neighbour(1), gather.neighbour(3), gather.partner()
+    greet([plus, minus, partner], (parts.first, parts.device))()
     rings = [Ring(z, plus, minus, send.at[p], recv.at[p]) for p in range(2)]
     half = GROUP // 2
     for p in range(2):
@@ -765,7 +878,15 @@
         ring.arrived(relay.at[p, 1], 1)
         ship(p, total(p, 3, 1) + relay[p, 1].astype(F32), 5, landed.at[p, 1, 1], minus, 5)
     lane_scale = scale[0:1, :]
-    mine = lax.div(col, 2)
+
+    def part_copy(i):
+        return remote(
+            stage.at[parts.slot(i)],
+            gathered.at[mine],
+            part_send.at[i],
+            part_recv.at[mine],
+            parts.device(i),
+        )
 
     def member(p, i):
         return i * 2 + lax.rem(mine + p, 2)
@@ -782,22 +903,27 @@
             stage[member(p, i)] = (value * lane_scale).astype(BF16)
 
         def spread(i, carry, p=p):
-            exchange.copy(2 * i + p, gathered).start()
+            part_copy(2 * i + p).start()
             return carry
 
         if p == 0:
 
-            @pl.when(exchange.first == 1)
+            @pl.when(parts.first == 1)
             def _():
                 gathered[mine] = stage[mine]
 
-        lax.fori_loop(exchange.first if p == 0 else 0, GROUP, spread, 0)
+        lax.fori_loop(parts.first if p == 0 else 0, GROUP, spread, 0)
 
     for p in range(2):
 
         def synthesise(i, carry, p=p):
             m = member(p, i)
-            exchange.wait_part(m, gathered)
+
+            @pl.when(jnp.logical_not(parts.own(m)))
+            def _():
+                ref = gathered.at[m]
+                remote(ref, ref, part_send.at[0], part_recv.at[m], partner).wait_recv()
+
             cells = lax.dot_general(
                 signs[...], gathered[m], (((1,), (1,)), ((), ())), preferred_element_type=F32
             )
@@ -805,9 +931,15 @@
             return carry
 
         lax.fori_loop(0, GROUP, synthesise, 0)
-        exchange.begin(p)
-    exchange.finish()
-    exchange.drain_parts(gathered)
+        gather.begin(p)
+    gather.pass_on()
+    gather.finish()
+
+    def drain(i, carry):
+        part_copy(i).wait_send()
+        return carry
+
+    lax.fori_loop(parts.first, PARTS, drain, 0)
     for ring in rings:
         ring.drain()
 
@@ -831,7 +963,9 @@
             pltpu.SemaphoreType.DMA,
             pltpu.SemaphoreType.DMA((2, 10)),
             pltpu.SemaphoreType.DMA((2, 10)),
-            *EXCHANGE_SEMS,
+            pltpu.SemaphoreType.DMA((PARTS,)),
+            pltpu.SemaphoreType.DMA((PARTS,)),
+            *GATHER_SEMS,
         ],
         compiler_params=pltpu.CompilerParams(
             collective_id=2, has_side_effects=True, vmem_limit_bytes=VMEM_LIMIT

time: 118 us -> 116 us (0.983)
    pallas_call x1, Pallas kernels: 29.4 us -> 27.1 us  [analyse(): pl.pallas_call(analyse_kernel, out_shape=(jax.ShapeDtypeStruct((COL_BLOCK...]
    pallas_call x1, Pallas kernels: 36.2 us -> 38.3 us  [give_back(): pl.pallas_call(return_kernel, out_shape=jax.ShapeDtypeStruct((NZ, 2, PART...]
    pallas_call x1, Pallas kernels: 32.6 us -> 31.3 us  [combine(): pl.pallas_call(kernel, out_shape=jax.ShapeDtypeStruct((rows, BLK), BF16),...]
where the time goes in v5:
time: 116 us
  Pallas kernels  115 us (99%)
  between operations  1.32 us (1%)
    pallas_call x1, Pallas kernels, give_back(): pl.pallas_call(return_kernel, out_shape=jax.ShapeDtypeStruct((NZ, 2, PART...  38.3 us
    pallas_call x1, Pallas kernels, combine(): pl.pallas_call(kernel, out_shape=jax.ShapeDtypeStruct((rows, BLK), BF16),...  31.3 us
    pallas_call x1, Pallas kernels, analyse(): pl.pallas_call(analyse_kernel, out_shape=(jax.ShapeDtypeStruct((COL_BLOCK...  27.1 us
    pallas_call x1, Pallas kernels, adjoin(): pl.pallas_call(adjoint_kernel, out_shape=(jax.ShapeDtypeStruct((ROW_BLOCK...  7.77 us
    pallas_call x1, Pallas kernels, forward(): pl.pallas_call(forward_kernel, out_shape=jax.ShapeDtypeStruct((ROW_BLOCKS...  6.06 us
    pallas_call x1, Pallas kernels, place_cells(): pl.pallas_call(place_kernel, out_shape=jax.ShapeDtypeStruct((COL_BLOCKS,...  4.22 us

profile of v5, /device:TPU:1, one launch (start us, length us, event | category | flops | bytes accessed | tf_op | source)
XLA Modules:
  0.0 116.0 jit_solution(4732161811615494122)
XLA Ops:
  1.3 27.1 %analyse.1 = (bf16[64,128,128]{2,1,0:T(8,128)(2,1)}, f32[8,128,128]{2,1,0:T(8,128)}) custom-call(s32[1,64]{1,0:T(1,128)} %order.3, f32[128,64,128]{2,1,0:T(8,128)} %bitcast.7, s32[4,8192]{1,0:T(4,128)} %neighbors_hbm.1, f32[4,8192]{1,0:T(4,128)} %weights_hbm.1, bf16[128,128]{1,0:T(8,128)(2,1)} %constant.8.clone.signs_hbm, f32[128,128]{1,0:T(8,128)} %constant.9.clone.scale_hbm), custom_call_target="tpu_custom_call" | custom-call | flops 1073741824 | bytes 62914560 | tf_op jit(solution)/shard_map/analyse/pallas_call | solution.py:433
  28.4 6.1 %forward.1 = f32[32,128,128]{2,1,0:T(8,128)} custom-call(s32[1,1]{1,0:T(1,128)S(6)} %copy.14.count, s32[1,384]{1,0:T(1,128)} %rows.3, s32[1,384]{1,0:T(1,128)} %cols.3, bf16[1,384,128,128]{3,2,1,0:T(8,128)(2,1)} %source.3, bf16[64,128,128]{2,1,0:T(8,128)(2,1)} %get-tuple-element.6.wavelet_hbm), custom_call_target="tpu_custom_call" | custom-call | tf_op jit(solution)/shard_map/forward/pallas_call | solution.py:550
  34.5 31.3 %combine.1 = bf16[4096,128]{1,0:T(8,128)(2,1)} custom-call(f32[4096,128]{1,0:T(8,128)} %bitcast.5), custom_call_target="tpu_custom_call" | custom-call | flops 1048576 | bytes 83886080 | tf_op jit(solution)/shard_map/combine/pallas_call | solution.py:750
  65.7 7.8 %adjoin.1 = (f32[32,128,128]{2,1,0:T(8,128)}, f32[2,4,2,4,128,128]{5,4,3,2,1,0:T(8,128)}) custom-call(s32[1,1]{1,0:T(1,128)S(6)} %copy.14.count, s32[1,384]{1,0:T(1,128)} %rows.3, s32[1,384]{1,0:T(1,128)} %cols.3, bf16[1,384,128,128]{3,2,1,0:T(8,128)(2,1)} %source.3, bf16[32,128,128]{2,1,0:T(8,128)(2,1)} %bitcast.6), custom_call_target="tpu_custom_call" | custom-call | tf_op jit(solution)/shard_map/adjoin/pallas_call | solution.py:808
  73.5 38.3 %give_back.1.product_hbm = bf16[4,2,8,128,128]{4,3,2,1,0:T(8,128)(2,1)} custom-call(f32[2,4,2,4,128,128]{5,4,3,2,1,0:T(8,128)} %get-tuple-element.8.partial, f32[8,128,128]{2,1,0:T(8,128)} %get-tuple-element.9.smooth, f32[8,128]{1,0:T(8,128)} %constant.10.clone.scale, bf16[128,128]{1,0:T(8,128)(2,1)} %constant.11.clone.signs), custom_call_target="tpu_custom_call" | custom-call | flops 1073741824 | bytes 83886080 | tf_op jit(solution)/shard_map/give_back/pallas_call | solution.py:950
  111.8 4.2 %place_cells.1 = f32[64,128,128]{2,1,0:T(8,128)} custom-call(s32[1,64]{1,0:T(1,128)} %order.3, bf16[4,2,8,128,128]{4,3,2,1,0:T(8,128)(2,1)} %give_back.1.product_hbm), custom_call_target="tpu_custom_call" | custom-call | tf_op jit(solution)/shard_map/place_cells/pallas_call | solution.py:1011

commit v6 on v5

--- a/solution.py
+++ b/solution.py
@@ -101,27 +101,29 @@
 
 PARTS = NCOLS // 2
 GROUP = PARTS // 2
+LANES = 4
+EACH = PARTS // LANES
 
 
 class RowGather:
     def __init__(self, piece, sem_refs, where):
-        self.piece_of = piece
+        self.piece = piece
         self.g_send, self.minus, self.plus, self.far, self.pair = sem_refs
         self.row, self.col, self.z, self.core = where
         self.sends = []
 
-    def piece(self, step, p, core=None):
-        return self.piece_of(lax.rem(self.z + step, NZ), self.core if core is None else core, p)
-
-    def send(self, step, p, device, recv_sem):
-        piece = self.piece(step, p)
-        copy = remote(piece, piece, self.g_send.at[len(self.sends)], recv_sem, device)
+    def ref(self, step, p, h=None, core=None):
+        return self.piece(
+            lax.rem(self.z + step, NZ), self.core if core is None else core, p, h
+        )
+
+    def send(self, ref, device, recv_sem):
+        copy = remote(ref, ref, self.g_send.at[len(self.sends)], recv_sem, device)
         copy.start()
         self.sends.append(copy)
 
-    def arrived(self, step, p, recv_sem, core=None):
-        piece = self.piece(step, p, core)
-        remote(piece, piece, self.g_send.at[0], recv_sem, self.partner()).wait_recv()
+    def arrived(self, ref, recv_sem):
+        remote(ref, ref, self.g_send.at[0], recv_sem, self.partner()).wait_recv()
 
     def partner(self):
         return self.z * 2 + 1 - self.core, self.col
@@ -130,40 +132,44 @@
         return z_device(self.z, step, self.core, self.col)
 
     def begin(self, p):
-        self.send(0, p, self.neighbour(1), self.minus.at[p])
-        self.send(0, p, self.neighbour(3), self.plus.at[p])
-        self.send(0, p, self.partner(), self.pair.at[0, p])
-
-    def pass_on(self):
-        self.arrived(3, 0, self.minus.at[0])
-        self.send(3, 0, self.neighbour(1), self.far.at[0])
-        self.send(3, 0, self.partner(), self.pair.at[3, 0])
-        self.arrived(1, 1, self.plus.at[1])
-        self.send(1, 1, self.neighbour(3), self.far.at[1])
-        self.send(1, 1, self.partner(), self.pair.at[1, 1])
-        self.arrived(1, 0, self.plus.at[0])
-        self.send(1, 0, self.partner(), self.pair.at[1, 0])
-        self.arrived(3, 1, self.minus.at[1])
-        self.send(3, 1, self.partner(), self.pair.at[3, 1])
-
-    def finish(self):
-        for p in range(2):
-            self.arrived(2, p, self.far.at[p])
-            self.send(2, p, self.partner(), self.pair.at[2, p])
-        for p in range(2):
-            for step in (0, 1, 3, 2):
-                self.arrived(step, p, self.pair.at[step, p], 1 - self.core)
+        own = self.ref(0, p)
+        self.send(own, self.neighbour(1), self.minus.at[p])
+        self.send(own, self.neighbour(3), self.plus.at[p])
+        self.send(own, self.partner(), self.pair.at[0, p])
+
+    def pass_on(self, p):
+        self.arrived(self.ref(3, p), self.minus.at[p])
+        self.send(self.ref(3, p, 0), self.neighbour(1), self.far.at[0, p])
+        self.arrived(self.ref(1, p), self.plus.at[p])
+        self.send(self.ref(1, p, 1), self.neighbour(3), self.far.at[1, p])
+        self.send(self.ref(3, p), self.partner(), self.pair.at[3, p])
+        self.send(self.ref(1, p), self.partner(), self.pair.at[1, p])
+
+    def finish(self, p):
+        for h in range(2):
+            half = self.ref(2, p, h)
+            self.arrived(half, self.far.at[h, p])
+            self.send(half, self.partner(), self.pair.at[2 + 2 * h, p])
+
+    def close(self, pieces):
+        other = 1 - self.core
+        for p in range(pieces):
+            for step in (0, 1, 3):
+                self.arrived(self.ref(step, p, None, other), self.pair.at[step, p])
+            for h in range(2):
+                self.arrived(self.ref(2, p, h, other), self.pair.at[2 + 2 * h, p])
         for copy in self.sends:
             copy.wait_send()
 
 
-GATHER_SEMS = [
-    pltpu.SemaphoreType.DMA((14,)),
-    pltpu.SemaphoreType.DMA((2,)),
-    pltpu.SemaphoreType.DMA((2,)),
-    pltpu.SemaphoreType.DMA((2,)),
-    pltpu.SemaphoreType.DMA((4, 2)),
-]
+def gather_sems(pieces):
+    return [
+        pltpu.SemaphoreType.DMA((9 * pieces,)),
+        pltpu.SemaphoreType.DMA((pieces,)),
+        pltpu.SemaphoreType.DMA((pieces,)),
+        pltpu.SemaphoreType.DMA((2, pieces)),
+        pltpu.SemaphoreType.DMA((5, pieces)),
+    ]
 
 
 class Parts:
@@ -255,7 +261,7 @@
     plane_send,
     plane_recv,
     plane_pair,
-    *gather_sems,
+    *sem_refs,
 ):
     where = place()
     row, col, z, core = where
@@ -276,10 +282,11 @@
     parts = Parts(where)
     mine, lane = parts.mine, lax.div(z, 2)
 
-    def ring_piece(at, k, p):
-        return wavelet.at[pl.ds(ring_place(at, k, p * 2), 2)]
-
-    gather = RowGather(ring_piece, gather_sems, where)
+    def ring_piece(at, k, p, h):
+        first = ring_place(at, k, p * 2)
+        return wavelet.at[pl.ds(first, 2) if h is None else pl.ds(first + h, 1)]
+
+    gather = RowGather(ring_piece, sem_refs, where)
     below, above = (row, lax.rem(col + NCOLS - 1, NCOLS)), (row, lax.rem(col + 1, NCOLS))
     wait_for_all = greet(
         [gather.neighbour(1), gather.neighbour(3), gather.partner(), below, above],
@@ -401,12 +408,15 @@
     up.wait_recv()
     down.wait_recv()
     lax.fori_loop(0, 2, smooth_one, 0)
-    gather.pass_on()
+    for p in range(2):
+        gather.pass_on(p)
     lax.fori_loop(2, PARTS, smooth_one, 0)
     for h in range(2):
         lax.fori_loop(h * GROUP, (h + 1) * GROUP, wait_plane, 0)
         swap(h).start()
-    gather.finish()
+    for p in range(2):
+        gather.finish(p)
+    gather.close(2)
     for h in range(2):
         ref = half_plane(1 - core, h)
         remote(ref, ref, plane_pair.at[h], plane_pair.at[2 + h], gather.partner()).wait_recv()
@@ -454,7 +464,7 @@
             pltpu.SemaphoreType.DMA((PARTS,)),
             pltpu.SemaphoreType.DMA((PARTS,)),
             pltpu.SemaphoreType.DMA((4,)),
-            *GATHER_SEMS,
+            *gather_sems(2),
         ],
         compiler_params=pltpu.CompilerParams(
             collective_id=0, has_side_effects=True, vmem_limit_bytes=VMEM_LIMIT
@@ -797,7 +807,7 @@
         for u in range(width):
             at = cols[0, first + u]
             part = at >> 3
-            adjoint[(at >> 2) & 1, at & 3, (part + shift) & 1, part >> 1] += terms[u]
+            adjoint[(at >> 2) & 1, at & 3, (part + shift) & 3, part >> 2] += terms[u]
 
     sensors.run(add)
     store.wait()
@@ -809,7 +819,7 @@
         adjoint_kernel,
         out_shape=(
             jax.ShapeDtypeStruct((ROW_BLOCKS, BLK, BLK), F32),
-            jax.ShapeDtypeStruct((2, NZ, 2, GROUP, BLK, BLK), F32),
+            jax.ShapeDtypeStruct((2, NZ, LANES, EACH, BLK, BLK), F32),
         ),
         in_specs=[SMEM, SMEM, SMEM, ANY, ANY],
         out_specs=(ANY, VMEM),
@@ -836,15 +846,15 @@
     parts = Parts(where)
     mine = parts.mine
 
-    def out_piece(at, k, p):
-        return out.at[at, k, pl.ds(p * GROUP, GROUP)]
+    def out_piece(at, k, p, h):
+        first = p * EACH
+        return out.at[at, k, pl.ds(first, EACH) if h is None else pl.ds(first + h, 1)]
 
     gather = RowGather(out_piece, sem_refs, where)
     plus, minus, partner = gather.neighbour(1), gather.neighbour(3), gather.partner()
     greet([plus, minus, partner], (parts.first, parts.device))()
-    rings = [Ring(z, plus, minus, send.at[p], recv.at[p]) for p in range(2)]
-    half = GROUP // 2
-    for p in range(2):
+    rings = [Ring(z, plus, minus, send.at[p], recv.at[p]) for p in range(LANES)]
+    for p in range(LANES):
         ring = rings[p]
         for slot, step in ((6, 2), (7, 1), (8, 3), (9, 0)):
             q = ring.at(step)
@@ -852,9 +862,8 @@
     fill.wait()
 
     def total(p, step, h):
-        group = pl.ds(h * half, half)
         q = rings[p].at(step)
-        return own[q, p, group] + pair[q, p, group]
+        return own[q, p, h] + pair[q, p, h]
 
     def paired(p, step, slot):
         rings[p].arrived(pair.at[rings[p].at(step), p], slot)
@@ -863,7 +872,7 @@
         relay_out[p, slot] = value.astype(BF16)
         rings[p].copy(relay_out.at[p, slot], dst, device, sem)
 
-    for p in range(2):
+    def launch(p):
         paired(p, 2, 6)
         ship(p, total(p, 2, 0), 0, relay.at[p, 0], plus, 0)
         ship(p, total(p, 2, 1), 1, relay.at[p, 1], minus, 1)
@@ -871,101 +880,111 @@
         ship(p, total(p, 1, 1), 3, landed.at[p, 0, 1], plus, 2)
         paired(p, 3, 8)
         ship(p, total(p, 3, 0), 4, landed.at[p, 1, 0], minus, 3)
-    for p in range(2):
+
+    def pass_on(p):
         ring = rings[p]
         ring.arrived(relay.at[p, 0], 0)
         ship(p, total(p, 1, 0) + relay[p, 0].astype(F32), 2, landed.at[p, 0, 0], plus, 4)
         ring.arrived(relay.at[p, 1], 1)
         ship(p, total(p, 3, 1) + relay[p, 1].astype(F32), 5, landed.at[p, 1, 1], minus, 5)
+
     lane_scale = scale[0:1, :]
 
-    def part_copy(i):
+    def member(p, i):
+        return i * LANES + lax.rem(p + PARTS - mine, LANES)
+
+    def part_copy(m):
         return remote(
-            stage.at[parts.slot(i)],
-            gathered.at[mine],
-            part_send.at[i],
-            part_recv.at[mine],
-            parts.device(i),
+            stage.at[m], gathered.at[mine], part_send.at[m], part_recv.at[mine], parts.device_at(m)
         )
 
-    def member(p, i):
-        return i * 2 + lax.rem(mine + p, 2)
-
-    for p in range(2):
+    def hand_over(p):
         ring = rings[p]
         paired(p, 0, 9)
-        for slot, ref in ((2, landed.at[p, 0, 1]), (3, landed.at[p, 1, 0]), (4, landed.at[p, 0, 0]), (5, landed.at[p, 1, 1])):
-            ring.arrived(ref, slot)
-        for i in range(GROUP):
-            h, j = i // half, i % half
-            value = own[z, p, i] + pair[z, p, i]
-            value = value + landed[p, 0, h, j].astype(F32) + landed[p, 1, h, j].astype(F32)
-            stage[member(p, i)] = (value * lane_scale).astype(BF16)
-
-        def spread(i, carry, p=p):
-            part_copy(2 * i + p).start()
-            return carry
-
-        if p == 0:
-
-            @pl.when(parts.first == 1)
-            def _():
-                gathered[mine] = stage[mine]
-
-        lax.fori_loop(parts.first if p == 0 else 0, GROUP, spread, 0)
-
-    for p in range(2):
-
-        def synthesise(i, carry, p=p):
-            m = member(p, i)
+        for slot, (side, h) in ((2, (0, 1)), (3, (1, 0)), (4, (0, 0)), (5, (1, 1))):
+            ring.arrived(landed.at[p, side, h], slot)
+        for h in range(EACH):
+            m = member(p, h)
+            value = total(p, 0, h) + (landed[p, 0, h].astype(F32) + landed[p, 1, h].astype(F32))
+            value = (value * lane_scale).astype(BF16)
+            stage[m] = value
+
+            @pl.when(parts.own(m))
+            def _(m=m):
+                gathered[m] = stage[m]
 
             @pl.when(jnp.logical_not(parts.own(m)))
-            def _():
+            def _(m=m):
+                part_copy(m).start()
+
+    def synthesise(p):
+        for h in range(EACH):
+            m = member(p, h)
+
+            @pl.when(jnp.logical_not(parts.own(m)))
+            def _(m=m):
                 ref = gathered.at[m]
                 remote(ref, ref, part_send.at[0], part_recv.at[m], partner).wait_recv()
 
             cells = lax.dot_general(
                 signs[...], gathered[m], (((1,), (1,)), ((), ())), preferred_element_type=F32
             )
-            out[z, core, p * GROUP + i] = (cells + smooth[m]).astype(BF16)
-            return carry
-
-        lax.fori_loop(0, GROUP, synthesise, 0)
+            out[z, core, p * EACH + h] = (cells + smooth[m]).astype(BF16)
         gather.begin(p)
-    gather.pass_on()
-    gather.finish()
-
-    def drain(i, carry):
-        part_copy(i).wait_send()
-        return carry
-
-    lax.fori_loop(parts.first, PARTS, drain, 0)
+
+    for p in range(LANES):
+        launch(p)
+    pass_on(0)
+    pass_on(1)
+    hand_over(0)
+    pass_on(2)
+    hand_over(1)
+    pass_on(3)
+    hand_over(2)
+    synthesise(0)
+    hand_over(3)
+    synthesise(1)
+    synthesise(2)
+    gather.pass_on(0)
+    synthesise(3)
+    for p in range(1, LANES):
+        gather.pass_on(p)
+        gather.finish(p - 1)
+    gather.finish(LANES - 1)
+    gather.close(LANES)
+
+    def drain(m, carry):
+        @pl.when(jnp.logical_not(parts.own(m)))
+        def _():
+            part_copy(m).wait_send()
+
+        return carry
+
+    lax.fori_loop(0, PARTS, drain, 0)
     for ring in rings:
         ring.drain()
 
 
 def give_back(partial, smooth):
-    vmem = pl.BlockSpec(memory_space=pltpu.VMEM)
-    half = GROUP // 2
     return pl.pallas_call(
         return_kernel,
         out_shape=jax.ShapeDtypeStruct((NZ, 2, PARTS, BLK, BLK), BF16),
-        in_specs=[ANY, vmem, vmem, vmem],
-        out_specs=vmem,
+        in_specs=[ANY, VMEM, VMEM, VMEM],
+        out_specs=VMEM,
         scratch_shapes=[
-            pltpu.VMEM((NZ, 2, GROUP, BLK, BLK), F32),
+            pltpu.VMEM((NZ, LANES, EACH, BLK, BLK), F32),
             pltpu.VMEM((PARTS, BLK, BLK), BF16),
-            pltpu.VMEM((NZ, 2, GROUP, BLK, BLK), F32),
-            pltpu.VMEM((2, 6, half, BLK, BLK), BF16),
-            pltpu.VMEM((2, 2, half, BLK, BLK), BF16),
-            pltpu.VMEM((2, 2, 2, half, BLK, BLK), BF16),
+            pltpu.VMEM((NZ, LANES, EACH, BLK, BLK), F32),
+            pltpu.VMEM((LANES, 6, BLK, BLK), BF16),
+            pltpu.VMEM((LANES, 2, BLK, BLK), BF16),
+            pltpu.VMEM((LANES, 2, 2, BLK, BLK), BF16),
             pltpu.VMEM((PARTS, BLK, BLK), BF16),
             pltpu.SemaphoreType.DMA,
-            pltpu.SemaphoreType.DMA((2, 10)),
-            pltpu.SemaphoreType.DMA((2, 10)),
+            pltpu.SemaphoreType.DMA((LANES, 10)),
+            pltpu.SemaphoreType.DMA((LANES, 10)),
             pltpu.SemaphoreType.DMA((PARTS,)),
             pltpu.SemaphoreType.DMA((PARTS,)),
-            *GATHER_SEMS,
+            *gather_sems(LANES),
         ],
         compiler_params=pltpu.CompilerParams(
             collective_id=2, has_side_effects=True, vmem_limit_bytes=VMEM_LIMIT
@@ -994,10 +1013,10 @@
     for i in range(2 * NZ):
         load(i).wait()
         for n in range(PARTS):
-            q, core, p = i // 2, i % 2, n // GROUP
+            q, core, p = i // 2, i % 2, n // EACH
             at = i * PARTS + n
             cells[at] = product[q, core, n].astype(F32)
-            m = (n % GROUP) * 2 + ((shift + p) & 1)
+            m = (n % EACH) * LANES + ((p + PARTS - shift) & (LANES - 1))
             store(at, order[0, (m * 2 + core) * 4 + q]).start()
 
     def finish(i, carry):

time: 116 us -> 118 us (1.017)
    pallas_call x1, Pallas kernels: 38.3 us -> 42.3 us  [give_back(): pl.pallas_call(return_kernel, out_shape=jax.ShapeDtypeStruct((NZ, 2, PART...]
    pallas_call x1, Pallas kernels: 31.3 us -> 29 us  [combine(): pl.pallas_call(kernel, out_shape=jax.ShapeDtypeStruct((rows, BLK), BF16),...]
where the time goes in v6:
time: 118 us
  Pallas kernels  116 us (98%)
  between operations  1.32 us (1%)
    pallas_call x1, Pallas kernels, give_back(): pl.pallas_call(return_kernel, out_shape=jax.ShapeDtypeStruct((NZ, 2, PART...  42.3 us
    pallas_call x1, Pallas kernels, combine(): pl.pallas_call(kernel, out_shape=jax.ShapeDtypeStruct((rows, BLK), BF16),...  29 us
    pallas_call x1, Pallas kernels, analyse(): pl.pallas_call(analyse_kernel, out_shape=(jax.ShapeDtypeStruct((COL_BLOCK...  27.2 us
    pallas_call x1, Pallas kernels, adjoin(): pl.pallas_call(adjoint_kernel, out_shape=(jax.ShapeDtypeStruct((ROW_BLOCK...  7.62 us
    pallas_call x1, Pallas kernels, forward(): pl.pallas_call(forward_kernel, out_shape=jax.ShapeDtypeStruct((ROW_BLOCKS...  5.92 us
    pallas_call x1, Pallas kernels, place_cells(): pl.pallas_call(place_kernel, out_shape=jax.ShapeDtypeStruct((COL_BLOCKS,...  4.22 us

profile of v6, /device:TPU:1, one launch (start us, length us, event | category | flops | bytes accessed | tf_op | source)
XLA Modules:
  0.0 117.5 jit_solution(7179295362578154051)
XLA Ops:
  1.3 27.2 %analyse.1 = (bf16[64,128,128]{2,1,0:T(8,128)(2,1)}, f32[8,128,128]{2,1,0:T(8,128)}) custom-call(s32[1,64]{1,0:T(1,128)} %order.3, f32[128,64,128]{2,1,0:T(8,128)} %bitcast.7, s32[4,8192]{1,0:T(4,128)} %neighbors_hbm.1, f32[4,8192]{1,0:T(4,128)} %weights_hbm.1, bf16[128,128]{1,0:T(8,128)(2,1)} %constant.8.clone.signs_hbm, f32[128,128]{1,0:T(8,128)} %constant.9.clone.scale_hbm), custom_call_target="tpu_custom_call" | custom-call | flops 1073741824 | bytes 62914560 | tf_op jit(solution)/shard_map/analyse/pallas_call | solution.py:443
  28.5 5.9 %forward.1 = f32[32,128,128]{2,1,0:T(8,128)} custom-call(s32[1,1]{1,0:T(1,128)S(6)} %copy.14.count, s32[1,384]{1,0:T(1,128)} %rows.3, s32[1,384]{1,0:T(1,128)} %cols.3, bf16[1,384,128,128]{3,2,1,0:T(8,128)(2,1)} %source.3, bf16[64,128,128]{2,1,0:T(8,128)(2,1)} %get-tuple-element.6.wavelet_hbm), custom_call_target="tpu_custom_call" | custom-call | tf_op jit(solution)/shard_map/forward/pallas_call | solution.py:560
  34.4 29.0 %combine.1 = bf16[4096,128]{1,0:T(8,128)(2,1)} custom-call(f32[4096,128]{1,0:T(8,128)} %bitcast.5), custom_call_target="tpu_custom_call" | custom-call | flops 1048576 | bytes 83886080 | tf_op jit(solution)/shard_map/combine/pallas_call | solution.py:760
  63.4 7.6 %adjoin.1 = (f32[32,128,128]{2,1,0:T(8,128)}, f32[2,4,4,2,128,128]{5,4,3,2,1,0:T(8,128)}) custom-call(s32[1,1]{1,0:T(1,128)S(6)} %copy.14.count, s32[1,384]{1,0:T(1,128)} %rows.3, s32[1,384]{1,0:T(1,128)} %cols.3, bf16[1,384,128,128]{3,2,1,0:T(8,128)(2,1)} %source.3, bf16[32,128,128]{2,1,0:T(8,128)(2,1)} %bitcast.6), custom_call_target="tpu_custom_call" | custom-call | tf_op jit(solution)/shard_map/adjoin/pallas_call | solution.py:818
  71.0 42.3 %give_back.1.product_hbm = bf16[4,2,8,128,128]{4,3,2,1,0:T(8,128)(2,1)} custom-call(f32[2,4,4,2,128,128]{5,4,3,2,1,0:T(8,128)} %get-tuple-element.8.partial, f32[8,128,128]{2,1,0:T(8,128)} %get-tuple-element.9.smooth, f32[8,128]{1,0:T(8,128)} %constant.10.clone.scale, bf16[128,128]{1,0:T(8,128)(2,1)} %constant.11.clone.signs), custom_call_target="tpu_custom_call" | custom-call | flops 1073741824 | bytes 83886080 | tf_op jit(solution)/shard_map/give_back/pallas_call | solution.py:969
  113.3 4.2 %place_cells.1 = f32[64,128,128]{2,1,0:T(8,128)} custom-call(s32[1,64]{1,0:T(1,128)} %order.3, bf16[4,2,8,128,128]{4,3,2,1,0:T(8,128)(2,1)} %give_back.1.product_hbm), custom_call_target="tpu_custom_call" | custom-call | tf_op jit(solution)/shard_map/place_cells/pallas_call | solution.py:1030

commit v7 on v6

--- a/solution.py
+++ b/solution.py
@@ -18,6 +18,7 @@
 SLOTS = 384
 CHUNK = 32
 VMEM_LIMIT = 56 << 20
+MIDDLE_LIMIT = 42 << 20
 MESH = pl.DeviceIdType.MESH
 F32 = jnp.float32
 BF16 = jnp.bfloat16
@@ -522,9 +523,7 @@
             done = done + groups * width
 
 
-def forward_kernel(count, rows, cols, source, wavelet_hbm, image, held, wavelet, places, sem, sems):
-    load = pltpu.make_async_copy(wavelet_hbm, wavelet, sem)
-    load.start()
+def forward_kernel(count, rows, cols, source, wavelet, image, held, places, sems):
     sensors = Sensors(count, source, held, sems)
     sensors.start()
     image[...] = jnp.zeros_like(image)
@@ -537,7 +536,6 @@
         return carry
 
     lax.fori_loop(0, COL_BLOCKS, note, 0)
-    load.wait()
 
     def add(first, width):
         terms = []
@@ -560,16 +558,14 @@
     return pl.pallas_call(
         forward_kernel,
         out_shape=jax.ShapeDtypeStruct((ROW_BLOCKS, BLK, BLK), F32),
-        in_specs=[SMEM, SMEM, SMEM, ANY, ANY],
+        in_specs=[SMEM, SMEM, SMEM, ANY, VMEM],
         out_specs=VMEM,
         scratch_shapes=[
             held,
-            pltpu.VMEM(wavelet.shape, BF16),
             pltpu.SMEM((COL_BLOCKS,), jnp.int32),
-            pltpu.SemaphoreType.DMA,
             sems,
         ],
-        compiler_params=pltpu.CompilerParams(vmem_limit_bytes=VMEM_LIMIT),
+        compiler_params=pltpu.CompilerParams(vmem_limit_bytes=MIDDLE_LIMIT),
         name="forward",
     )(count, rows, cols, sens, wavelet)
 
@@ -772,7 +768,7 @@
             pltpu.SemaphoreType.DMA,
         ],
         compiler_params=pltpu.CompilerParams(
-            collective_id=1, has_side_effects=True, vmem_limit_bytes=VMEM_LIMIT
+            collective_id=1, has_side_effects=True, vmem_limit_bytes=MIDDLE_LIMIT
         ),
         cost_estimate=cost(1 << 20, 80 << 20),
         name="combine",
@@ -780,14 +776,11 @@
 
 
 def adjoint_kernel(
-    count, rows, cols, source, image_hbm, data_image, adjoint, held, image, flipped, plain, sem, sems
+    count, rows, cols, source, image, data_image, adjoint, held, flipped, plain, sem, sems
 ):
-    load = pltpu.make_async_copy(image_hbm, image, sem.at[0])
-    load.start()
     sensors = Sensors(count, source, held, sems)
     sensors.start()
     adjoint[...] = jnp.zeros_like(adjoint)
-    load.wait()
 
     def flip(b, carry):
         block = image[b].astype(F32)
@@ -796,7 +789,7 @@
         return carry
 
     lax.fori_loop(0, ROW_BLOCKS, flip, 0, unroll=2)
-    store = pltpu.make_async_copy(plain, data_image, sem.at[1])
+    store = pltpu.make_async_copy(plain, data_image, sem)
     store.start()
     shift = lax.axis_index("cols") >> 1
 
@@ -821,17 +814,16 @@
             jax.ShapeDtypeStruct((ROW_BLOCKS, BLK, BLK), F32),
             jax.ShapeDtypeStruct((2, NZ, LANES, EACH, BLK, BLK), F32),
         ),
-        in_specs=[SMEM, SMEM, SMEM, ANY, ANY],
+        in_specs=[SMEM, SMEM, SMEM, ANY, VMEM],
         out_specs=(ANY, VMEM),
         scratch_shapes=[
             held,
             pltpu.VMEM((ROW_BLOCKS, BLK, BLK), BF16),
-            pltpu.VMEM((ROW_BLOCKS, BLK, BLK), BF16),
             pltpu.VMEM((ROW_BLOCKS, BLK, BLK), F32),
-            pltpu.SemaphoreType.DMA((2,)),
+            pltpu.SemaphoreType.DMA,
             sems,
         ],
-        compiler_params=pltpu.CompilerParams(vmem_limit_bytes=VMEM_LIMIT),
+        compiler_params=pltpu.CompilerParams(vmem_limit_bytes=MIDDLE_LIMIT),
         name="adjoin",
     )(count, rows, cols, sens, image)
 
@@ -987,7 +979,7 @@
             *gather_sems(LANES),
         ],
         compiler_params=pltpu.CompilerParams(
-            collective_id=2, has_side_effects=True, vmem_limit_bytes=VMEM_LIMIT
+            collective_id=2, has_side_effects=True, vmem_limit_bytes=MIDDLE_LIMIT
         ),
         cost_estimate=cost(1 << 30, 80 << 20),
         name="give_back",
@@ -999,19 +991,12 @@
     )
 
 
-def place_kernel(order, product_hbm, out, product, cells, in_sems, out_sems):
-    def load(i):
-        at = lax.div(i, 2), lax.rem(i, 2)
-        return pltpu.make_async_copy(product_hbm.at[at], product.at[at], in_sems.at[i])
-
+def place_kernel(order, product, out, cells, out_sems):
     def store(i, block):
         return pltpu.make_async_copy(cells.at[i], out.at[block], out_sems.at[i])
 
-    for i in range(2 * NZ):
-        load(i).start()
     shift = lax.axis_index("cols") >> 1
     for i in range(2 * NZ):
-        load(i).wait()
         for n in range(PARTS):
             q, core, p = i // 2, i % 2, n // EACH
             at = i * PARTS + n
@@ -1030,15 +1015,13 @@
     return pl.pallas_call(
         place_kernel,
         out_shape=jax.ShapeDtypeStruct((COL_BLOCKS, BLK, BLK), F32),
-        in_specs=[SMEM, ANY],
+        in_specs=[SMEM, VMEM],
         out_specs=ANY,
         scratch_shapes=[
-            pltpu.VMEM(product.shape, BF16),
             pltpu.VMEM((COL_BLOCKS, BLK, BLK), F32),
-            pltpu.SemaphoreType.DMA((2 * NZ,)),
             pltpu.SemaphoreType.DMA((COL_BLOCKS,)),
         ],
-        compiler_params=pltpu.CompilerParams(vmem_limit_bytes=VMEM_LIMIT),
+        compiler_params=pltpu.CompilerParams(vmem_limit_bytes=MIDDLE_LIMIT),
         name="place_cells",
     )(order, product)
 

time: 118 us -> 111 us (0.941)
  Pallas kernels: 116 us -> 108 us
  local copies, waits for them, and re-layouts: 0 us -> 1.62 us
    pallas_call x1, Pallas kernels: 7.62 us -> 4.06 us  [adjoin(): pl.pallas_call(adjoint_kernel, out_shape=(jax.ShapeDtypeStruct((ROW_BLOCK...]
    pallas_call x1, Pallas kernels: 5.92 us -> 3.31 us  [forward(): pl.pallas_call(forward_kernel, out_shape=jax.ShapeDtypeStruct((ROW_BLOCKS...]
    unnamed x0 -> x14, local copies, waits for them, and re-layouts: none -> 1.62 us
where the time goes in v7:
time: 111 us
  Pallas kernels  108 us (97%)
  local copies, waits for them, and re-layouts  1.62 us (1%)
  between operations  1.44 us (1%)
    pallas_call x1, Pallas kernels, give_back(): pl.pallas_call(return_kernel, out_shape=jax.ShapeDtypeStruct((NZ, 2, PART...  42.3 us
    pallas_call x1, Pallas kernels, combine(): pl.pallas_call(kernel, out_shape=jax.ShapeDtypeStruct((rows, BLK), BF16),...  27.9 us
    pallas_call x1, Pallas kernels, analyse(): pl.pallas_call(analyse_kernel, out_shape=(jax.ShapeDtypeStruct((COL_BLOCK...  27.2 us
    pallas_call x1, Pallas kernels, adjoin(): pl.pallas_call(adjoint_kernel, out_shape=(jax.ShapeDtypeStruct((ROW_BLOCK...  4.06 us
    pallas_call x1, Pallas kernels, forward(): pl.pallas_call(forward_kernel, out_shape=jax.ShapeDtypeStruct((ROW_BLOCKS...  3.31 us
    pallas_call x1, Pallas kernels, place_cells(): pl.pallas_call(place_kernel, out_shape=jax.ShapeDtypeStruct((COL_BLOCKS,...  3.14 us

profile of v7, /device:TPU:1, one launch (start us, length us, event | category | flops | bytes accessed | tf_op | source)
XLA Modules:
  0.0 110.9 jit_solution(9884504026257568510)
XLA Ops:
  0.6 0.0 copy-start.4
  0.6 0.0 copy-start.3
  1.3 27.2 %analyse.1 = (bf16[64,128,128]{2,1,0:T(8,128)(2,1)}, f32[8,128,128]{2,1,0:T(8,128)}) custom-call(s32[1,64]{1,0:T(1,128)} %order.3, f32[128,64,128]{2,1,0:T(8,128)} %bitcast.7, s32[4,8192]{1,0:T(4,128)} %neighbors_hbm.1, f32[4,8192]{1,0:T(4,128)} %weights_hbm.1, bf16[128,128]{1,0:T(8,128)(2,1)} %constant.8.clone.signs_hbm, f32[128,128]{1,0:T(8,128)} %constant.9.clone.scale_hbm), custom_call_target="tpu_custom_call" | custom-call | flops 1073741824 | bytes 62914560 | tf_op jit(solution)/shard_map/analyse/pallas_call | solution.py:444
  28.5 0.0 copy-done.4
  28.5 0.0 copy-done.3
  28.5 0.0 copy-start
  28.5 1.6 %copy-done = bf16[64,128,128]{2,1,0:T(8,128)(2,1)S(1)} copy-done((bf16[64,128,128]{2,1,0:T(8,128)(2,1)S(1)}, bf16[64,128,128]{2,1,0:T(8,128)(2,1)}, u32[]{:S(2)}) %copy-start) | copy-done | bytes 2097176
  30.1 3.3 %forward.1 = f32[32,128,128]{2,1,0:T(8,128)S(1)} custom-call(s32[1,1]{1,0:T(1,128)S(6)} %copy.14.count, s32[1,384]{1,0:T(1,128)S(1)} %copy-done.3, s32[1,384]{1,0:T(1,128)S(1)} %copy-done.4, bf16[1,384,128,128]{3,2,1,0:T(8,128)(2,1)} %source.3, bf16[64,128,128]{2,1,0:T(8,128)(2,1)S(1)} %copy-done), custom_call_target="tpu_custom_call" | custom-call | tf_op jit(solution)/shard_map/forward/pallas_call | solution.py:558
  33.4 27.9 %combine.1 = bf16[4096,128]{1,0:T(8,128)(2,1)S(1)} custom-call(f32[4096,128]{1,0:T(8,128)S(1)} %bitcast.5), custom_call_target="tpu_custom_call" | custom-call | flops 1048576 | bytes 83886080 | tf_op jit(solution)/shard_map/combine/pallas_call | solution.py:756
  61.3 0.0 copy-start.1
  61.3 0.0 copy-start.2
  61.3 0.0 copy-start.5
  61.4 4.1 %adjoin.1 = (f32[32,128,128]{2,1,0:T(8,128)}, f32[2,4,4,2,128,128]{5,4,3,2,1,0:T(8,128)S(1)}) custom-call(s32[1,1]{1,0:T(1,128)S(6)} %copy.14.count, s32[1,384]{1,0:T(1,128)S(1)} %copy-done.3, s32[1,384]{1,0:T(1,128)S(1)} %copy-done.4, bf16[1,384,128,128]{3,2,1,0:T(8,128)(2,1)} %source.3, bf16[32,128,128]{2,1,0:T(8,128)(2,1)S(1)} %bitcast.6), custom_call_target="tpu_custom_call" | custom-call | tf_op jit(solution)/shard_map/adjoin/pallas_call | solution.py:811
  65.4 0.0 copy-start.6
  65.4 0.0 copy-done.1
  65.4 0.0 copy-done.2
  65.5 0.0 copy-done.5
  65.5 42.3 %give_back.1.product = bf16[4,2,8,128,128]{4,3,2,1,0:T(8,128)(2,1)S(1)} custom-call(f32[2,4,4,2,128,128]{5,4,3,2,1,0:T(8,128)S(1)} %get-tuple-element.8.partial, f32[8,128,128]{2,1,0:T(8,128)S(1)} %copy-done.1, f32[8,128]{1,0:T(8,128)S(1)} %copy-done.5, bf16[128,128]{1,0:T(8,128)(2,1)S(1)} %copy-done.2), custom_call_target="tpu_custom_call" | custom-call | flops 1073741824 | bytes 83886080 | tf_op jit(solution)/shard_map/give_back/pallas_call | solution.py:961
  107.8 0.0 copy-done.6
  107.8 3.1 %place_cells.1 = f32[64,128,128]{2,1,0:T(8,128)} custom-call(s32[1,64]{1,0:T(1,128)S(1)} %copy-done.6, bf16[4,2,8,128,128]{4,3,2,1,0:T(8,128)(2,1)S(1)} %give_back.1.product), custom_call_target="tpu_custom_call" | custom-call | tf_op jit(solution)/shard_map/place_cells/pallas_call | solution.py:1015
Async XLA Ops:
  0.6 27.9 %copy-start.4 = (s32[1,384]{1,0:T(1,128)S(1)}, s32[1,384]{1,0:T(1,128)}, u32[]{:S(2)}) copy-start(s32[1,384]{1,0:T(1,128)} %cols.3) | copy-start | bytes 4612
  0.6 27.9 %copy-start.3 = (s32[1,384]{1,0:T(1,128)S(1)}, s32[1,384]{1,0:T(1,128)}, u32[]{:S(2)}) copy-start(s32[1,384]{1,0:T(1,128)} %rows.3) | copy-start | bytes 4612
  28.5 1.6 %copy-start = (bf16[64,128,128]{2,1,0:T(8,128)(2,1)S(1)}, bf16[64,128,128]{2,1,0:T(8,128)(2,1)}, u32[]{:S(2)}) copy-start(bf16[64,128,128]{2,1,0:T(8,128)(2,1)} %get-tuple-element.6.wavelet) | copy-start | bytes 6291460
  61.3 4.1 %copy-start.1 = (f32[8,128,128]{2,1,0:T(8,128)S(1)}, f32[8,128,128]{2,1,0:T(8,128)}, u32[]{:S(2)}) copy-start(f32[8,128,128]{2,1,0:T(8,128)} %get-tuple-element.9.smooth) | copy-start | bytes 1572868
  61.3 4.1 %copy-start.2 = (bf16[128,128]{1,0:T(8,128)(2,1)S(1)}, bf16[128,128]{1,0:T(8,128)(2,1)}, u32[]{:S(2)}) copy-start(bf16[128,128]{1,0:T(8,128)(2,1)} %constant.11.clone.signs) | copy-start | bytes 98308
  61.3 4.1 %copy-start.5 = (f32[8,128]{1,0:T(8,128)S(1)}, f32[8,128]{1,0:T(8,128)}, u32[]{:S(2)}) copy-start(f32[8,128]{1,0:T(8,128)} %constant.10.clone.scale) | copy-start | bytes 12292
  65.4 42.4 %copy-start.6 = (s32[1,64]{1,0:T(1,128)S(1)}, s32[1,64]{1,0:T(1,128)}, u32[]{:S(2)}) copy-start(s32[1,64]{1,0:T(1,128)} %order.3) | copy-start | bytes 772

commit v8 on v7

--- a/solution.py
+++ b/solution.py
@@ -17,8 +17,10 @@
 COL_BLOCKS = 64
 SLOTS = 384
 CHUNK = 32
-VMEM_LIMIT = 56 << 20
+VMEM_LIMIT = 51 << 20
 MIDDLE_LIMIT = 42 << 20
+ADJOIN_LIMIT = 38 << 20
+LATE_LIMIT = 32 << 20
 MESH = pl.DeviceIdType.MESH
 F32 = jnp.float32
 BF16 = jnp.bfloat16
@@ -46,6 +48,25 @@
 
 
 SIGNS, SCALE = haar_parts()
+
+
+def haar_tiles():
+    row = lax.broadcasted_iota(jnp.int32, (BLK, BLK), 0)
+    col = lax.broadcasted_iota(jnp.int32, (BLK, BLK), 1)
+    width = jnp.full((BLK, BLK), BLK, jnp.int32)
+    start = jnp.zeros((BLK, BLK), jnp.int32)
+    scale = jnp.full((BLK, BLK), SCALE[0], F32)
+    for level in range(7):
+        first, long = 1 << level, BLK >> level
+        inside = row >= first
+        width = jnp.where(inside, long, width)
+        start = jnp.where(inside, (row - first) * long, start)
+        scale = jnp.where(inside, np.float32(SCALE[first]), scale)
+    at = col - start
+    middle = jnp.where(row == 0, width, jnp.where(width > 0, width >> 1, 0))
+    signs = jnp.where(at < middle, 1.0, -1.0)
+    signs = jnp.where((at >= 0) & (at < width), signs, 0.0)
+    return signs.astype(BF16), scale
 
 
 def split(value):
@@ -241,19 +262,9 @@
 def analyse_kernel(
     order,
     model,
-    neighbors_hbm,
-    weights_hbm,
-    signs_hbm,
-    scale_hbm,
     wavelet,
-    smooth,
+    rims,
     body,
-    neighbors,
-    weights,
-    signs,
-    scale,
-    rims,
-    tables,
     ring_stage,
     plane_stage,
     sems,
@@ -266,20 +277,8 @@
 ):
     where = place()
     row, col, z, core = where
-    fills = [
-        pltpu.make_async_copy(src, dst, sems.at[4 + i])
-        for i, (src, dst) in enumerate(
-            (
-                (model, body),
-                (signs_hbm, signs),
-                (scale_hbm, scale),
-                (neighbors_hbm, neighbors),
-                (weights_hbm, weights),
-            )
-        )
-    ]
-    for fill in fills:
-        fill.start()
+    fill = pltpu.make_async_copy(model, body, sems.at[4])
+    fill.start()
     parts = Parts(where)
     mine, lane = parts.mine, lax.div(z, 2)
 
@@ -307,9 +306,9 @@
         sems.at[3],
         below,
     )
-    for fill in fills:
-        fill.wait()
-    sign_pair = jnp.concatenate([signs[...], signs[...]], axis=1)
+    signs, scale = haar_tiles()
+    sign_pair = jnp.concatenate([signs, signs], axis=1)
+    fill.wait()
 
     def block_of(m, q):
         return order[0, (m * 2 + core) * 4 + q]
@@ -317,7 +316,7 @@
     def coefficients(m, q):
         high, low = split(cells_of(body, block_of(m, q)))
         product = dot(sign_pair, jnp.concatenate([high, low], axis=0))
-        return (product * scale[...]).astype(BF16)
+        return (product * scale).astype(BF16)
 
     def ring_part(i):
         return i * 2 + lax.rem(lane + mine, 2)
@@ -398,20 +397,11 @@
         ref = half_plane(core, h)
         return remote(ref, ref, plane_pair.at[h], plane_pair.at[2 + h], gather.partner())
 
-    def smooth_one(m, carry):
-        smooth[m] = smooth_tile(body, rims, tables, block_of(m, z))
-        return carry
-
     for p in range(2):
         lax.fori_loop(2 * p, 2 * p + 2, wait_ring, 0)
         gather.begin(p)
-    tabulate(neighbors, weights, tables, col * CELLS)
-    up.wait_recv()
-    down.wait_recv()
-    lax.fori_loop(0, 2, smooth_one, 0)
     for p in range(2):
         gather.pass_on(p)
-    lax.fori_loop(2, PARTS, smooth_one, 0)
     for h in range(2):
         lax.fori_loop(h * GROUP, (h + 1) * GROUP, wait_plane, 0)
         swap(h).start()
@@ -436,30 +426,24 @@
 
     lax.fori_loop(0, GROUP, drain_ring, 0)
     lax.fori_loop(parts.first, PARTS, drain_plane, 0)
-    up.wait_send()
-    down.wait_send()
-
-
-def analyse(order, model, neighbors, weights):
+    up.wait()
+    down.wait()
+
+
+def analyse(order, model):
     return pl.pallas_call(
         analyse_kernel,
         out_shape=(
             jax.ShapeDtypeStruct((COL_BLOCKS, BLK, BLK), BF16),
-            jax.ShapeDtypeStruct((PARTS, BLK, BLK), F32),
+            jax.ShapeDtypeStruct((2, RIM, BLK), F32),
         ),
-        in_specs=[SMEM, *[ANY] * 5],
+        in_specs=[SMEM, ANY],
         out_specs=(VMEM, VMEM),
         scratch_shapes=[
             pltpu.VMEM((2 * COL_BLOCKS, RIM, BLK), F32),
-            pltpu.VMEM((4, CELLS), jnp.int32),
-            pltpu.VMEM((4, CELLS), F32),
-            pltpu.VMEM((BLK, BLK), BF16),
-            pltpu.VMEM((BLK, BLK), F32),
-            pltpu.VMEM((2, RIM, BLK), F32),
-            pltpu.VMEM((COL_BLOCKS, 8, BLK), F32),
             pltpu.VMEM((GROUP, BLK, BLK), BF16),
             pltpu.VMEM((PARTS, 2, BLK, BLK), BF16),
-            pltpu.SemaphoreType.DMA((9,)),
+            pltpu.SemaphoreType.DMA((5,)),
             pltpu.SemaphoreType.DMA((GROUP,)),
             pltpu.SemaphoreType.DMA((GROUP,)),
             pltpu.SemaphoreType.DMA((PARTS,)),
@@ -472,14 +456,7 @@
         ),
         cost_estimate=cost(1 << 30, 60 << 20),
         name="analyse",
-    )(
-        order,
-        model.reshape(2 * COL_BLOCKS, RIM, BLK),
-        neighbors,
-        weights,
-        jnp.asarray(SIGNS, BF16),
-        jnp.asarray(np.broadcast_to(SCALE[:, None], (BLK, BLK)), F32),
-    )
+    )(order, model)
 
 
 class Sensors:
@@ -688,7 +665,7 @@
 SMALL = BIG // 4
 
 
-def combine_kernel(partial, image, fill, big_relay, big_landed, small_landed, send, recv):
+def combine_kernel(partial, flipped, plain, image, fill, big_relay, big_landed, small_landed, send, recv):
     row, col, _, _ = place()
     y, x = lax.div(col, 4), lax.rem(col, 4)
     x_ring = [(row, y * 4 + lax.rem(x + step, 4)) for step in range(4)]
@@ -739,6 +716,15 @@
             last[a].begin()
     for a in streams:
         last[a].finish()
+
+        def turn(b, carry):
+            block = image[pl.ds(pl.multiple_of(b * BLK, BLK), BLK), :].astype(F32)
+            plain[b] = block
+            flipped[b] = block.T.astype(BF16)
+            return carry
+
+        blocks = STREAM // BLK
+        lax.fori_loop(a * blocks, (a + 1) * blocks, turn, 0, unroll=2)
     for group in (wide_rings, cross_rings, back_rings, last_rings):
         for one in group:
             one.drain()
@@ -748,18 +734,22 @@
     vmem = pl.BlockSpec(memory_space=pltpu.VMEM)
     rows = ROW_BLOCKS * BLK
 
-    def kernel(partial_ref, image_ref, data, *rest):
+    def kernel(partial_ref, flipped, plain, data, image, *rest):
         copy = pltpu.make_async_copy(partial_ref, data, rest[-1])
         copy.start()
-        combine_kernel(data, image_ref, copy, *rest[:-1])
+        combine_kernel(data, flipped, plain, image, copy, *rest[:-1])
 
     return pl.pallas_call(
         kernel,
-        out_shape=jax.ShapeDtypeStruct((rows, BLK), BF16),
-        in_specs=[pl.BlockSpec(memory_space=pl.ANY)],
-        out_specs=vmem,
+        out_shape=(
+            jax.ShapeDtypeStruct((ROW_BLOCKS, BLK, BLK), BF16),
+            jax.ShapeDtypeStruct((ROW_BLOCKS, BLK, BLK), F32),
+        ),
+        in_specs=[ANY],
+        out_specs=(VMEM, VMEM),
         scratch_shapes=[
             pltpu.VMEM((rows, BLK), F32),
+            pltpu.VMEM((rows, BLK), BF16),
             pltpu.VMEM((STREAMS, 2, BIG // 2, BLK), F32),
             pltpu.VMEM((STREAMS, 2, BIG, BLK), F32),
             pltpu.VMEM((STREAMS, 3, SMALL, BLK), F32),
@@ -776,21 +766,13 @@
 
 
 def adjoint_kernel(
-    count, rows, cols, source, image, data_image, adjoint, held, flipped, plain, sem, sems
+    count, rows, cols, source, flipped, plain, data_image, adjoint, held, sem, sems
 ):
     sensors = Sensors(count, source, held, sems)
     sensors.start()
-    adjoint[...] = jnp.zeros_like(adjoint)
-
-    def flip(b, carry):
-        block = image[b].astype(F32)
-        plain[b] = block
-        flipped[b] = block.T.astype(BF16)
-        return carry
-
-    lax.fori_loop(0, ROW_BLOCKS, flip, 0, unroll=2)
     store = pltpu.make_async_copy(plain, data_image, sem)
     store.start()
+    adjoint[...] = jnp.zeros_like(adjoint)
     shift = lax.axis_index("cols") >> 1
 
     def add(first, width):
@@ -806,7 +788,7 @@
     store.wait()
 
 
-def adjoin(count, rows, cols, sens, image):
+def adjoin(count, rows, cols, sens, flipped, plain):
     held, sems = SENSOR_SCRATCH
     return pl.pallas_call(
         adjoint_kernel,
@@ -814,22 +796,16 @@
             jax.ShapeDtypeStruct((ROW_BLOCKS, BLK, BLK), F32),
             jax.ShapeDtypeStruct((2, NZ, LANES, EACH, BLK, BLK), F32),
         ),
-        in_specs=[SMEM, SMEM, SMEM, ANY, VMEM],
+        in_specs=[SMEM, SMEM, SMEM, ANY, VMEM, ANY],
         out_specs=(ANY, VMEM),
-        scratch_shapes=[
-            held,
-            pltpu.VMEM((ROW_BLOCKS, BLK, BLK), BF16),
-            pltpu.VMEM((ROW_BLOCKS, BLK, BLK), F32),
-            pltpu.SemaphoreType.DMA,
-            sems,
-        ],
-        compiler_params=pltpu.CompilerParams(vmem_limit_bytes=MIDDLE_LIMIT),
+        scratch_shapes=[held, pltpu.SemaphoreType.DMA, sems],
+        compiler_params=pltpu.CompilerParams(vmem_limit_bytes=ADJOIN_LIMIT),
         name="adjoin",
-    )(count, rows, cols, sens, image)
+    )(count, rows, cols, sens, flipped, plain)
 
 
 def return_kernel(
-    partial, smooth, scale, signs, out, own, stage, pair, relay_out, relay, landed, gathered, sem, send, recv, part_send, part_recv, *sem_refs
+    order, partial, body, rims, neighbors, weights, scale, signs, out, smooth, tables, own, stage, pair, relay_out, relay, landed, gathered, sem, send, recv, part_send, part_recv, *sem_refs
 ):
     where = place()
     row, col, z, core = where
@@ -924,17 +900,27 @@
             out[z, core, p * EACH + h] = (cells + smooth[m]).astype(BF16)
         gather.begin(p)
 
+    def smooth_one(m, carry):
+        block = order[0, (m * 2 + core) * 4 + z]
+        smooth[m] = smooth_tile(body, rims, tables, block)
+        return carry
+
     for p in range(LANES):
         launch(p)
+        if p == 0:
+            tabulate(neighbors, weights, tables, col * CELLS)
+    lax.fori_loop(0, 2, smooth_one, 0)
     pass_on(0)
     pass_on(1)
     hand_over(0)
     pass_on(2)
     hand_over(1)
     pass_on(3)
+    lax.fori_loop(2, 4, smooth_one, 0)
     hand_over(2)
+    hand_over(3)
+    lax.fori_loop(4, PARTS, smooth_one, 0)
     synthesise(0)
-    hand_over(3)
     synthesise(1)
     synthesise(2)
     gather.pass_on(0)
@@ -957,13 +943,15 @@
         ring.drain()
 
 
-def give_back(partial, smooth):
+def give_back(order, partial, model, rims, neighbors, weights):
     return pl.pallas_call(
         return_kernel,
         out_shape=jax.ShapeDtypeStruct((NZ, 2, PARTS, BLK, BLK), BF16),
-        in_specs=[ANY, VMEM, VMEM, VMEM],
+        in_specs=[SMEM, ANY, *[VMEM] * 6],
         out_specs=VMEM,
         scratch_shapes=[
+            pltpu.VMEM((PARTS, BLK, BLK), F32),
+            pltpu.VMEM((COL_BLOCKS, 8, BLK), F32),
             pltpu.VMEM((NZ, LANES, EACH, BLK, BLK), F32),
             pltpu.VMEM((PARTS, BLK, BLK), BF16),
             pltpu.VMEM((NZ, LANES, EACH, BLK, BLK), F32),
@@ -979,13 +967,17 @@
             *gather_sems(LANES),
         ],
         compiler_params=pltpu.CompilerParams(
-            collective_id=2, has_side_effects=True, vmem_limit_bytes=MIDDLE_LIMIT
+            collective_id=2, has_side_effects=True, vmem_limit_bytes=LATE_LIMIT
         ),
         cost_estimate=cost(1 << 30, 80 << 20),
         name="give_back",
     )(
+        order,
         partial,
-        smooth,
+        model,
+        rims,
+        neighbors,
+        weights,
         jnp.asarray(np.broadcast_to(SCALE[None, :], (8, BLK)), F32),
         jnp.asarray(SIGNS.T, BF16),
     )
@@ -1027,11 +1019,13 @@
 
 
 def local(model_dir, sens_blocks, blk_row, blk_col, blk_count, send_order, neighbors, face_weight):
-    wavelet, smooth = analyse(send_order, model_dir, neighbors, face_weight)
+    model = model_dir.reshape(2 * COL_BLOCKS, RIM, BLK)
+    wavelet, rims = analyse(send_order, model)
     partial_image = forward(blk_count, blk_row, blk_col, sens_blocks, wavelet)
-    image_half = combine(partial_image).reshape(ROW_BLOCKS, BLK, BLK)
-    data_image, partial_adjoint = adjoin(blk_count, blk_row, blk_col, sens_blocks, image_half)
-    normal_product = place_cells(send_order, give_back(partial_adjoint, smooth))
+    flipped, plain = combine(partial_image)
+    data_image, partial_adjoint = adjoin(blk_count, blk_row, blk_col, sens_blocks, flipped, plain)
+    product = give_back(send_order, partial_adjoint, model, rims, neighbors, face_weight)
+    normal_product = place_cells(send_order, product)
     return data_image.reshape(ROW_BLOCKS * BLK, BLK), normal_product.reshape(CELLS, BLK)
 
 

time: 111 us -> 113 us (1.018)
  Pallas kernels: 108 us -> 110 us
    pallas_call x1, Pallas kernels: 27.2 us -> 23.5 us  [analyse(): pl.pallas_call(analyse_kernel, out_shape=(jax.ShapeDtypeStruct((COL_BLOCK...]
    pallas_call x1, Pallas kernels: 27.9 us -> 30.4 us  [combine(): pl.pallas_call(kernel, out_shape=(jax.ShapeDtypeStruct((ROW_BLOCKS, BLK,...]
    pallas_call x1, Pallas kernels: 42.3 us -> 44.6 us  [give_back(): pl.pallas_call(return_kernel, out_shape=jax.ShapeDtypeStruct((NZ, 2, PART...]
where the time goes in v8:
time: 113 us
  Pallas kernels  110 us (97%)
  between operations  1.44 us (1%)
    pallas_call x1, Pallas kernels, give_back(): pl.pallas_call(return_kernel, out_shape=jax.ShapeDtypeStruct((NZ, 2, PART...  44.6 us
    pallas_call x1, Pallas kernels, combine(): pl.pallas_call(kernel, out_shape=(jax.ShapeDtypeStruct((ROW_BLOCKS, BLK,...  30.4 us
    pallas_call x1, Pallas kernels, analyse(): pl.pallas_call(analyse_kernel, out_shape=(jax.ShapeDtypeStruct((COL_BLOCK...  23.5 us
    pallas_call x1, Pallas kernels, adjoin(): pl.pallas_call(adjoint_kernel, out_shape=(jax.ShapeDtypeStruct((ROW_BLOCK...  4.89 us
    pallas_call x1, Pallas kernels, forward(): pl.pallas_call(forward_kernel, out_shape=jax.ShapeDtypeStruct((ROW_BLOCKS...  3.85 us
    pallas_call x1, Pallas kernels, place_cells(): pl.pallas_call(place_kernel, out_shape=jax.ShapeDtypeStruct((COL_BLOCKS,...  3.14 us

profile of v8, /device:TPU:1, one launch (start us, length us, event | category | flops | bytes accessed | tf_op | source)
XLA Modules:
  0.0 112.5 jit_solution(8177142964923653122)
XLA Ops:
  1.3 0.0 copy-start.6
  1.3 0.6 copy-done.6
  1.9 0.0 copy-start.4
  1.9 0.0 copy-start.5
  1.9 23.5 %analyse.1 = (bf16[64,128,128]{2,1,0:T(8,128)(2,1)S(1)}, f32[2,64,128]{2,1,0:T(8,128)S(1)}) custom-call(s32[1,64]{1,0:T(1,128)S(1)} %copy-done.6, f32[128,64,128]{2,1,0:T(8,128)} %bitcast.4), custom_call_target="tpu_custom_call" | custom-call | flops 1073741824 | bytes 62914560 | tf_op jit(solution)/shard_map/analyse/pallas_call | solution.py:434
  25.4 0.0 copy-done.4
  25.4 0.0 copy-done.5
  25.4 3.8 %forward.1 = f32[32,128,128]{2,1,0:T(8,128)S(1)} custom-call(s32[1,1]{1,0:T(1,128)S(6)} %copy.12.count, s32[1,384]{1,0:T(1,128)S(1)} %copy-done.4, s32[1,384]{1,0:T(1,128)S(1)} %copy-done.5, bf16[1,384,128,128]{3,2,1,0:T(8,128)(2,1)} %source.3, bf16[64,128,128]{2,1,0:T(8,128)(2,1)S(1)} %get-tuple-element.8.wavelet), custom_call_target="tpu_custom_call" | custom-call | tf_op jit(solution)/shard_map/forward/pallas_call | solution.py:535
  29.3 30.4 %combine.1 = (bf16[32,128,128]{2,1,0:T(8,128)(2,1)S(1)}, f32[32,128,128]{2,1,0:T(8,128)S(1)}) custom-call(f32[4096,128]{1,0:T(8,128)S(1)} %bitcast.6), custom_call_target="tpu_custom_call" | custom-call | flops 1048576 | bytes 83886080 | tf_op jit(solution)/shard_map/combine/pallas_call | solution.py:742
  59.7 0.0 copy-start
  59.7 0.0 copy-start.1
  59.7 0.0 copy-start.2
  59.7 0.0 copy-start.3
  59.8 0.0 copy-start.7
  59.8 0.0 copy-start.8
  59.8 4.9 %adjoin.1 = (f32[32,128,128]{2,1,0:T(8,128)}, f32[2,4,4,2,128,128]{5,4,3,2,1,0:T(8,128)S(1)}) custom-call(s32[1,1]{1,0:T(1,128)S(6)} %copy.12.count, s32[1,384]{1,0:T(1,128)S(1)} %copy-done.4, s32[1,384]{1,0:T(1,128)S(1)} %copy-done.5, bf16[1,384,128,128]{3,2,1,0:T(8,128)(2,1)} %source.3, bf16[32,128,128]{2,1,0:T(8,128)(2,1)S(1)} %get-tuple-element.9.flipped, ...), custom_call_target="tpu_custom_call" | custom-call | tf_op jit(solution)/shard_map/adjoin/pallas_call | solution.py:793
  64.7 0.0 copy-done
  64.7 0.0 copy-done.1
  64.7 0.0 copy-done.2
  64.7 0.0 copy-done.3
  64.7 0.0 copy-done.7
  64.7 0.0 copy-done.8
  64.7 44.6 %give_back.1.product = bf16[4,2,8,128,128]{4,3,2,1,0:T(8,128)(2,1)S(1)} custom-call(s32[1,64]{1,0:T(1,128)S(1)} %copy-done.7, f32[2,4,4,2,128,128]{5,4,3,2,1,0:T(8,128)S(1)} %get-tuple-element.12.partial, f32[128,64,128]{2,1,0:T(8,128)S(1)} %bitcast.5, f32[2,64,128]{2,1,0:T(8,128)S(1)} %get-tuple-element.13.rims, s32[4,8192]{1,0:T(4,128)S(1)} %copy-done.1, ...), custom_call_target="tpu_custom_call" | custom-call | flops 1073741824 | bytes 83886080 | tf_op jit(solution)/shard_map/give_back/pallas_call | solution.py:947
  109.4 3.1 %place_cells.1 = f32[64,128,128]{2,1,0:T(8,128)} custom-call(s32[1,64]{1,0:T(1,128)S(1)} %copy-done.7, bf16[4,2,8,128,128]{4,3,2,1,0:T(8,128)(2,1)S(1)} %give_back.1.product), custom_call_target="tpu_custom_call" | custom-call | tf_op jit(solution)/shard_map/place_cells/pallas_call | solution.py:1007
Async XLA Ops:
  1.3 0.7 copy-start.6
  1.9 23.5 %copy-start.4 = (s32[1,384]{1,0:T(1,128)S(1)}, s32[1,384]{1,0:T(1,128)}, u32[]{:S(2)}) copy-start(s32[1,384]{1,0:T(1,128)} %rows.3) | copy-start | bytes 4612
  1.9 23.5 %copy-start.5 = (s32[1,384]{1,0:T(1,128)S(1)}, s32[1,384]{1,0:T(1,128)}, u32[]{:S(2)}) copy-start(s32[1,384]{1,0:T(1,128)} %cols.3) | copy-start | bytes 4612
  59.7 5.0 %copy-start = (f32[8192,128]{1,0:T(8,128)S(1)}, f32[8192,128]{1,0:T(8,128)}, u32[]{:S(2)}) copy-start(f32[8192,128]{1,0:T(8,128)} %param.10) | copy-start | bytes 12582916
  59.7 5.0 %copy-start.1 = (s32[4,8192]{1,0:T(4,128)S(1)}, s32[4,8192]{1,0:T(4,128)}, u32[]{:S(2)}) copy-start(s32[4,8192]{1,0:T(4,128)} %neighbors.1) | copy-start | bytes 393220
  59.7 5.0 %copy-start.2 = (f32[4,8192]{1,0:T(4,128)S(1)}, f32[4,8192]{1,0:T(4,128)}, u32[]{:S(2)}) copy-start(f32[4,8192]{1,0:T(4,128)} %weights.1) | copy-start | bytes 393220
  59.7 5.0 %copy-start.3 = (bf16[128,128]{1,0:T(8,128)(2,1)S(1)}, bf16[128,128]{1,0:T(8,128)(2,1)}, u32[]{:S(2)}) copy-start(bf16[128,128]{1,0:T(8,128)(2,1)} %constant.5.clone.signs) | copy-start | bytes 98308
  59.8 5.0 %copy-start.7 = (s32[1,64]{1,0:T(1,128)S(1)}, s32[1,64]{1,0:T(1,128)}, u32[]{:S(2)}) copy-start(s32[1,64]{1,0:T(1,128)} %order.5) | copy-start | bytes 772
  59.8 5.0 %copy-start.8 = (f32[8,128]{1,0:T(8,128)S(1)}, f32[8,128]{1,0:T(8,128)}, u32[]{:S(2)}) copy-start(f32[8,128]{1,0:T(8,128)} %constant.4.clone.scale) | copy-start | bytes 12292

commit v9 on v8

--- a/solution.py
+++ b/solution.py
@@ -17,7 +17,7 @@
 COL_BLOCKS = 64
 SLOTS = 384
 CHUNK = 32
-VMEM_LIMIT = 51 << 20
+VMEM_LIMIT = 101 << 19
 MIDDLE_LIMIT = 42 << 20
 ADJOIN_LIMIT = 38 << 20
 LATE_LIMIT = 32 << 20
@@ -230,18 +230,21 @@
     lax.fori_loop(0, COL_BLOCKS, tile, 0)
 
 
-def smooth_tile(body, rims, tables, tile):
-    table = tables[tile].T
+def window_of(body, rims, tile):
+    last = COL_BLOCKS - 1
+    low = jnp.where(tile == 0, rims[0], body[jnp.maximum(2 * tile - 1, 0)])
+    high = jnp.where(tile == last, rims[1], body[jnp.minimum(2 * tile + 2, 2 * last)])
+    return jnp.concatenate([low, cells_of(body, tile), high], axis=0)
+
+
+def smooth_tile(window, table):
+    table = table.T
     span = lax.broadcasted_iota(jnp.int32, (BLK, 2 * BLK), 1).astype(F32)
     mix = jnp.zeros((BLK, 2 * BLK), F32)
     for face in range(4):
         mix += jnp.where(table[:, face : face + 1] == span, table[:, 4 + face : 5 + face], 0.0)
     mix_high, mix_low = split(mix)
-    center = cells_of(body, tile)
-    last = COL_BLOCKS - 1
-    low = jnp.where(tile == 0, rims[0], body[jnp.maximum(2 * tile - 1, 0)])
-    high = jnp.where(tile == last, rims[1], body[jnp.minimum(2 * tile + 2, 2 * last)])
-    window = jnp.concatenate([low, center, high], axis=0)
+    center = window[RIM : RIM + BLK]
     near_high, near_low = split(window)
     mixed = dot(mix_high, near_high) + dot(mix_low, near_high) + dot(mix_high, near_low)
     total = table[:, 4:5] + table[:, 5:6] + table[:, 6:7] + table[:, 7:8]
@@ -263,8 +266,9 @@
     order,
     model,
     wavelet,
+    windows,
+    body,
     rims,
-    body,
     ring_stage,
     plane_stage,
     sems,
@@ -400,6 +404,14 @@
     for p in range(2):
         lax.fori_loop(2 * p, 2 * p + 2, wait_ring, 0)
         gather.begin(p)
+    up.wait_recv()
+    down.wait_recv()
+
+    def keep_window(m, carry):
+        windows[m] = window_of(body, rims, block_of(m, z))
+        return carry
+
+    lax.fori_loop(0, PARTS, keep_window, 0)
     for p in range(2):
         gather.pass_on(p)
     for h in range(2):
@@ -426,8 +438,8 @@
 
     lax.fori_loop(0, GROUP, drain_ring, 0)
     lax.fori_loop(parts.first, PARTS, drain_plane, 0)
-    up.wait()
-    down.wait()
+    up.wait_send()
+    down.wait_send()
 
 
 def analyse(order, model):
@@ -435,12 +447,13 @@
         analyse_kernel,
         out_shape=(
             jax.ShapeDtypeStruct((COL_BLOCKS, BLK, BLK), BF16),
-            jax.ShapeDtypeStruct((2, RIM, BLK), F32),
+            jax.ShapeDtypeStruct((PARTS, 2 * BLK, BLK), F32),
         ),
         in_specs=[SMEM, ANY],
         out_specs=(VMEM, VMEM),
         scratch_shapes=[
             pltpu.VMEM((2 * COL_BLOCKS, RIM, BLK), F32),
+            pltpu.VMEM((2, RIM, BLK), F32),
             pltpu.VMEM((GROUP, BLK, BLK), BF16),
             pltpu.VMEM((PARTS, 2, BLK, BLK), BF16),
             pltpu.SemaphoreType.DMA((5,)),
@@ -665,7 +678,7 @@
 SMALL = BIG // 4
 
 
-def combine_kernel(partial, flipped, plain, image, fill, big_relay, big_landed, small_landed, send, recv):
+def combine_kernel(partial, image, fill, big_relay, big_landed, small_landed, send, recv):
     row, col, _, _ = place()
     y, x = lax.div(col, 4), lax.rem(col, 4)
     x_ring = [(row, y * 4 + lax.rem(x + step, 4)) for step in range(4)]
@@ -716,15 +729,6 @@
             last[a].begin()
     for a in streams:
         last[a].finish()
-
-        def turn(b, carry):
-            block = image[pl.ds(pl.multiple_of(b * BLK, BLK), BLK), :].astype(F32)
-            plain[b] = block
-            flipped[b] = block.T.astype(BF16)
-            return carry
-
-        blocks = STREAM // BLK
-        lax.fori_loop(a * blocks, (a + 1) * blocks, turn, 0, unroll=2)
     for group in (wide_rings, cross_rings, back_rings, last_rings):
         for one in group:
             one.drain()
@@ -734,22 +738,18 @@
     vmem = pl.BlockSpec(memory_space=pltpu.VMEM)
     rows = ROW_BLOCKS * BLK
 
-    def kernel(partial_ref, flipped, plain, data, image, *rest):
+    def kernel(partial_ref, image_ref, data, *rest):
         copy = pltpu.make_async_copy(partial_ref, data, rest[-1])
         copy.start()
-        combine_kernel(data, flipped, plain, image, copy, *rest[:-1])
+        combine_kernel(data, image_ref, copy, *rest[:-1])
 
     return pl.pallas_call(
         kernel,
-        out_shape=(
-            jax.ShapeDtypeStruct((ROW_BLOCKS, BLK, BLK), BF16),
-            jax.ShapeDtypeStruct((ROW_BLOCKS, BLK, BLK), F32),
-        ),
-        in_specs=[ANY],
-        out_specs=(VMEM, VMEM),
+        out_shape=jax.ShapeDtypeStruct((rows, BLK), BF16),
+        in_specs=[pl.BlockSpec(memory_space=pl.ANY)],
+        out_specs=vmem,
         scratch_shapes=[
             pltpu.VMEM((rows, BLK), F32),
-            pltpu.VMEM((rows, BLK), BF16),
             pltpu.VMEM((STREAMS, 2, BIG // 2, BLK), F32),
             pltpu.VMEM((STREAMS, 2, BIG, BLK), F32),
             pltpu.VMEM((STREAMS, 3, SMALL, BLK), F32),
@@ -766,13 +766,21 @@
 
 
 def adjoint_kernel(
-    count, rows, cols, source, flipped, plain, data_image, adjoint, held, sem, sems
+    count, rows, cols, source, image, data_image, adjoint, held, flipped, plain, sem, sems
 ):
     sensors = Sensors(count, source, held, sems)
     sensors.start()
+    adjoint[...] = jnp.zeros_like(adjoint)
+
+    def flip(b, carry):
+        block = image[b].astype(F32)
+        plain[b] = block
+        flipped[b] = block.T.astype(BF16)
+        return carry
+
+    lax.fori_loop(0, ROW_BLOCKS, flip, 0, unroll=2)
     store = pltpu.make_async_copy(plain, data_image, sem)
     store.start()
-    adjoint[...] = jnp.zeros_like(adjoint)
     shift = lax.axis_index("cols") >> 1
 
     def add(first, width):
@@ -788,7 +796,7 @@
     store.wait()
 
 
-def adjoin(count, rows, cols, sens, flipped, plain):
+def adjoin(count, rows, cols, sens, image):
     held, sems = SENSOR_SCRATCH
     return pl.pallas_call(
         adjoint_kernel,
@@ -796,16 +804,22 @@
             jax.ShapeDtypeStruct((ROW_BLOCKS, BLK, BLK), F32),
             jax.ShapeDtypeStruct((2, NZ, LANES, EACH, BLK, BLK), F32),
         ),
-        in_specs=[SMEM, SMEM, SMEM, ANY, VMEM, ANY],
+        in_specs=[SMEM, SMEM, SMEM, ANY, VMEM],
         out_specs=(ANY, VMEM),
-        scratch_shapes=[held, pltpu.SemaphoreType.DMA, sems],
+        scratch_shapes=[
+            held,
+            pltpu.VMEM((ROW_BLOCKS, BLK, BLK), BF16),
+            pltpu.VMEM((ROW_BLOCKS, BLK, BLK), F32),
+            pltpu.SemaphoreType.DMA,
+            sems,
+        ],
         compiler_params=pltpu.CompilerParams(vmem_limit_bytes=ADJOIN_LIMIT),
         name="adjoin",
-    )(count, rows, cols, sens, flipped, plain)
+    )(count, rows, cols, sens, image)
 
 
 def return_kernel(
-    order, partial, body, rims, neighbors, weights, scale, signs, out, smooth, tables, own, stage, pair, relay_out, relay, landed, gathered, sem, send, recv, part_send, part_recv, *sem_refs
+    order, partial, windows, neighbors, weights, scale, signs, out, tables, own, stage, pair, relay_out, relay, landed, gathered, sem, send, recv, part_send, part_recv, *sem_refs
 ):
     where = place()
     row, col, z, core = where
@@ -886,40 +900,35 @@
                 part_copy(m).start()
 
     def synthesise(p):
-        for h in range(EACH):
-            m = member(p, h)
+        members = [member(p, h) for h in range(EACH)]
+        smooth = [
+            smooth_tile(windows[m], tables[order[0, (m * 2 + core) * 4 + z]]) for m in members
+        ]
+        for m in members:
 
             @pl.when(jnp.logical_not(parts.own(m)))
             def _(m=m):
                 ref = gathered.at[m]
                 remote(ref, ref, part_send.at[0], part_recv.at[m], partner).wait_recv()
 
+        for h, m in enumerate(members):
             cells = lax.dot_general(
                 signs[...], gathered[m], (((1,), (1,)), ((), ())), preferred_element_type=F32
             )
-            out[z, core, p * EACH + h] = (cells + smooth[m]).astype(BF16)
+            out[z, core, p * EACH + h] = (cells + smooth[h]).astype(BF16)
         gather.begin(p)
-
-    def smooth_one(m, carry):
-        block = order[0, (m * 2 + core) * 4 + z]
-        smooth[m] = smooth_tile(body, rims, tables, block)
-        return carry
 
     for p in range(LANES):
         launch(p)
-        if p == 0:
-            tabulate(neighbors, weights, tables, col * CELLS)
-    lax.fori_loop(0, 2, smooth_one, 0)
     pass_on(0)
     pass_on(1)
     hand_over(0)
     pass_on(2)
     hand_over(1)
     pass_on(3)
-    lax.fori_loop(2, 4, smooth_one, 0)
     hand_over(2)
     hand_over(3)
-    lax.fori_loop(4, PARTS, smooth_one, 0)
+    tabulate(neighbors, weights, tables, col * CELLS)
     synthesise(0)
     synthesise(1)
     synthesise(2)
@@ -943,14 +952,13 @@
         ring.drain()
 
 
-def give_back(order, partial, model, rims, neighbors, weights):
+def give_back(order, partial, windows, neighbors, weights):
     return pl.pallas_call(
         return_kernel,
         out_shape=jax.ShapeDtypeStruct((NZ, 2, PARTS, BLK, BLK), BF16),
-        in_specs=[SMEM, ANY, *[VMEM] * 6],
+        in_specs=[SMEM, ANY, *[VMEM] * 5],
         out_specs=VMEM,
         scratch_shapes=[
-            pltpu.VMEM((PARTS, BLK, BLK), F32),
             pltpu.VMEM((COL_BLOCKS, 8, BLK), F32),
             pltpu.VMEM((NZ, LANES, EACH, BLK, BLK), F32),
             pltpu.VMEM((PARTS, BLK, BLK), BF16),
@@ -974,8 +982,7 @@
     )(
         order,
         partial,
-        model,
-        rims,
+        windows,
         neighbors,
         weights,
         jnp.asarray(np.broadcast_to(SCALE[None, :], (8, BLK)), F32),
@@ -1020,11 +1027,11 @@
 
 def local(model_dir, sens_blocks, blk_row, blk_col, blk_count, send_order, neighbors, face_weight):
     model = model_dir.reshape(2 * COL_BLOCKS, RIM, BLK)
-    wavelet, rims = analyse(send_order, model)
+    wavelet, windows = analyse(send_order, model)
     partial_image = forward(blk_count, blk_row, blk_col, sens_blocks, wavelet)
-    flipped, plain = combine(partial_image)
-    data_image, partial_adjoint = adjoin(blk_count, blk_row, blk_col, sens_blocks, flipped, plain)
-    product = give_back(send_order, partial_adjoint, model, rims, neighbors, face_weight)
+    image_half = combine(partial_image).reshape(ROW_BLOCKS, BLK, BLK)
+    data_image, partial_adjoint = adjoin(blk_count, blk_row, blk_col, sens_blocks, image_half)
+    product = give_back(send_order, partial_adjoint, windows, neighbors, face_weight)
     normal_product = place_cells(send_order, product)
     return data_image.reshape(ROW_BLOCKS * BLK, BLK), normal_product.reshape(CELLS, BLK)
 

time: 113 us -> 109 us (0.965)
  Pallas kernels: 110 us -> 107 us
    pallas_call x1, Pallas kernels: 30.4 us -> 27.3 us  [combine(): pl.pallas_call(kernel, out_shape=jax.ShapeDtypeStruct((rows, BLK), BF16),...]
    pallas_call x1, Pallas kernels: 44.6 us -> 43.3 us  [give_back(): pl.pallas_call(return_kernel, out_shape=jax.ShapeDtypeStruct((NZ, 2, PART...]
where the time goes in v9:
time: 109 us
  Pallas kernels  107 us (98%)
  between operations  1.44 us (1%)
    pallas_call x1, Pallas kernels, give_back(): pl.pallas_call(return_kernel, out_shape=jax.ShapeDtypeStruct((NZ, 2, PART...  43.3 us
    pallas_call x1, Pallas kernels, combine(): pl.pallas_call(kernel, out_shape=jax.ShapeDtypeStruct((rows, BLK), BF16),...  27.3 us
    pallas_call x1, Pallas kernels, analyse(): pl.pallas_call(analyse_kernel, out_shape=(jax.ShapeDtypeStruct((COL_BLOCK...  23.5 us
    pallas_call x1, Pallas kernels, adjoin(): pl.pallas_call(adjoint_kernel, out_shape=(jax.ShapeDtypeStruct((ROW_BLOCK...  5.04 us
    pallas_call x1, Pallas kernels, forward(): pl.pallas_call(forward_kernel, out_shape=jax.ShapeDtypeStruct((ROW_BLOCKS...  4.33 us
    pallas_call x1, Pallas kernels, place_cells(): pl.pallas_call(place_kernel, out_shape=jax.ShapeDtypeStruct((COL_BLOCKS,...  3.14 us

profile of v9, /device:TPU:1, one launch (start us, length us, event | category | flops | bytes accessed | tf_op | source)
XLA Modules:
  0.0 108.7 jit_solution(6769653853113011279)
XLA Ops:
  0.6 0.0 copy-start.4
  0.6 0.0 copy-start.3
  1.3 0.0 copy-start.5
  1.3 0.6 copy-done.5
  2.0 23.5 %analyse.1 = (bf16[64,128,128]{2,1,0:T(8,128)(2,1)S(1)}, f32[8,256,128]{2,1,0:T(8,128)S(1)}) custom-call(s32[1,64]{1,0:T(1,128)S(1)} %copy-done.5, f32[128,64,128]{2,1,0:T(8,128)} %bitcast.8), custom_call_target="tpu_custom_call" | custom-call | flops 1073741824 | bytes 62914560 | tf_op jit(solution)/shard_map/analyse/pallas_call | solution.py:446
  25.4 0.0 copy-done.4
  25.5 0.0 copy-done.3
  25.5 4.3 %forward.1 = f32[32,128,128]{2,1,0:T(8,128)S(1)} custom-call(s32[1,1]{1,0:T(1,128)S(6)} %copy.12.count, s32[1,384]{1,0:T(1,128)S(1)} %copy-done.3, s32[1,384]{1,0:T(1,128)S(1)} %copy-done.4, bf16[1,384,128,128]{3,2,1,0:T(8,128)(2,1)} %source.3, bf16[64,128,128]{2,1,0:T(8,128)(2,1)S(1)} %get-tuple-element.6.wavelet), custom_call_target="tpu_custom_call" | custom-call | tf_op jit(solution)/shard_map/forward/pallas_call | solution.py:548
  29.8 27.3 %combine.1 = bf16[4096,128]{1,0:T(8,128)(2,1)S(1)} custom-call(f32[4096,128]{1,0:T(8,128)S(1)} %bitcast.5), custom_call_target="tpu_custom_call" | custom-call | flops 1048576 | bytes 83886080 | tf_op jit(solution)/shard_map/combine/pallas_call | solution.py:746
  57.1 0.0 copy-start
  57.1 0.0 copy-start.1
  57.1 0.0 copy-start.2
  57.1 0.0 copy-start.6
  57.1 5.0 %adjoin.1 = (f32[32,128,128]{2,1,0:T(8,128)}, f32[2,4,4,2,128,128]{5,4,3,2,1,0:T(8,128)S(1)}) custom-call(s32[1,1]{1,0:T(1,128)S(6)} %copy.12.count, s32[1,384]{1,0:T(1,128)S(1)} %copy-done.3, s32[1,384]{1,0:T(1,128)S(1)} %copy-done.4, bf16[1,384,128,128]{3,2,1,0:T(8,128)(2,1)} %source.3, bf16[32,128,128]{2,1,0:T(8,128)(2,1)S(1)} %bitcast.6), custom_call_target="tpu_custom_call" | custom-call | tf_op jit(solution)/shard_map/adjoin/pallas_call | solution.py:801
  62.2 0.0 copy-done
  62.2 0.0 copy-done.1
  62.2 0.0 copy-done.2
  62.2 0.0 copy-done.6
  62.2 43.3 %give_back.1.product = bf16[4,2,8,128,128]{4,3,2,1,0:T(8,128)(2,1)S(1)} custom-call(s32[1,64]{1,0:T(1,128)S(1)} %copy-done.5, f32[2,4,4,2,128,128]{5,4,3,2,1,0:T(8,128)S(1)} %get-tuple-element.8.partial, f32[8,256,128]{2,1,0:T(8,128)S(1)} %get-tuple-element.9.windows, s32[4,8192]{1,0:T(4,128)S(1)} %copy-done, f32[4,8192]{1,0:T(4,128)S(1)} %copy-done.1, ...), custom_call_target="tpu_custom_call" | custom-call | flops 1073741824 | bytes 83886080 | tf_op jit(solution)/shard_map/give_back/pallas_call | solution.py:956
  105.6 3.1 %place_cells.1 = f32[64,128,128]{2,1,0:T(8,128)} custom-call(s32[1,64]{1,0:T(1,128)S(1)} %copy-done.5, bf16[4,2,8,128,128]{4,3,2,1,0:T(8,128)(2,1)S(1)} %give_back.1.product), custom_call_target="tpu_custom_call" | custom-call | tf_op jit(solution)/shard_map/place_cells/pallas_call | solution.py:1014
Async XLA Ops:
  0.6 24.8 %copy-start.4 = (s32[1,384]{1,0:T(1,128)S(1)}, s32[1,384]{1,0:T(1,128)}, u32[]{:S(2)}) copy-start(s32[1,384]{1,0:T(1,128)} %cols.3) | copy-start | bytes 4612
  0.6 24.8 %copy-start.3 = (s32[1,384]{1,0:T(1,128)S(1)}, s32[1,384]{1,0:T(1,128)}, u32[]{:S(2)}) copy-start(s32[1,384]{1,0:T(1,128)} %rows.3) | copy-start | bytes 4612
  1.3 0.7 copy-start.5
  57.1 5.1 %copy-start = (s32[4,8192]{1,0:T(4,128)S(1)}, s32[4,8192]{1,0:T(4,128)}, u32[]{:S(2)}) copy-start(s32[4,8192]{1,0:T(4,128)} %neighbors.1) | copy-start | bytes 393220
  57.1 5.1 %copy-start.1 = (f32[4,8192]{1,0:T(4,128)S(1)}, f32[4,8192]{1,0:T(4,128)}, u32[]{:S(2)}) copy-start(f32[4,8192]{1,0:T(4,128)} %weights.1) | copy-start | bytes 393220
  57.1 5.1 %copy-start.2 = (bf16[128,128]{1,0:T(8,128)(2,1)S(1)}, bf16[128,128]{1,0:T(8,128)(2,1)}, u32[]{:S(2)}) copy-start(bf16[128,128]{1,0:T(8,128)(2,1)} %constant.5.clone.signs) | copy-start | bytes 98308
  57.1 5.1 %copy-start.6 = (f32[8,128]{1,0:T(8,128)S(1)}, f32[8,128]{1,0:T(8,128)}, u32[]{:S(2)}) copy-start(f32[8,128]{1,0:T(8,128)} %constant.4.clone.scale) | copy-start | bytes 12292

commit v10 on v9

--- a/solution.py
+++ b/solution.py
@@ -227,7 +227,7 @@
         tables[t] = jnp.concatenate([near, weights[:, at]], axis=0)
         return carry
 
-    lax.fori_loop(0, COL_BLOCKS, tile, 0)
+    lax.fori_loop(0, COL_BLOCKS, tile, 0, unroll=4)
 
 
 def window_of(body, rims, tile):
@@ -585,8 +585,9 @@
 
 
 class Reduce:
-    def __init__(self, ring, data, base, chunk, relay, landed):
-        self.ring, self.data, self.base, self.chunk = ring, data, base, chunk
+    def __init__(self, ring, source, data, base, chunk, relay, landed):
+        self.ring, self.source, self.data = ring, source, data
+        self.base, self.chunk = base, chunk
         self.half = chunk // 2
         self.relay, self.landed = relay, landed
 
@@ -601,30 +602,31 @@
         return self.landed.at[side, pl.ds(h * self.half, self.half)]
 
     def begin(self):
-        ring, data = self.ring, self.data
-        ring.copy(data.at[self.rows(2, 0)], self.relay_at(0), ring.plus, 0)
-        ring.copy(data.at[self.rows(2, 1)], self.relay_at(1), ring.minus, 1)
-        ring.copy(data.at[self.rows(1, 1)], self.landed_at(0, 1), ring.plus, 2)
-        ring.copy(data.at[self.rows(3, 0)], self.landed_at(1, 0), ring.minus, 3)
+        ring, source = self.ring, self.source
+        ring.copy(source.at[self.rows(2, 0)], self.relay_at(0), ring.plus, 0)
+        ring.copy(source.at[self.rows(2, 1)], self.relay_at(1), ring.minus, 1)
+        ring.copy(source.at[self.rows(1, 1)], self.landed_at(0, 1), ring.plus, 2)
+        ring.copy(source.at[self.rows(3, 0)], self.landed_at(1, 0), ring.minus, 3)
 
     def pass_on(self):
-        ring, data = self.ring, self.data
+        ring, source, data = self.ring, self.source, self.data
         ring.arrived(self.relay_at(0), 0)
-        data[self.rows(1, 0), :] += self.relay[0, : self.half]
+        data[self.rows(1, 0), :] = source[self.rows(1, 0), :] + self.relay[0, : self.half]
         ring.copy(data.at[self.rows(1, 0)], self.landed_at(0, 0), ring.plus, 4)
         ring.arrived(self.relay_at(1), 1)
-        data[self.rows(3, 1), :] += self.relay[1, : self.half]
+        data[self.rows(3, 1), :] = source[self.rows(3, 1), :] + self.relay[1, : self.half]
         ring.copy(data.at[self.rows(3, 1)], self.landed_at(1, 1), ring.minus, 5)
 
     def finish(self):
-        ring, data = self.ring, self.data
+        ring, source, data = self.ring, self.source, self.data
         ring.arrived(self.landed_at(0, 1), 2)
         ring.arrived(self.landed_at(1, 0), 3)
         ring.arrived(self.landed_at(0, 0), 4)
         ring.arrived(self.landed_at(1, 1), 5)
         for h in range(2):
             part = pl.ds(h * self.half, self.half)
-            data[self.rows(0, h), :] += self.landed[0, part, :] + self.landed[1, part, :]
+            landed = self.landed[0, part, :] + self.landed[1, part, :]
+            data[self.rows(0, h), :] = source[self.rows(0, h), :] + landed
 
 
 class DirectReduce:
@@ -678,13 +680,12 @@
 SMALL = BIG // 4
 
 
-def combine_kernel(partial, image, fill, big_relay, big_landed, small_landed, send, recv):
+def combine_kernel(source, image, partial, big_relay, big_landed, small_landed, send, recv):
     row, col, _, _ = place()
     y, x = lax.div(col, 4), lax.rem(col, 4)
     x_ring = [(row, y * 4 + lax.rem(x + step, 4)) for step in range(4)]
     y_ring = [(row, lax.rem(y + step, 4) * 4 + x) for step in range(4)]
     greet(x_ring[1:] + y_ring[1:])()
-    fill.wait()
 
     def ring(axis, slot):
         me, devices = ((x, x_ring), (y, y_ring))[axis]
@@ -698,7 +699,10 @@
     cross_rings = [ring(1 - axis[a], STREAMS + a) for a in streams]
     back_rings = [ring(1 - axis[a], 2 * STREAMS + a) for a in streams]
     last_rings = [ring(axis[a], 3 * STREAMS + a) for a in streams]
-    wide = [Reduce(wide_rings[a], partial, bases[a], BIG, big_relay.at[a], big_landed.at[a]) for a in streams]
+    wide = [
+        Reduce(wide_rings[a], source, partial, bases[a], BIG, big_relay.at[a], big_landed.at[a])
+        for a in streams
+    ]
     cross = [DirectReduce(cross_rings[a], partial, inner[a], SMALL, small_landed.at[a]) for a in streams]
     back = [DirectGather(back_rings[a], image, inner[a], SMALL) for a in streams]
     last = [DirectGather(last_rings[a], image, bases[a], BIG) for a in streams]
@@ -738,15 +742,10 @@
     vmem = pl.BlockSpec(memory_space=pltpu.VMEM)
     rows = ROW_BLOCKS * BLK
 
-    def kernel(partial_ref, image_ref, data, *rest):
-        copy = pltpu.make_async_copy(partial_ref, data, rest[-1])
-        copy.start()
-        combine_kernel(data, image_ref, copy, *rest[:-1])
-
     return pl.pallas_call(
-        kernel,
+        combine_kernel,
         out_shape=jax.ShapeDtypeStruct((rows, BLK), BF16),
-        in_specs=[pl.BlockSpec(memory_space=pl.ANY)],
+        in_specs=[vmem],
         out_specs=vmem,
         scratch_shapes=[
             pltpu.VMEM((rows, BLK), F32),
@@ -755,7 +754,6 @@
             pltpu.VMEM((STREAMS, 3, SMALL, BLK), F32),
             pltpu.SemaphoreType.DMA((4 * STREAMS, 6)),
             pltpu.SemaphoreType.DMA((4 * STREAMS, 6)),
-            pltpu.SemaphoreType.DMA,
         ],
         compiler_params=pltpu.CompilerParams(
             collective_id=1, has_side_effects=True, vmem_limit_bytes=MIDDLE_LIMIT
@@ -819,12 +817,10 @@
 
 
 def return_kernel(
-    order, partial, windows, neighbors, weights, scale, signs, out, tables, own, stage, pair, relay_out, relay, landed, gathered, sem, send, recv, part_send, part_recv, *sem_refs
+    order, partial, windows, neighbors, weights, scale, signs, out, tables, stage, pair, relay_out, relay, landed, gathered, send, recv, part_send, part_recv, *sem_refs
 ):
     where = place()
     row, col, z, core = where
-    fill = pltpu.make_async_copy(partial.at[core], own, sem)
-    fill.start()
     parts = Parts(where)
     mine = parts.mine
 
@@ -841,11 +837,10 @@
         for slot, step in ((6, 2), (7, 1), (8, 3), (9, 0)):
             q = ring.at(step)
             ring.copy(partial.at[1 - core, q, p], pair.at[q, p], partner, slot)
-    fill.wait()
 
     def total(p, step, h):
         q = rings[p].at(step)
-        return own[q, p, h] + pair[q, p, h]
+        return partial[core, q, p, h] + pair[q, p, h]
 
     def paired(p, step, slot):
         rings[p].arrived(pair.at[rings[p].at(step), p], slot)
@@ -956,18 +951,16 @@
     return pl.pallas_call(
         return_kernel,
         out_shape=jax.ShapeDtypeStruct((NZ, 2, PARTS, BLK, BLK), BF16),
-        in_specs=[SMEM, ANY, *[VMEM] * 5],
+        in_specs=[SMEM, *[VMEM] * 6],
         out_specs=VMEM,
         scratch_shapes=[
             pltpu.VMEM((COL_BLOCKS, 8, BLK), F32),
-            pltpu.VMEM((NZ, LANES, EACH, BLK, BLK), F32),
             pltpu.VMEM((PARTS, BLK, BLK), BF16),
             pltpu.VMEM((NZ, LANES, EACH, BLK, BLK), F32),
             pltpu.VMEM((LANES, 6, BLK, BLK), BF16),
             pltpu.VMEM((LANES, 2, BLK, BLK), BF16),
             pltpu.VMEM((LANES, 2, 2, BLK, BLK), BF16),
             pltpu.VMEM((PARTS, BLK, BLK), BF16),
-            pltpu.SemaphoreType.DMA,
             pltpu.SemaphoreType.DMA((LANES, 10)),
             pltpu.SemaphoreType.DMA((LANES, 10)),
             pltpu.SemaphoreType.DMA((PARTS,)),

time: 109 us -> 109 us (level)
    pallas_call x1, Pallas kernels: 27.3 us -> 29.2 us  [combine(): pl.pallas_call(combine_kernel, out_shape=jax.ShapeDtypeStruct((rows, BLK)...]
where the time goes in v10:
time: 109 us; the launch traced here: 108 us
  Pallas kernels  106 us (97%)
  between operations  1.44 us (1%)
    pallas_call x1, Pallas kernels, give_back(): pl.pallas_call(return_kernel, out_shape=jax.ShapeDtypeStruct((NZ, 2, PART...  42.3 us
    pallas_call x1, Pallas kernels, combine(): pl.pallas_call(combine_kernel, out_shape=jax.ShapeDtypeStruct((rows, BLK)...  29.2 us
    pallas_call x1, Pallas kernels, analyse(): pl.pallas_call(analyse_kernel, out_shape=(jax.ShapeDtypeStruct((COL_BLOCK...  23.5 us
    pallas_call x1, Pallas kernels, adjoin(): pl.pallas_call(adjoint_kernel, out_shape=(jax.ShapeDtypeStruct((ROW_BLOCK...  4.46 us
    pallas_call x1, Pallas kernels, forward(): pl.pallas_call(forward_kernel, out_shape=jax.ShapeDtypeStruct((ROW_BLOCKS...  3.76 us
    pallas_call x1, Pallas kernels, place_cells(): pl.pallas_call(place_kernel, out_shape=jax.ShapeDtypeStruct((COL_BLOCKS,...  3.14 us

profile of v10, /device:TPU:1, one launch (start us, length us, event | category | flops | bytes accessed | tf_op | source)
XLA Modules:
  0.0 108.4 jit_solution(2003807054645229557)
XLA Ops:
  0.6 0.0 copy-start.4
  0.6 0.0 copy-start.3
  1.3 0.0 copy-start.5
  1.3 0.6 copy-done.5
  2.0 23.5 %analyse.1 = (bf16[64,128,128]{2,1,0:T(8,128)(2,1)S(1)}, f32[8,256,128]{2,1,0:T(8,128)S(1)}) custom-call(s32[1,64]{1,0:T(1,128)S(1)} %copy-done.5, f32[128,64,128]{2,1,0:T(8,128)} %bitcast.8), custom_call_target="tpu_custom_call" | custom-call | flops 1073741824 | bytes 62914560 | tf_op jit(solution)/shard_map/analyse/pallas_call | solution.py:446
  25.4 0.0 copy-done.4
  25.5 0.0 copy-done.3
  25.5 3.8 %forward.1 = f32[32,128,128]{2,1,0:T(8,128)S(1)} custom-call(s32[1,1]{1,0:T(1,128)S(6)} %copy.12.count, s32[1,384]{1,0:T(1,128)S(1)} %copy-done.3, s32[1,384]{1,0:T(1,128)S(1)} %copy-done.4, bf16[1,384,128,128]{3,2,1,0:T(8,128)(2,1)} %source.3, bf16[64,128,128]{2,1,0:T(8,128)(2,1)S(1)} %get-tuple-element.6.wavelet), custom_call_target="tpu_custom_call" | custom-call | tf_op jit(solution)/shard_map/forward/pallas_call | solution.py:548
  29.2 29.2 %combine.1 = bf16[4096,128]{1,0:T(8,128)(2,1)S(1)} custom-call(f32[4096,128]{1,0:T(8,128)S(1)} %bitcast.5), custom_call_target="tpu_custom_call" | custom-call | flops 1048576 | bytes 83886080 | tf_op jit(solution)/shard_map/combine/pallas_call | solution.py:745
  58.4 0.0 copy-start
  58.4 0.0 copy-start.1
  58.4 0.0 copy-start.2
  58.4 0.0 copy-start.6
  58.4 4.5 %adjoin.1 = (f32[32,128,128]{2,1,0:T(8,128)}, f32[2,4,4,2,128,128]{5,4,3,2,1,0:T(8,128)S(1)}) custom-call(s32[1,1]{1,0:T(1,128)S(6)} %copy.12.count, s32[1,384]{1,0:T(1,128)S(1)} %copy-done.3, s32[1,384]{1,0:T(1,128)S(1)} %copy-done.4, bf16[1,384,128,128]{3,2,1,0:T(8,128)(2,1)} %source.3, bf16[32,128,128]{2,1,0:T(8,128)(2,1)S(1)} %bitcast.6), custom_call_target="tpu_custom_call" | custom-call | tf_op jit(solution)/shard_map/adjoin/pallas_call | solution.py:799
  62.9 0.0 copy-done
  62.9 0.0 copy-done.1
  62.9 0.0 copy-done.2
  62.9 0.0 copy-done.6
  62.9 42.3 %give_back.1.product = bf16[4,2,8,128,128]{4,3,2,1,0:T(8,128)(2,1)S(1)} custom-call(s32[1,64]{1,0:T(1,128)S(1)} %copy-done.5, f32[2,4,4,2,128,128]{5,4,3,2,1,0:T(8,128)S(1)} %get-tuple-element.8.partial, f32[8,256,128]{2,1,0:T(8,128)S(1)} %get-tuple-element.9.windows, s32[4,8192]{1,0:T(4,128)S(1)} %copy-done, f32[4,8192]{1,0:T(4,128)S(1)} %copy-done.1, ...), custom_call_target="tpu_custom_call" | custom-call | flops 1073741824 | bytes 83886080 | tf_op jit(solution)/shard_map/give_back/pallas_call | solution.py:951
  105.2 3.1 %place_cells.1 = f32[64,128,128]{2,1,0:T(8,128)} custom-call(s32[1,64]{1,0:T(1,128)S(1)} %copy-done.5, bf16[4,2,8,128,128]{4,3,2,1,0:T(8,128)(2,1)S(1)} %give_back.1.product), custom_call_target="tpu_custom_call" | custom-call | tf_op jit(solution)/shard_map/place_cells/pallas_call | solution.py:1007
Async XLA Ops:
  0.6 24.8 %copy-start.4 = (s32[1,384]{1,0:T(1,128)S(1)}, s32[1,384]{1,0:T(1,128)}, u32[]{:S(2)}) copy-start(s32[1,384]{1,0:T(1,128)} %cols.3) | copy-start | bytes 4612
  0.6 24.8 %copy-start.3 = (s32[1,384]{1,0:T(1,128)S(1)}, s32[1,384]{1,0:T(1,128)}, u32[]{:S(2)}) copy-start(s32[1,384]{1,0:T(1,128)} %rows.3) | copy-start | bytes 4612
  1.3 0.7 copy-start.5
  58.4 4.5 %copy-start = (s32[4,8192]{1,0:T(4,128)S(1)}, s32[4,8192]{1,0:T(4,128)}, u32[]{:S(2)}) copy-start(s32[4,8192]{1,0:T(4,128)} %neighbors.1) | copy-start | bytes 393220
  58.4 4.5 %copy-start.1 = (f32[4,8192]{1,0:T(4,128)S(1)}, f32[4,8192]{1,0:T(4,128)}, u32[]{:S(2)}) copy-start(f32[4,8192]{1,0:T(4,128)} %weights.1) | copy-start | bytes 393220
  58.4 4.5 %copy-start.2 = (bf16[128,128]{1,0:T(8,128)(2,1)S(1)}, bf16[128,128]{1,0:T(8,128)(2,1)}, u32[]{:S(2)}) copy-start(bf16[128,128]{1,0:T(8,128)(2,1)} %constant.5.clone.signs) | copy-start | bytes 98308
  58.4 4.5 %copy-start.6 = (f32[8,128]{1,0:T(8,128)S(1)}, f32[8,128]{1,0:T(8,128)}, u32[]{:S(2)}) copy-start(f32[8,128]{1,0:T(8,128)} %constant.4.clone.scale) | copy-start | bytes 12292

commit v11 on v10

--- a/solution.py
+++ b/solution.py
@@ -123,8 +123,9 @@
 
 PARTS = NCOLS // 2
 GROUP = PARTS // 2
-LANES = 4
+LANES = 2
 EACH = PARTS // LANES
+PAIR = EACH // 2
 
 
 class RowGather:
@@ -788,7 +789,7 @@
         for u in range(width):
             at = cols[0, first + u]
             part = at >> 3
-            adjoint[(at >> 2) & 1, at & 3, (part + shift) & 3, part >> 2] += terms[u]
+            adjoint[(at >> 2) & 1, at & 3, (part + shift) & (LANES - 1), part >> (LANES // 2)] += terms[u]
 
     sensors.run(add)
     store.wait()
@@ -826,7 +827,7 @@
 
     def out_piece(at, k, p, h):
         first = p * EACH
-        return out.at[at, k, pl.ds(first, EACH) if h is None else pl.ds(first + h, 1)]
+        return out.at[at, k, pl.ds(first, EACH) if h is None else pl.ds(first + h * PAIR, PAIR)]
 
     gather = RowGather(out_piece, sem_refs, where)
     plus, minus, partner = gather.neighbour(1), gather.neighbour(3), gather.partner()
@@ -840,7 +841,8 @@
 
     def total(p, step, h):
         q = rings[p].at(step)
-        return partial[core, q, p, h] + pair[q, p, h]
+        part = pl.ds(h * PAIR, PAIR)
+        return partial[core, q, p, part] + pair[q, p, part]
 
     def paired(p, step, slot):
         rings[p].arrived(pair.at[rings[p].at(step), p], slot)
@@ -880,11 +882,11 @@
         paired(p, 0, 9)
         for slot, (side, h) in ((2, (0, 1)), (3, (1, 0)), (4, (0, 0)), (5, (1, 1))):
             ring.arrived(landed.at[p, side, h], slot)
-        for h in range(EACH):
-            m = member(p, h)
-            value = total(p, 0, h) + (landed[p, 0, h].astype(F32) + landed[p, 1, h].astype(F32))
-            value = (value * lane_scale).astype(BF16)
-            stage[m] = value
+        for i in range(EACH):
+            m, h, j = member(p, i), i // PAIR, i % PAIR
+            landed_sum = landed[p, 0, h, j].astype(F32) + landed[p, 1, h, j].astype(F32)
+            value = partial[core, z, p, i] + pair[z, p, i] + landed_sum
+            stage[m] = (value * lane_scale).astype(BF16)
 
             @pl.when(parts.own(m))
             def _(m=m):
@@ -915,24 +917,17 @@
 
     for p in range(LANES):
         launch(p)
-    pass_on(0)
-    pass_on(1)
-    hand_over(0)
-    pass_on(2)
-    hand_over(1)
-    pass_on(3)
-    hand_over(2)
-    hand_over(3)
+    for p in range(LANES):
+        pass_on(p)
+    for p in range(LANES):
+        hand_over(p)
     tabulate(neighbors, weights, tables, col * CELLS)
-    synthesise(0)
-    synthesise(1)
-    synthesise(2)
-    gather.pass_on(0)
-    synthesise(3)
-    for p in range(1, LANES):
+    for p in range(LANES):
+        synthesise(p)
+    for p in range(LANES):
         gather.pass_on(p)
-        gather.finish(p - 1)
-    gather.finish(LANES - 1)
+    for p in range(LANES):
+        gather.finish(p)
     gather.close(LANES)
 
     def drain(m, carry):
@@ -957,9 +952,9 @@
             pltpu.VMEM((COL_BLOCKS, 8, BLK), F32),
             pltpu.VMEM((PARTS, BLK, BLK), BF16),
             pltpu.VMEM((NZ, LANES, EACH, BLK, BLK), F32),
-            pltpu.VMEM((LANES, 6, BLK, BLK), BF16),
-            pltpu.VMEM((LANES, 2, BLK, BLK), BF16),
-            pltpu.VMEM((LANES, 2, 2, BLK, BLK), BF16),
+            pltpu.VMEM((LANES, 6, PAIR, BLK, BLK), BF16),
+            pltpu.VMEM((LANES, 2, PAIR, BLK, BLK), BF16),
+            pltpu.VMEM((LANES, 2, 2, PAIR, BLK, BLK), BF16),
             pltpu.VMEM((PARTS, BLK, BLK), BF16),
             pltpu.SemaphoreType.DMA((LANES, 10)),
             pltpu.SemaphoreType.DMA((LANES, 10)),

time: 109 us -> 105 us (0.963)
  Pallas kernels: 106 us -> 102 us
    pallas_call x1, Pallas kernels: 42.3 us -> 38.7 us  [give_back(): pl.pallas_call(return_kernel, out_shape=jax.ShapeDtypeStruct((NZ, 2, PART...]
where the time goes in v11:
time: 105 us; the launch traced here: 104 us
  Pallas kernels  102 us (97%)
  between operations  1.44 us (1%)
    pallas_call x1, Pallas kernels, give_back(): pl.pallas_call(return_kernel, out_shape=jax.ShapeDtypeStruct((NZ, 2, PART...  38.7 us
    pallas_call x1, Pallas kernels, combine(): pl.pallas_call(combine_kernel, out_shape=jax.ShapeDtypeStruct((rows, BLK)...  28.9 us
    pallas_call x1, Pallas kernels, analyse(): pl.pallas_call(analyse_kernel, out_shape=(jax.ShapeDtypeStruct((COL_BLOCK...  23.5 us
    pallas_call x1, Pallas kernels, adjoin(): pl.pallas_call(adjoint_kernel, out_shape=(jax.ShapeDtypeStruct((ROW_BLOCK...  4.38 us
    pallas_call x1, Pallas kernels, forward(): pl.pallas_call(forward_kernel, out_shape=jax.ShapeDtypeStruct((ROW_BLOCKS...  3.69 us
    pallas_call x1, Pallas kernels, place_cells(): pl.pallas_call(place_kernel, out_shape=jax.ShapeDtypeStruct((COL_BLOCKS,...  3.14 us

profile of v11, /device:TPU:1, one launch (start us, length us, event | category | flops | bytes accessed | tf_op | source)
XLA Modules:
  0.0 104.4 jit_solution(15373165175995245434)
XLA Ops:
  0.6 0.0 copy-start.4
  0.6 0.0 copy-start.3
  1.3 0.0 copy-start.5
  1.3 0.6 copy-done.5
  2.0 23.5 %analyse.1 = (bf16[64,128,128]{2,1,0:T(8,128)(2,1)S(1)}, f32[8,256,128]{2,1,0:T(8,128)S(1)}) custom-call(s32[1,64]{1,0:T(1,128)S(1)} %copy-done.5, f32[128,64,128]{2,1,0:T(8,128)} %bitcast.8), custom_call_target="tpu_custom_call" | custom-call | flops 1073741824 | bytes 62914560 | tf_op jit(solution)/shard_map/analyse/pallas_call | solution.py:447
  25.4 0.0 copy-done.4
  25.5 0.0 copy-done.3
  25.5 3.7 %forward.1 = f32[32,128,128]{2,1,0:T(8,128)S(1)} custom-call(s32[1,1]{1,0:T(1,128)S(6)} %copy.12.count, s32[1,384]{1,0:T(1,128)S(1)} %copy-done.3, s32[1,384]{1,0:T(1,128)S(1)} %copy-done.4, bf16[1,384,128,128]{3,2,1,0:T(8,128)(2,1)} %source.3, bf16[64,128,128]{2,1,0:T(8,128)(2,1)S(1)} %get-tuple-element.6.wavelet), custom_call_target="tpu_custom_call" | custom-call | tf_op jit(solution)/shard_map/forward/pallas_call | solution.py:549
  29.2 28.9 %combine.1 = bf16[4096,128]{1,0:T(8,128)(2,1)S(1)} custom-call(f32[4096,128]{1,0:T(8,128)S(1)} %bitcast.5), custom_call_target="tpu_custom_call" | custom-call | flops 1048576 | bytes 83886080 | tf_op jit(solution)/shard_map/combine/pallas_call | solution.py:746
  58.1 0.0 copy-start
  58.1 0.0 copy-start.1
  58.1 0.0 copy-start.2
  58.1 0.0 copy-start.6
  58.1 4.4 %adjoin.1 = (f32[32,128,128]{2,1,0:T(8,128)}, f32[2,4,2,4,128,128]{5,4,3,2,1,0:T(8,128)S(1)}) custom-call(s32[1,1]{1,0:T(1,128)S(6)} %copy.12.count, s32[1,384]{1,0:T(1,128)S(1)} %copy-done.3, s32[1,384]{1,0:T(1,128)S(1)} %copy-done.4, bf16[1,384,128,128]{3,2,1,0:T(8,128)(2,1)} %source.3, bf16[32,128,128]{2,1,0:T(8,128)(2,1)S(1)} %bitcast.6), custom_call_target="tpu_custom_call" | custom-call | tf_op jit(solution)/shard_map/adjoin/pallas_call | solution.py:800
  62.5 0.0 copy-done
  62.5 0.0 copy-done.1
  62.5 0.0 copy-done.2
  62.5 0.0 copy-done.6
  62.5 38.7 %give_back.1.product = bf16[4,2,8,128,128]{4,3,2,1,0:T(8,128)(2,1)S(1)} custom-call(s32[1,64]{1,0:T(1,128)S(1)} %copy-done.5, f32[2,4,2,4,128,128]{5,4,3,2,1,0:T(8,128)S(1)} %get-tuple-element.8.partial, f32[8,256,128]{2,1,0:T(8,128)S(1)} %get-tuple-element.9.windows, s32[4,8192]{1,0:T(4,128)S(1)} %copy-done, f32[4,8192]{1,0:T(4,128)S(1)} %copy-done.1, ...), custom_call_target="tpu_custom_call" | custom-call | flops 1073741824 | bytes 83886080 | tf_op jit(solution)/shard_map/give_back/pallas_call | solution.py:946
  101.3 3.1 %place_cells.1 = f32[64,128,128]{2,1,0:T(8,128)} custom-call(s32[1,64]{1,0:T(1,128)S(1)} %copy-done.5, bf16[4,2,8,128,128]{4,3,2,1,0:T(8,128)(2,1)S(1)} %give_back.1.product), custom_call_target="tpu_custom_call" | custom-call | tf_op jit(solution)/shard_map/place_cells/pallas_call | solution.py:1002
Async XLA Ops:
  0.6 24.8 %copy-start.4 = (s32[1,384]{1,0:T(1,128)S(1)}, s32[1,384]{1,0:T(1,128)}, u32[]{:S(2)}) copy-start(s32[1,384]{1,0:T(1,128)} %cols.3) | copy-start | bytes 4612
  0.6 24.8 %copy-start.3 = (s32[1,384]{1,0:T(1,128)S(1)}, s32[1,384]{1,0:T(1,128)}, u32[]{:S(2)}) copy-start(s32[1,384]{1,0:T(1,128)} %rows.3) | copy-start | bytes 4612
  1.3 0.7 copy-start.5
  58.1 4.4 %copy-start = (s32[4,8192]{1,0:T(4,128)S(1)}, s32[4,8192]{1,0:T(4,128)}, u32[]{:S(2)}) copy-start(s32[4,8192]{1,0:T(4,128)} %neighbors.1) | copy-start | bytes 393220
  58.1 4.4 %copy-start.1 = (f32[4,8192]{1,0:T(4,128)S(1)}, f32[4,8192]{1,0:T(4,128)}, u32[]{:S(2)}) copy-start(f32[4,8192]{1,0:T(4,128)} %weights.1) | copy-start | bytes 393220
  58.1 4.4 %copy-start.2 = (bf16[128,128]{1,0:T(8,128)(2,1)S(1)}, bf16[128,128]{1,0:T(8,128)(2,1)}, u32[]{:S(2)}) copy-start(bf16[128,128]{1,0:T(8,128)(2,1)} %constant.5.clone.signs) | copy-start | bytes 98308
  58.1 4.4 %copy-start.6 = (f32[8,128]{1,0:T(8,128)S(1)}, f32[8,128]{1,0:T(8,128)}, u32[]{:S(2)}) copy-start(f32[8,128]{1,0:T(8,128)} %constant.4.clone.scale) | copy-start | bytes 12292

commit v12 on v11

--- a/solution.py
+++ b/solution.py
@@ -675,7 +675,7 @@
             self.ring.arrived(self.rows(4 - step), step - 1)
 
 
-STREAMS = 4
+STREAMS = 2
 STREAM = ROW_BLOCKS * BLK // STREAMS
 BIG = STREAM // 4
 SMALL = BIG // 4

time: 105 us -> 107 us (1.019)
  Pallas kernels: 102 us -> 104 us
    pallas_call x1, Pallas kernels: 4.38 us -> 5.59 us  [adjoin(): pl.pallas_call(adjoint_kernel, out_shape=(jax.ShapeDtypeStruct((ROW_BLOCK...]
    pallas_call x1, Pallas kernels: 3.69 us -> 4.86 us  [forward(): pl.pallas_call(forward_kernel, out_shape=jax.ShapeDtypeStruct((ROW_BLOCKS...]
where the time goes in v12:
time: 107 us
  Pallas kernels  104 us (97%)
  between operations  1.44 us (1%)
    pallas_call x1, Pallas kernels, give_back(): pl.pallas_call(return_kernel, out_shape=jax.ShapeDtypeStruct((NZ, 2, PART...  38.3 us
    pallas_call x1, Pallas kernels, combine(): pl.pallas_call(combine_kernel, out_shape=jax.ShapeDtypeStruct((rows, BLK)...  29 us
    pallas_call x1, Pallas kernels, analyse(): pl.pallas_call(analyse_kernel, out_shape=(jax.ShapeDtypeStruct((COL_BLOCK...  23.5 us
    pallas_call x1, Pallas kernels, adjoin(): pl.pallas_call(adjoint_kernel, out_shape=(jax.ShapeDtypeStruct((ROW_BLOCK...  5.59 us
    pallas_call x1, Pallas kernels, forward(): pl.pallas_call(forward_kernel, out_shape=jax.ShapeDtypeStruct((ROW_BLOCKS...  4.86 us
    pallas_call x1, Pallas kernels, place_cells(): pl.pallas_call(place_kernel, out_shape=jax.ShapeDtypeStruct((COL_BLOCKS,...  3.14 us

profile of v12, /device:TPU:1, one launch (start us, length us, event | category | flops | bytes accessed | tf_op | source)
XLA Modules:
  0.0 106.5 jit_solution(6896215257831349138)
XLA Ops:
  0.6 0.0 copy-start.4
  0.6 0.0 copy-start.3
  1.3 0.0 copy-start.5
  1.3 0.6 copy-done.5
  2.0 23.5 %analyse.1 = (bf16[64,128,128]{2,1,0:T(8,128)(2,1)S(1)}, f32[8,256,128]{2,1,0:T(8,128)S(1)}) custom-call(s32[1,64]{1,0:T(1,128)S(1)} %copy-done.5, f32[128,64,128]{2,1,0:T(8,128)} %bitcast.8), custom_call_target="tpu_custom_call" | custom-call | flops 1073741824 | bytes 62914560 | tf_op jit(solution)/shard_map/analyse/pallas_call | solution.py:447
  25.4 0.0 copy-done.4
  25.5 0.0 copy-done.3
  25.5 4.9 %forward.1 = f32[32,128,128]{2,1,0:T(8,128)S(1)} custom-call(s32[1,1]{1,0:T(1,128)S(6)} %copy.12.count, s32[1,384]{1,0:T(1,128)S(1)} %copy-done.3, s32[1,384]{1,0:T(1,128)S(1)} %copy-done.4, bf16[1,384,128,128]{3,2,1,0:T(8,128)(2,1)} %source.3, bf16[64,128,128]{2,1,0:T(8,128)(2,1)S(1)} %get-tuple-element.6.wavelet), custom_call_target="tpu_custom_call" | custom-call | tf_op jit(solution)/shard_map/forward/pallas_call | solution.py:549
  30.3 29.0 %combine.1 = bf16[4096,128]{1,0:T(8,128)(2,1)S(1)} custom-call(f32[4096,128]{1,0:T(8,128)S(1)} %bitcast.5), custom_call_target="tpu_custom_call" | custom-call | flops 1048576 | bytes 83886080 | tf_op jit(solution)/shard_map/combine/pallas_call | solution.py:746
  59.3 0.0 copy-start
  59.3 0.0 copy-start.1
  59.4 0.0 copy-start.2
  59.4 0.0 copy-start.6
  59.4 5.6 %adjoin.1 = (f32[32,128,128]{2,1,0:T(8,128)}, f32[2,4,2,4,128,128]{5,4,3,2,1,0:T(8,128)S(1)}) custom-call(s32[1,1]{1,0:T(1,128)S(6)} %copy.12.count, s32[1,384]{1,0:T(1,128)S(1)} %copy-done.3, s32[1,384]{1,0:T(1,128)S(1)} %copy-done.4, bf16[1,384,128,128]{3,2,1,0:T(8,128)(2,1)} %source.3, bf16[32,128,128]{2,1,0:T(8,128)(2,1)S(1)} %bitcast.6), custom_call_target="tpu_custom_call" | custom-call | tf_op jit(solution)/shard_map/adjoin/pallas_call | solution.py:800
  65.0 0.0 copy-done
  65.0 0.0 copy-done.1
  65.0 0.0 copy-done.2
  65.0 0.0 copy-done.6
  65.0 38.3 %give_back.1.product = bf16[4,2,8,128,128]{4,3,2,1,0:T(8,128)(2,1)S(1)} custom-call(s32[1,64]{1,0:T(1,128)S(1)} %copy-done.5, f32[2,4,2,4,128,128]{5,4,3,2,1,0:T(8,128)S(1)} %get-tuple-element.8.partial, f32[8,256,128]{2,1,0:T(8,128)S(1)} %get-tuple-element.9.windows, s32[4,8192]{1,0:T(4,128)S(1)} %copy-done, f32[4,8192]{1,0:T(4,128)S(1)} %copy-done.1, ...), custom_call_target="tpu_custom_call" | custom-call | flops 1073741824 | bytes 83886080 | tf_op jit(solution)/shard_map/give_back/pallas_call | solution.py:946
  103.4 3.1 %place_cells.1 = f32[64,128,128]{2,1,0:T(8,128)} custom-call(s32[1,64]{1,0:T(1,128)S(1)} %copy-done.5, bf16[4,2,8,128,128]{4,3,2,1,0:T(8,128)(2,1)S(1)} %give_back.1.product), custom_call_target="tpu_custom_call" | custom-call | tf_op jit(solution)/shard_map/place_cells/pallas_call | solution.py:1002
Async XLA Ops:
  0.6 24.8 %copy-start.4 = (s32[1,384]{1,0:T(1,128)S(1)}, s32[1,384]{1,0:T(1,128)}, u32[]{:S(2)}) copy-start(s32[1,384]{1,0:T(1,128)} %cols.3) | copy-start | bytes 4612
  0.6 24.8 %copy-start.3 = (s32[1,384]{1,0:T(1,128)S(1)}, s32[1,384]{1,0:T(1,128)}, u32[]{:S(2)}) copy-start(s32[1,384]{1,0:T(1,128)} %rows.3) | copy-start | bytes 4612
  1.3 0.7 copy-start.5
  59.3 5.6 %copy-start = (s32[4,8192]{1,0:T(4,128)S(1)}, s32[4,8192]{1,0:T(4,128)}, u32[]{:S(2)}) copy-start(s32[4,8192]{1,0:T(4,128)} %neighbors.1) | copy-start | bytes 393220
  59.3 5.6 %copy-start.1 = (f32[4,8192]{1,0:T(4,128)S(1)}, f32[4,8192]{1,0:T(4,128)}, u32[]{:S(2)}) copy-start(f32[4,8192]{1,0:T(4,128)} %weights.1) | copy-start | bytes 393220
  59.4 5.6 %copy-start.2 = (bf16[128,128]{1,0:T(8,128)(2,1)S(1)}, bf16[128,128]{1,0:T(8,128)(2,1)}, u32[]{:S(2)}) copy-start(bf16[128,128]{1,0:T(8,128)(2,1)} %constant.5.clone.signs) | copy-start | bytes 98308
  59.4 5.6 %copy-start.6 = (f32[8,128]{1,0:T(8,128)S(1)}, f32[8,128]{1,0:T(8,128)}, u32[]{:S(2)}) copy-start(f32[8,128]{1,0:T(8,128)} %constant.4.clone.scale) | copy-start | bytes 12292
